TPU v7x, 256 devices: a whole 4x4x8 slice. The times are simulated.
256 devices in a mesh: zonal: 64 (over y_lo, x, z), merid: 4 (over y_hi, core).
Axes of the slice: x: 4, y: 4 (y_hi: 2, y_lo: 2; y = y_hi * 2 + y_lo), z: 8, core: 2. Of those that a mesh axis runs over, the one named last changes fastest.
Arguments:
- field: bfloat16 [64, 4096, 256], P('merid', 'zonal'), may hold values from -6 to 6
- weight_one: bfloat16 [3, 3, 256, 256], replicated, may hold values from -0.125 to 0.125
- bias_one: float32 [256], replicated, may hold values from -3 to 3
- weight_two: bfloat16 [3, 3, 256, 256], replicated, may hold values from -0.125 to 0.125
- bias_two: float32 [256], replicated, may hold values from -3 to 3
- depth_levels: int32 [64, 4096], P('merid', 'zonal'), may hold values from 0 to 64
- fold_partner: int32 [4096], replicated, may hold values from 0 to 4095, as said below
- cotangent: bfloat16 [64, 4096, 256], P('merid', 'zonal'), may hold values from -6 to 6
Outputs:
- output: bfloat16 [64, 4096, 256], P('merid', 'zonal')
- input_grad: bfloat16 [64, 4096, 256], P('merid', 'zonal')
- grad_one: float32 [3, 3, 256, 256], replicated
- grad_two: float32 [3, 3, 256, 256], replicated
Inputs may be any that keep to these rules, and one draw needn't show every extreme that they name: fold_partner[i] = (4095 - i + s) mod 4096 with one pivot offset s, 0 to 4095, for the whole table.
All inputs are finite; a program needn't handle non-finite values.
Results may differ from a plain program's by a relative error of at most 0.003.
Values may be sent and summed in bfloat16 or wider, within the bound.
No kernel may reach another device: no remote copies, remote signals or barrier semaphores. Data moves between devices by JAX's collectives and lax.ppermute only.
A program may use at most 128 MiB of HBM per device.

v0:
```python
import math

import jax
import jax.numpy as jnp
from jax import lax
from jax.sharding import PartitionSpec as P

LEV = 64


def with_halo(cells, sides, width, closed):
    for axis, dim in sides:
        count = lax.axis_size(axis)
        ends = count if closed else count - 1
        head = lax.slice_in_dim(cells, 0, width, axis=dim)
        tail = lax.slice_in_dim(cells, cells.shape[dim] - width, cells.shape[dim], axis=dim)
        cells = jnp.concatenate(
            [
                lax.ppermute(tail, axis, [(i, (i + 1) % count) for i in range(ends)]),
                cells,
                lax.ppermute(head, axis, [((i + 1) % count, i) for i in range(ends)]),
            ],
            axis=dim,
        )
    return cells


def level_mask(depth_levels, channels):
    level_index = lax.broadcasted_iota(jnp.int32, (1, 1, channels), 2) % LEV
    return (level_index < depth_levels[:, :, None]).astype(jnp.float32)


def fold_forward(top_row, fold_partner):
    columns = top_row.shape[0]
    whole_row = lax.all_gather(top_row, "zonal", axis=0, tiled=True)
    partners = lax.dynamic_slice_in_dim(fold_partner, lax.axis_index("zonal") * columns, columns, 0)
    return jnp.take(whole_row, partners, axis=0)


def fold_backward(fold_grad, fold_partner):
    columns = fold_grad.shape[0]
    whole_row = lax.all_gather(fold_grad.astype(jnp.bfloat16), "zonal", axis=0, tiled=True).astype(
        fold_grad.dtype
    )
    partners = lax.dynamic_slice_in_dim(fold_partner, lax.axis_index("zonal") * columns, columns, 0)
    return jnp.take(whole_row, partners, axis=0)


def pad_field(values, fold_partner, is_top):
    with_rows = with_halo(values, (("merid", 0),), 1, False)
    fold_row = fold_forward(values[-1], fold_partner)
    upper_row = jnp.where(is_top, fold_row, with_rows[-1])
    with_rows = jnp.concatenate([with_rows[:-1], upper_row[None]], axis=0)
    return with_halo(with_rows, (("zonal", 1),), 1, True)


def unpad_grad(grad_pad, fold_partner, is_top):
    sides = jnp.concatenate([grad_pad[:, :1], grad_pad[:, -1:]], axis=1)
    returned = with_halo(sides.astype(jnp.bfloat16), (("zonal", 1),), 1, True).astype(sides.dtype)
    inner = grad_pad[:, 1:-1]
    inner = inner.at[:, 0].add(returned[:, 0]).at[:, -1].add(returned[:, 3])
    rims = jnp.concatenate([inner[:1], inner[-1:]], axis=0)
    back_rows = with_halo(rims.astype(jnp.bfloat16), (("merid", 0),), 1, False).astype(rims.dtype)
    folded = fold_backward(inner[-1], fold_partner)
    top_added = back_rows[3] + jnp.where(is_top, folded, jnp.zeros_like(folded))
    middle = inner[1:-1]
    return middle.at[0].add(back_rows[0]).at[-1].add(top_added)


def patches_of(padded, rows, columns):
    pieces = [
        padded[row_step : row_step + rows, col_step : col_step + columns]
        for row_step in range(3)
        for col_step in range(3)
    ]
    return jnp.concatenate(pieces, axis=2).reshape(rows * columns, -1)


def transpose_conv(delta, flat_weight, rows, columns):
    channels = delta.shape[1]
    parts = lax.dot_general(
        delta, flat_weight, (((1,), (1,)), ((), ())), preferred_element_type=jnp.float32
    )
    parts = parts.reshape(rows, columns, 9, channels)
    grad_pad = jnp.zeros((rows + 2, columns + 2, channels), jnp.float32)
    for row_step in range(3):
        for col_step in range(3):
            grad_pad = grad_pad.at[row_step : row_step + rows, col_step : col_step + columns].add(
                parts[:, :, 3 * row_step + col_step]
            )
    return grad_pad


def kernel_grad(patches, delta):
    channels = delta.shape[1]
    summed = lax.dot_general(
        patches, delta, (((0,), (0,)), ((), ())), preferred_element_type=jnp.float32
    )
    return summed.reshape(3, 3, channels, channels)


def shards(
    field, weight_one, bias_one, weight_two, bias_two, depth_levels, fold_partner, cotangent
):
    rows, columns, channels = field.shape
    is_top = lax.axis_index("merid") == lax.axis_size("merid") - 1
    mask = level_mask(depth_levels, channels)
    flat_one = weight_one.reshape(9 * channels, channels)
    flat_two = weight_two.reshape(9 * channels, channels)
    patches_one = patches_of(pad_field(field, fold_partner, is_top), rows, columns)
    pre_one = (
        jnp.dot(patches_one, flat_one, preferred_element_type=jnp.float32).reshape(
            rows, columns, channels
        )
        + bias_one
    )
    hidden = (jax.nn.gelu(pre_one) * mask).astype(jnp.bfloat16)
    patches_two = patches_of(pad_field(hidden, fold_partner, is_top), rows, columns)
    pre_two = jnp.dot(patches_two, flat_two, preferred_element_type=jnp.float32).reshape(
        rows, columns, channels
    )
    output = ((field.astype(jnp.float32) + pre_two + bias_two) * mask).astype(jnp.bfloat16)
    masked_grad = cotangent.astype(jnp.float32) * mask
    delta_two = masked_grad.astype(jnp.bfloat16).reshape(rows * columns, channels)
    grad_two = kernel_grad(patches_two, delta_two)
    hidden_grad = unpad_grad(
        transpose_conv(delta_two, flat_two, rows, columns), fold_partner, is_top
    )
    _, gelu_back = jax.vjp(jax.nn.gelu, pre_one)
    delta_one = (
        gelu_back(hidden_grad * mask)[0].astype(jnp.bfloat16).reshape(rows * columns, channels)
    )
    grad_one = kernel_grad(patches_one, delta_one)
    field_grad = unpad_grad(
        transpose_conv(delta_one, flat_one, rows, columns), fold_partner, is_top
    )
    input_grad = (masked_grad + field_grad).astype(jnp.bfloat16)
    grad_one, grad_two = lax.psum((grad_one, grad_two), ("zonal", "merid"))
    scale = 1.0 / math.sqrt(rows * columns * lax.axis_size("zonal") * lax.axis_size("merid"))
    return (output, input_grad, grad_one * scale, grad_two * scale)


def solution(mesh):
    placed = (
        P("merid", "zonal", None),
        P(),
        P(),
        P(),
        P(),
        P("merid", "zonal"),
        P(),
        P("merid", "zonal", None),
    )
    return jax.shard_map(
        shards,
        mesh=mesh,
        in_specs=placed,
        out_specs=(P("merid", "zonal", None), P("merid", "zonal", None), P(), P()),
        check_vma=False,
    )
```

profile of v0, /device:TPU:1, one launch (start us, length us, event | category | flops | bytes accessed | tf_op | source)
XLA Modules:
  0.0 1508.1 jit_solution(12286972379343277605)
XLA Ops:
  19.0 6.4 scatter-add.89
  26.8 4.3 add_select_fusion.1
  31.1 6.4 scatter-add.90
  41.3 5.1 scatter-add.94
  48.8 5.1 scatter-add.95
  57.7 5.1 scatter-add.99
  65.2 5.1 scatter-add.100
  73.0 7.3 collective-permute-start.9
  87.4 5.8 collective-permute-start
  97.4 5.1 collective-permute-start.10
  104.4 162.6 %all-gather.9.cloned.1.call-done = bf16[1,4096,256]{2,1,0:T(8,128)(2,1)} async-done(((bf16[1,64,256]{2,1,0:T(8,128)(2,1)}), bf16[1,4096,256]{2,1,0:T(8,128)(2,1)}) %all-gather.9.cloned.1.call-update) | async-done | bytes 2097168 | tf_op jit(solution)/shard_map/all_gather | solution.py:35
  270.0 5.5 collective-permute-start.3
  285.4 281.1 %all-gather.13.cloned.1.call-done = bf16[1,4096,256]{2,1,0:T(8,128)(2,1)} async-done(((bf16[1,64,256]{2,1,0:T(8,128)(2,1)}), bf16[1,4096,256]{2,1,0:T(8,128)(2,1)}) %all-gather.13.cloned.1.call-update) | async-done | bytes 2097168 | tf_op jit(solution)/shard_map/all_gather | solution.py:42
  566.6 3.9 bitcast_convert_fusion.1
  573.5 5.2 fusion.8
  587.7 6.4 scatter-add.110
  617.6 5.4 collective-permute-start.13
  628.7 51.0 %collective-permute-start.5 = (bf16[1,64,256]{2,1,0:T(8,128)(2,1)}, bf16[1,64,256]{2,1,0:T(8,128)(2,1)S(1)}, u32[]{:S(2)}, u32[]{:S(2)}) collective-permute-start(bf16[1,64,256]{2,1,0:T(8,128)(2,1)} %get-tuple-element.341), channel_id=1, source_target_pairs={{1,0},{2,1},{3,2},{5,4},{6,5},{7,6},{9,8},{10,9},{11,10},{13,12},{... | collective-permute-start | bytes 98312 | tf_op jit(solution)/shard_map/ppermute | solution.py:21
  679.7 4.2 collective-permute-start.4
  684.0 6.8 copy.30
  690.8 185.9 %all-gather.11.cloned.1.call-done = bf16[1,4096,256]{2,1,0:T(8,128)(2,1)} async-done(((bf16[1,64,256]{2,1,0:T(8,128)(2,1)}), bf16[1,4096,256]{2,1,0:T(8,128)(2,1)}) %all-gather.11.cloned.1.call-update) | async-done | bytes 2097168 | tf_op jit(solution)/shard_map/all_gather | solution.py:35
  879.8 5.5 collective-permute-start.7
  885.3 5.1 fusion.55
  893.8 6.8 copy.31
  900.6 5.1 fusion.56
  906.5 52.6 %collective-permute-start.14 = (bf16[1,64,256]{2,1,0:T(8,128)(2,1)S(1)}, bf16[1,64,256]{2,1,0:T(8,128)(2,1)S(1)}, u32[]{:S(2)}, u32[]{:S(2)}) collective-permute-start(bf16[1,64,256]{2,1,0:T(8,128)(2,1)S(1)} %copy-done.14), channel_id=1, source_target_pairs={{0,1},{1,2},{2,3},{4,5},{5,6},{6,7},{8,9},{9,10},{10,11},{12,13},{... | collective-permute-start | bytes 98312 | tf_op jit(solution)/shard_map/ppermute | solution.py:19
  961.1 4.7 collective-permute-done.15
  965.9 209.6 %all-gather.15.cloned.1.call-done = bf16[1,4096,256]{2,1,0:T(8,128)(2,1)} async-done(((bf16[1,64,256]{2,1,0:T(8,128)(2,1)}), bf16[1,4096,256]{2,1,0:T(8,128)(2,1)}) %all-gather.15.cloned.1.call-update) | async-done | bytes 2097168 | tf_op jit(solution)/shard_map/all_gather | solution.py:42
  1175.4 3.9 bitcast_convert_fusion
  1183.6 4.5 fusion.1
  1188.1 308.4 %all-reduce.5.cloned.1.call-done = (f32[3,3,256,256]{3,2,1,0:T(8,128)}, f32[3,3,256,256]{3,2,1,0:T(8,128)}) async-done(((f32[3,3,256,256]{3,2,1,0:T(8,128)}, f32[3,3,256,256]{3,2,1,0:T(8,128)}), (f32[3,3,256,256]{3,2,1,0:T(8,128)}, f32[3,3,256,256]{3,2,1,0:T(8,128)})) %all-reduce.5.cloned.1.call-update) | async-done | bytes 4718608 | tf_op jit(solution)/shard_map/psum | solution.py:138
  1496.5 5.1 broadcast_multiply_fusion
  (180 shorter events, 108.4 us)
Async XLA Ops:
  7.2 566.3 %copy-start = (bf16[3,3,256,256]{3,2,1,0:T(8,128)(2,1)S(1)}, bf16[3,3,256,256]{3,2,1,0:T(8,128)(2,1)}, u32[]{:S(2)}) copy-start(bf16[3,3,256,256]{3,2,1,0:T(8,128)(2,1)} %param.65) | copy-start | bytes 3538948
  7.2 259.9 %all-gather.9.cloned.1.call-start = ((), (), s32[]{:S(2)}) async-start(), calls=%async_computation | async-start | bytes 2129920 | tf_op jit(solution)/shard_map/all_gather | solution.py:35
  8.7 557.8 %all-gather.13.cloned.1.call-start = ((), (), s32[]{:S(2)}) async-start(), calls=%async_computation.2 | async-start | bytes 2129920 | tf_op jit(solution)/shard_map/all_gather | solution.py:42
  8.8 564.6 %copy-start.25 = (s32[256]{0:T(256)}, s32[256]{0:T(256)S(1)}, u32[]{:S(2)}) copy-start(s32[256]{0:T(256)S(1)} %and_select_fusion) | copy-start | bytes 3076
  70.5 10.9 collective-permute-start.8
  73.0 196.6 %copy-start.4 = (bf16[16,64,256]{2,1,0:T(8,128)(2,1)S(1)}, bf16[16,64,256]{2,1,0:T(8,128)(2,1)}, u32[]{:S(2)}) copy-start(bf16[16,64,256]{2,1,0:T(8,128)(2,1)} %param.64) | copy-start | bytes 1572868
  73.0 8.4 collective-permute-start.9
  87.4 789.3 %all-gather.11.cloned.1.call-start = ((), (), s32[]{:S(2)}) async-start(), calls=%async_computation.1 | async-start | bytes 2129920 | tf_op jit(solution)/shard_map/all_gather | solution.py:35
  87.4 182.2 %collective-permute-start = (bf16[1,64,256]{2,1,0:T(8,128)(2,1)S(1)}, bf16[1,64,256]{2,1,0:T(8,128)(2,1)S(1)}, u32[]{:S(2)}, u32[]{:S(2)}) collective-permute-start(bf16[1,64,256]{2,1,0:T(8,128)(2,1)S(1)} %copy-done.17), channel_id=1, source_target_pairs={{0,1},{1,2},{2,3},{4,5},{5,6},{6,7},{8,9},{9,10},{10,11},{12,13},{... | collective-permute-start | bytes 98312 | tf_op jit(solution)/shard_map/ppermute | solution.py:19
  93.3 176.3 %collective-permute-start.1 = (bf16[1,64,256]{2,1,0:T(8,128)(2,1)S(1)}, bf16[1,64,256]{2,1,0:T(8,128)(2,1)S(1)}, u32[]{:S(2)}, u32[]{:S(2)}) collective-permute-start(bf16[1,64,256]{2,1,0:T(8,128)(2,1)S(1)} %get-tuple-element.343), channel_id=1, source_target_pairs={{1,0},{2,1},{3,2},{5,4},{6,5},{7,6},{9,8},{10,9},{11,10},{13,12},{... | collective-permute-start | bytes 98312 | tf_op jit(solution)/shard_map/ppermute | solution.py:21
  96.0 477.3 %copy-start.22 = (pred[64]{0:T(512)(128)(4,1)}, pred[64]{0:T(512)(128)(4,1)S(1)}, u32[]{:S(2)}) copy-start(pred[64]{0:T(512)(128)(4,1)S(1)} %get-tuple-element.320) | copy-start | bytes 196
  96.0 474.5 %copy-start.24 = (s32[1024]{0:T(1024)}, s32[1024]{0:T(1024)S(1)}, u32[]{:S(2)}) copy-start(s32[1024]{0:T(1024)S(1)} %pad_clamp_fusion) | copy-start | bytes 12292
  97.4 178.1 %collective-permute-start.10 = (bf16[1,64,256]{2,1,0:T(8,128)(2,1)}, bf16[1,64,256]{2,1,0:T(8,128)(2,1)S(1)}, u32[]{:S(2)}, u32[]{:S(2)}) collective-permute-start(bf16[1,64,256]{2,1,0:T(8,128)(2,1)} %get-tuple-element.324), channel_id=1, source_target_pairs={{0,1},{1,2},{2,3},{4,5},{5,6},{6,7},{8,9},{9,10},{10,11},{12,13},{... | collective-permute-start | bytes 98312 | tf_op jit(solution)/shard_map/ppermute | solution.py:19
  102.5 173.0 %collective-permute-start.11 = (bf16[1,64,256]{2,1,0:T(8,128)(2,1)S(1)}, bf16[1,64,256]{2,1,0:T(8,128)(2,1)S(1)}, u32[]{:S(2)}, u32[]{:S(2)}) collective-permute-start(bf16[1,64,256]{2,1,0:T(8,128)(2,1)S(1)} %get-tuple-element.325), channel_id=1, source_target_pairs={{1,0},{2,1},{3,2},{5,4},{6,5},{7,6},{9,8},{10,9},{11,10},{13,12},{... | collective-permute-start | bytes 98312 | tf_op jit(solution)/shard_map/ppermute | solution.py:21
  269.7 6.9 collective-permute-start.2
  270.0 6.6 collective-permute-start.3
  285.4 288.0 %copy-start.20 = (s32[16,64]{1,0:T(8,128)S(1)}, s32[16,64]{1,0:T(8,128)}, u32[]{:S(2)}) copy-start(s32[16,64]{1,0:T(8,128)} %param.69) | copy-start | bytes 12292
  285.4 288.0 %copy-start.28 = (f32[256]{0:T(256)S(1)}, f32[256]{0:T(256)}, u32[]{:S(2)}) copy-start(f32[256]{0:T(256)} %param.66) | copy-start | bytes 3076
  579.3 596.2 %all-gather.15.cloned.1.call-start = ((), (), s32[]{:S(2)}) async-start(), calls=%async_computation.3 | async-start | bytes 2129920 | tf_op jit(solution)/shard_map/all_gather | solution.py:42
  617.3 6.9 collective-permute-start.12
  617.6 6.6 collective-permute-start.13
  628.6 867.8 %all-reduce.5.cloned.1.call-start = ((), (), s32[]{:S(2)}) async-start(), calls=%async_computation.4 | async-start | bytes 9437184 | tf_op jit(solution)/shard_map/psum | solution.py:138
  628.7 250.6 %collective-permute-start.5 = (bf16[1,64,256]{2,1,0:T(8,128)(2,1)}, bf16[1,64,256]{2,1,0:T(8,128)(2,1)S(1)}, u32[]{:S(2)}, u32[]{:S(2)}) collective-permute-start(bf16[1,64,256]{2,1,0:T(8,128)(2,1)} %get-tuple-element.341), channel_id=1, source_target_pairs={{1,0},{2,1},{3,2},{5,4},{6,5},{7,6},{9,8},{10,9},{11,10},{13,12},{... | collective-permute-start | bytes 98312 | tf_op jit(solution)/shard_map/ppermute | solution.py:21
  679.7 199.7 %collective-permute-start.4 = (bf16[1,64,256]{2,1,0:T(8,128)(2,1)}, bf16[1,64,256]{2,1,0:T(8,128)(2,1)S(1)}, u32[]{:S(2)}, u32[]{:S(2)}) collective-permute-start(bf16[1,64,256]{2,1,0:T(8,128)(2,1)} %get-tuple-element.340), channel_id=1, source_target_pairs={{0,1},{1,2},{2,3},{4,5},{5,6},{6,7},{8,9},{9,10},{10,11},{12,13},{... | collective-permute-start | bytes 98312 | tf_op jit(solution)/shard_map/ppermute | solution.py:19
  684.0 201.3 %copy-start.12 = (bf16[16,64,256]{2,1,0:T(8,128)(2,1)S(1)}, bf16[16,64,256]{2,1,0:T(8,128)(2,1)}, u32[]{:S(2)}) copy-start(bf16[16,64,256]{2,1,0:T(8,128)(2,1)} %get-tuple-element.326) | copy-start | bytes 1572868
  879.5 10.9 collective-permute-start.6
  879.8 10.6 collective-permute-start.7
  906.5 54.6 %collective-permute-start.14 = (bf16[1,64,256]{2,1,0:T(8,128)(2,1)S(1)}, bf16[1,64,256]{2,1,0:T(8,128)(2,1)S(1)}, u32[]{:S(2)}, u32[]{:S(2)}) collective-permute-start(bf16[1,64,256]{2,1,0:T(8,128)(2,1)S(1)} %copy-done.14), channel_id=1, source_target_pairs={{0,1},{1,2},{2,3},{4,5},{5,6},{6,7},{8,9},{9,10},{10,11},{12,13},{... | collective-permute-start | bytes 98312 | tf_op jit(solution)/shard_map/ppermute | solution.py:19
  959.1 6.7 collective-permute-start.15
  965.8 216.5 %copy-start.10 = (bf16[16,64,256]{2,1,0:T(8,128)(2,1)S(1)}, bf16[16,64,256]{2,1,0:T(8,128)(2,1)}, u32[]{:S(2)}) copy-start(bf16[16,64,256]{2,1,0:T(8,128)(2,1)} %param.71) | copy-start | bytes 1572868
  965.9 216.5 %copy-start.21 = (s32[16,64]{1,0:T(8,128)S(1)}, s32[16,64]{1,0:T(8,128)}, u32[]{:S(2)}) copy-start(s32[16,64]{1,0:T(8,128)} %param.69) | copy-start | bytes 12292
  965.9 216.5 %copy-start.26 = (s32[256]{0:T(256)S(1)}, s32[256]{0:T(256)}, u32[]{:S(2)}) copy-start(s32[256]{0:T(256)} %copy-done.25) | copy-start | bytes 3076
  (19 other events, 573.6 us)
Sparse Core Ops, SparseCore 0:
  10.4 256.6 all-gather.8
  269.4 297.1 all-gather.12
  579.4 297.2 all-gather.10
  878.3 297.0 all-gather.14
  1181.5 314.9 all-reduce.4
where the time goes:
time: 1510 us
  waiting for transfers between devices  1150 us (76%)
  starting transfers between devices  152 us (10%)
  local copies, waits for them, and re-layouts  106 us (7%)
  other arithmetic  56.4 us (4%)
  matrix products  25.3 us (2%)
    all_gather x2, waiting for transfers between devices, fold_backward(): lax.all_gather(fold_grad.astype(jnp.bfloat16), 'zonal', axis=0, tiled=True)  491 us
    all_gather x2, waiting for transfers between devices, fold_forward(): whole_row = lax.all_gather(top_row, 'zonal', axis=0, tiled=True)  349 us
    psum x1, waiting for transfers between devices, shards(): grad_one, grad_two = lax.psum((grad_one, grad_two), ('zonal', 'merid'))  308 us
    ppermute x8, starting transfers between devices, with_halo(): lax.ppermute(head, axis, [((i + 1) % count, i) for i in range(ends)])  80.4 us
    ppermute x8, starting transfers between devices, with_halo(): lax.ppermute(tail, axis, [(i, (i + 1) % count) for i in range(ends)])  71.3 us
    scatter-add x14, local copies, waits for them, and re-layouts, transpose_conv(): grad_pad.at[row_step:row_step + rows, col_step:col_step + columns]  51.2 us
  transfers between devices with their start and end apart: 21, of which 8 were waited for; matrix products, arithmetic and copies ran while one was open for 11% of the time, Pallas kernels for 0%

commit v1 on v0

v1 whole, which is shorter than its diff:
```python
import math

import jax
import jax.numpy as jnp
from jax import lax
from jax.experimental import pallas as pl
from jax.experimental.pallas import tpu as pltpu
from jax.sharding import Mesh
from jax.sharding import PartitionSpec as P

LEV = 64
SPLIT = (2, 4, 8)
ZONAL = ("yl", "x", "z")
MERID = ("yh", "c")
PLANE = ("yl", "x", "yh")
SCALE = 1.0 / 512.0
ROWS = 16
COLS = 64
CH = 256
PITCH = 72
EXT = 20 * PITCH + 16
MID = 18 * PITCH + 8
INNER = 16 * PITCH
LANES = 2 * CH + 128
HEAD = 8
F32 = jnp.float32
BF16 = jnp.bfloat16
C0 = math.sqrt(2.0 / math.pi)
C1 = 0.044715


def dot(a, b, dims=((1,), (0,))):
    return lax.dot_general(a, b, (dims, ((), ())), preferred_element_type=F32)


def taps(lhs_ref, row, count, w_ref, picks, transposed):
    total = None
    for a, b, index in picks:
        lhs = lhs_ref[row + a * PITCH : row + a * PITCH + count, b * CH : (b + 1) * CH]
        part = dot(lhs, w_ref[index], ((1,), (1 if transposed else 0,)))
        total = part if total is None else total + part
    return total


def plain(rows_of=(0, 1, 2)):
    return [(a, b, 3 * a + b) for a in rows_of for b in range(3)]


def turned(rows_of=(0, 1, 2)):
    return [(a, b, 8 - 3 * a - b) for a in rows_of for b in range(3)]


def shifted(out_ref, src_ref, count):
    step = 112
    for start in range(0, count, step):
        size = min(step, count - start)
        for b in range(3):
            at = HEAD + start + b - 1
            out_ref[start : start + size, b * CH : (b + 1) * CH] = src_ref[at : at + size, :].astype(BF16)


def own_cells(count, first):
    place = (lax.broadcasted_iota(jnp.int32, (count, CH), 0) + first) % PITCH
    return place >= 8


def transposed_own(ref, first, out_ref):
    eye = (
        lax.broadcasted_iota(jnp.int32, (CH, CH), 0) == lax.broadcasted_iota(jnp.int32, (CH, CH), 1)
    ).astype(BF16)
    step = 128
    for start in range(0, INNER, step):
        cells = ref[first + start : first + start + step, CH : 2 * CH].astype(F32)
        cells = jnp.where(own_cells(step, start), cells, 0.0).astype(BF16)
        out_ref[:, start : start + step] = dot(eye, cells, ((1,), (1,))).astype(BF16)


def weight_grad(keep_ref, send_ref, core, turned_ref, patches_ref, row):
    for a in range(3):
        for b in range(3):
            cells = patches_ref[row + a * PITCH : row + a * PITCH + INNER, b * CH : (b + 1) * CH]
            at = (3 * a + b) * CH
            sums = dot(turned_ref[...], cells)
            low, high = sums[: CH // 2], sums[CH // 2 :]
            keep_ref[:, at : at + CH] = jnp.where(core == 0, low, high)
            send_ref[:, at : at + CH] = jnp.where(core == 0, high, low)


def first_kernel(
    scal_ref, field_ref, cot_ref, dep_ref, west_ref, east_ref, south_ref, north_ref, fold_ref,
    w_ref, bias_ref,
    pf_ref, pd_ref, ph_ref, slope_ref, keep_ref, send_ref,
    ext, depth, west, east, south, north, back,
):
    top = scal_ref[0] == 1
    west[...] = west_ref[...].astype(F32)
    east[...] = east_ref[...].astype(F32)
    south[...] = south_ref[...].astype(F32)
    to = lax.broadcasted_iota(jnp.int32, (PITCH, 2 * PITCH), 0)
    at = lax.broadcasted_iota(jnp.int32, (PITCH, 2 * PITCH), 1)
    want = 63 - jnp.where(to >= 70, to - PITCH, to) + scal_ref[1]
    near = at < PITCH
    here = jnp.where(at >= 70, at - PITCH, at)
    have = jnp.where(near, jnp.where((at >= 64) & (at < 70), -99, here), at - PITCH + 64)
    have = jnp.where(at >= PITCH + 66, -99, have)
    want = jnp.where((to >= 66) & (to < 70), -98, want)
    pick = (want == have).astype(F32).astype(BF16)
    for j in range(2):
        i = 1 - j
        blocks = jnp.concatenate(
            [
                fold_ref[i * PITCH : (i + 1) * PITCH, :],
                fold_ref[(2 + i) * PITCH : (3 + i) * PITCH, :],
            ],
            axis=0,
        )
        north[j * PITCH : (j + 1) * PITCH, :] = north_ref[j * PITCH : (j + 1) * PITCH, :].astype(F32) + dot(pick, blocks)

    def fill(out_ref, lanes, own, width, head):
        if head:
            out_ref[0:head, :] = jnp.zeros((head, width), F32)
        for g in range(21):
            base = head + g * PITCH
            out_ref[base : base + 8, :] = jnp.zeros((8, width), F32)
            y = g - 3
            if 0 <= y < 16:
                out_ref[base : base + 2, :] = east[2 * y : 2 * y + 2, lanes]
            elif -2 <= y < 0:
                at = (y + 2) * PITCH + 64
                out_ref[base : base + 2, :] = south[at : at + 2, lanes]
            elif y >= 16:
                at = (y - 16) * PITCH + 64
                out_ref[base : base + 2, :] = north[at : at + 2, lanes]
            y = g - 2
            if 0 <= y < 16:
                out_ref[base + 6 : base + 8, :] = west[2 * y : 2 * y + 2, lanes]
            elif -2 <= y < 0:
                at = (y + 2) * PITCH + 70
                out_ref[base + 6 : base + 8, :] = south[at : at + 2, lanes]
            elif 16 <= y < 18:
                at = (y - 16) * PITCH + 70
                out_ref[base + 6 : base + 8, :] = north[at : at + 2, lanes]
        for y in range(-2, 18):
            base = head + (y + 2) * PITCH + 8
            if y < 0:
                out_ref[base : base + 64, :] = south[(y + 2) * PITCH : (y + 2) * PITCH + 64, lanes]
            elif y < 16:
                out_ref[base : base + 64, :] = own(y)
            else:
                out_ref[base : base + 64, :] = north[(y - 16) * PITCH : (y - 16) * PITCH + 64, lanes]
        tail = head + 20 * PITCH + 8
        rest = out_ref.shape[0] - tail
        if rest:
            out_ref[tail:, :] = jnp.zeros((rest, width), F32)

    level = lax.broadcasted_iota(jnp.int32, (1, CH), 1) % LEV
    level = level.astype(F32)

    def wet(values):
        return level < jnp.concatenate([values, values], axis=1)

    def own_field(y):
        return field_ref[y * 64 : (y + 1) * 64, :].astype(F32)

    def own_depth(y):
        return dep_ref[y * 64 : (y + 1) * 64, :].astype(F32)

    def own_delta(y):
        cells = cot_ref[y * 64 : (y + 1) * 64, :].astype(F32)
        return jnp.where(wet(own_depth(y)), cells, 0.0)

    fill(ext, slice(0, CH), own_field, CH, HEAD)
    fill(depth, slice(2 * CH, LANES), own_depth, 128, 0)
    shifted(pf_ref, ext, EXT)
    fill(ext, slice(CH, 2 * CH), own_delta, CH, HEAD)
    shifted(pd_ref, ext, EXT)

    bias = bias_ref[...]

    def finish(pre, p):
        count = pre.shape[0]
        x = pre + bias
        square = x * x
        t = jnp.tanh(C0 * (x + C1 * (square * x)))
        keep = wet(depth[p : p + count, :])
        half = 0.5 * (1.0 + t)
        hidden = jnp.where(keep, x * half, 0.0).astype(BF16).astype(F32)
        slope = half + (0.5 * C0) * x * (1.0 - t * t) * (1.0 + (3.0 * C1) * square)
        return hidden, jnp.where(keep, slope, 0.0)

    first = 72
    step = 176
    for start in range(first, first + 1232, step):
        hidden, slope = finish(taps(pf_ref, start - PITCH, step, w_ref, plain(), False), start)
        ext[HEAD + start - first : HEAD + start - first + step, :] = hidden
        slope_ref[start - first : start - first + step, :] = slope
    start = 1296
    picks = [(a, b, jnp.where(top, 8 - 3 * a - b, 3 * a + b)) for a in range(3) for b in range(3)]
    hidden, slope = finish(taps(pf_ref, start - PITCH, 80, w_ref, picks, False), start)
    at = start - first
    beyond = lax.broadcasted_iota(jnp.int32, (8, CH), 0) >= 4
    ext[HEAD + at : HEAD + at + 8, :] = jnp.where(beyond, hidden[:8], ext[HEAD + at : HEAD + at + 8, :])
    slope_ref[at : at + 8, :] = jnp.where(beyond, slope[:8], slope_ref[at : at + 8, :])
    ext[HEAD + at + 8 : HEAD + at + 80, :] = hidden[8:]
    slope_ref[at + 8 : at + 80, :] = slope[8:]
    ext[HEAD + MID : HEAD + MID + 8, :] = jnp.zeros((8, CH), F32)
    shifted(ph_ref, ext, MID)
    transposed_own(pd_ref, 144, back)
    weight_grad(keep_ref, send_ref, scal_ref[2], back, ph_ref, 0)


def second_kernel(
    scal_ref, pd_ref, pf_ref, slope_ref, w_ref, pe_ref, keep_ref, send_ref, ext, back
):
    top = scal_ref[0] == 1
    first = 72
    ext[0:HEAD, :] = jnp.zeros((HEAD, CH), F32)
    ext[HEAD + MID : HEAD + MID + 8, :] = jnp.zeros((8, CH), F32)

    def put(sums, p):
        at = p - first
        count = sums.shape[0]
        delta = (slope_ref[at : at + count, :] * sums).astype(BF16).astype(F32)
        ext[HEAD + at : HEAD + at + count, :] = delta

    step = 232
    for start in range(first, first + 1160, step):
        put(taps(pd_ref, start - PITCH, step, w_ref, turned(), True), start)
    start = 1232
    sums = taps(pd_ref, start - PITCH, 144, w_ref, turned((0,)), True)
    over = [(2, b, jnp.where(top, 6 + b, 2 - b)) for b in range(3)]
    sums = sums + taps(pd_ref, start - PITCH, 144, w_ref, over, True)
    middle = taps(pd_ref, start - PITCH, 72, w_ref, turned((1,)), True)
    beside = [(1, b, jnp.where(top, 3 + b, 5 - b)) for b in range(3)]
    upper = taps(pd_ref, 1296 - PITCH, 80, w_ref, beside, True)
    beyond = lax.broadcasted_iota(jnp.int32, (8, CH), 0) >= 4
    put(sums[:64] + middle[:64], 1232)
    put(sums[64:72] + jnp.where(beyond, upper[:8], middle[64:]), 1296)
    put(sums[72:] + upper[8:], 1304)
    start = 1224
    gap = taps(pd_ref, start - PITCH, 16, w_ref, turned((0, 1)), True)
    gap = gap + taps(pd_ref, start - PITCH, 16, w_ref, over, True)
    at = start - first
    delta = (slope_ref[at : at + 8, :] * gap[:8]).astype(BF16).astype(F32)
    ext[HEAD + at : HEAD + at + 8, :] = jnp.where(beyond, delta, ext[HEAD + at : HEAD + at + 8, :])
    shifted(pe_ref, ext, MID)
    transposed_own(pe_ref, 72, back)
    weight_grad(keep_ref, send_ref, scal_ref[2], back, pf_ref, 72)


def third_kernel(
    scal_ref, ph_ref, pe_ref, pf_ref, pd_ref, dep_ref, w1_ref, w2_ref, bias_ref, out_ref, in_ref
):
    top = scal_ref[0] == 1
    level = (lax.broadcasted_iota(jnp.int32, (1, CH), 1) % LEV).astype(F32)
    bias = bias_ref[...]
    for y in range(0, 16, 4):
        p = 144 + y * PITCH
        sums = taps(ph_ref, p - 144, 4 * PITCH, w2_ref, plain(), False)
        for k in range(4):
            at = p + k * PITCH + 8
            cells = pf_ref[at : at + 64, CH : 2 * CH].astype(F32) + sums[k * PITCH + 8 : (k + 1) * PITCH] + bias
            deep = dep_ref[(y + k) * 64 : (y + k + 1) * 64, :].astype(F32)
            keep = level < jnp.concatenate([deep, deep], axis=1)
            out_ref[(y + k) * 64 : (y + k + 1) * 64, :] = jnp.where(keep, cells, 0.0).astype(BF16)

    def put(cells, y):
        at = 144 + y * PITCH + 8
        total = pd_ref[at : at + 64, CH : 2 * CH].astype(F32) + cells
        in_ref[y * 64 : (y + 1) * 64, :] = total.astype(BF16)

    for y in range(0, 15, 5):
        p = 144 + y * PITCH
        sums = taps(pe_ref, p - 144, 5 * PITCH, w1_ref, turned(), True)
        for k in range(5):
            put(sums[k * PITCH + 8 : (k + 1) * PITCH], y + k)
    p = 144 + 15 * PITCH + 8
    over = [(2, b, jnp.where(top, 6 + b, 2 - b)) for b in range(3)]
    sums = taps(pe_ref, p - 144, 64, w1_ref, turned((0, 1)), True)
    put(sums + taps(pe_ref, p - 144, 64, w1_ref, over, True), 15)


def last_kernel(scal_ref, mine_ref, other_ref, one_ref, two_ref):
    first = scal_ref[2] == 0
    down = lax.broadcasted_iota(jnp.int32, (CH, CH), 0)
    across = lax.broadcasted_iota(jnp.int32, (CH, CH), 1)
    eye = jnp.where(down == across, SCALE, 0.0).astype(BF16)
    for k in range(18):
        mine = mine_ref[:, k * CH : (k + 1) * CH]
        other = other_ref[:, k * CH : (k + 1) * CH]
        low, high = jnp.where(first, mine, other), jnp.where(first, other, mine)
        kernel = dot(eye, jnp.concatenate([low, high], axis=0), ((1,), (1,)))
        out_ref, at = (one_ref, k) if k < 9 else (two_ref, k - 9)
        out_ref[at * CH : (at + 1) * CH, :] = kernel


VM = pl.BlockSpec(memory_space=pltpu.VMEM)
SM = pl.BlockSpec(memory_space=pltpu.SMEM)


def call(body, name, outs, scratch, *args):
    return pl.pallas_call(
        body,
        name=name,
        out_shape=[jax.ShapeDtypeStruct(s, t) for s, t in outs],
        in_specs=[SM] + [VM] * (len(args) - 1),
        out_specs=[VM] * len(outs),
        scratch_shapes=scratch,
        compiler_params=pltpu.CompilerParams(vmem_limit_bytes=60 << 20),
    )(*args)


def shards(
    field, weight_one, bias_one, weight_two, bias_two, depth_levels, fold_partner, cotangent
):
    n_low = lax.axis_size("z")
    n_high = lax.axis_size("yl") * lax.axis_size("x")
    n_z, n_m = n_low * n_high, 4
    merid = lax.axis_index(MERID)
    core = lax.axis_index("c")
    deep = jnp.broadcast_to(depth_levels[:, :, None].astype(BF16), (ROWS, COLS, 128))

    def packed(y, x):
        cut_depth = depth_levels[y, x][:, :, None]
        level = lax.broadcasted_iota(jnp.int32, (1, 1, CH), 2) % LEV
        own = jnp.where(level < cut_depth, cotangent[y, x], jnp.zeros((), BF16))
        return jnp.concatenate([field[y, x], own, deep[y, x]], axis=2)

    whole = slice(None)
    east_edge = packed(whole, slice(COLS - 2, COLS)).reshape(2 * ROWS, LANES)
    west_edge = packed(whole, slice(0, 2)).reshape(2 * ROWS, LANES)
    forward = [(i, (i + 1) % n_z) for i in range(n_z)]
    backward = [((i + 1) % n_z, i) for i in range(n_z)]
    west = lax.ppermute(east_edge, ZONAL, forward)
    east = lax.ppermute(west_edge, ZONAL, backward)

    def strip(y):
        rows = slice(y, y + 2)
        left = west[2 * y : 2 * y + 4].reshape(2, 2, LANES)
        right = east[2 * y : 2 * y + 4].reshape(2, 2, LANES)
        gap = jnp.zeros((2, 4, LANES), BF16)
        return jnp.concatenate([packed(rows, whole), right, gap, left], axis=1).reshape(2 * PITCH, LANES)

    upper, lower = strip(ROWS - 2), strip(0)
    south = lax.ppermute(upper, MERID, [(i, i + 1) for i in range(n_m - 1)])
    north = lax.ppermute(lower, MERID, [(i + 1, i) for i in range(n_m - 1)])
    shift = (fold_partner[0] + 1) % (n_z * COLS)
    quotient, rest = shift // COLS, shift % COLS

    def hop(rows, target):
        route = [(m * n_m + n_m - 1, (target(m) % n_z) * n_m + n_m - 1) for m in range(n_z)]
        return lax.ppermute(rows, ZONAL + MERID, route)

    def turn(rows, high):
        return hop(rows, lambda m: n_z - 1 + n_low * high - m)

    def slide(rows, low):
        return jnp.concatenate([hop(rows, lambda m: m + low), hop(rows, lambda m: m + low + 1)], axis=0)

    fold = lax.switch(quotient // n_low, [lambda rows, h=h: turn(rows, h) for h in range(n_high)], upper)
    fold = lax.switch(quotient % n_low, [lambda rows, h=h: slide(rows, h) for h in range(n_low)], fold)

    scal = jnp.stack([(merid == n_m - 1).astype(jnp.int32), rest.astype(jnp.int32), core.astype(jnp.int32)])
    flat_field = field.reshape(ROWS * COLS, CH)
    flat_cot = cotangent.reshape(ROWS * COLS, CH)
    flat_deep = deep.reshape(ROWS * COLS, 128)
    w1 = weight_one.reshape(9, CH, CH)
    w2 = weight_two.reshape(9, CH, CH)
    half = ((CH // 2, 9 * CH), F32)
    pf, pd, ph, slope, keep_two, send_two = call(
        first_kernel,
        "forward_block",
        [((EXT, 3 * CH), BF16), ((EXT, 3 * CH), BF16), ((MID, 3 * CH), BF16), ((MID, CH), F32), half, half],
        [
            pltpu.VMEM((EXT + 16, CH), F32),
            pltpu.VMEM((EXT, 128), F32),
            pltpu.VMEM((32, LANES), F32),
            pltpu.VMEM((32, LANES), F32),
            pltpu.VMEM((2 * PITCH, LANES), F32),
            pltpu.VMEM((2 * PITCH, LANES), F32),
            pltpu.VMEM((CH, INNER), BF16),
        ],
        scal, flat_field, flat_cot, flat_deep, west, east, south, north, fold, w1, bias_one.reshape(1, CH),
    )
    swap = [(0, 1), (1, 0)]
    came_two = lax.ppermute(send_two, "c", swap)
    pe, keep_one, send_one = call(
        second_kernel,
        "backward_block",
        [((MID, 3 * CH), BF16), half, half],
        [pltpu.VMEM((MID + 16, CH), F32), pltpu.VMEM((CH, INNER), BF16)],
        scal, pd, pf, slope, w2,
    )
    came_one = lax.ppermute(send_one, "c", swap)
    output, input_grad = call(
        third_kernel,
        "outputs_block",
        [((ROWS * COLS, CH), BF16), ((ROWS * COLS, CH), BF16)],
        [],
        scal, ph, pe, pf, pd, flat_deep, w1, w2, bias_two.reshape(1, CH),
    )

    n_p = lax.axis_size("yl") * lax.axis_size("x") * lax.axis_size("yh")
    rows = CH // 2 // n_p
    width = 18 * CH
    sums = jnp.concatenate([keep_one + came_one, keep_two + came_two], axis=1).astype(BF16)
    sums = lax.all_to_all(sums.reshape(n_p, rows, width), PLANE, 0, 0)
    sums = jnp.sum(sums.astype(F32), axis=0)
    part = rows // n_low
    sums = lax.all_to_all(sums.reshape(n_low, part * 36, 128), "z", 0, 0)
    piece = jnp.sum(sums, axis=0).astype(BF16)
    line = lax.all_to_all(jnp.broadcast_to(piece[None], (n_low, part * 36, 128)), "z", 0, 0)
    line = line.reshape(rows, width)
    mine = lax.all_to_all(jnp.broadcast_to(line[None], (n_p, rows, width)), PLANE, 0, 0)
    mine = mine.reshape(CH // 2, width)
    other = lax.ppermute(mine, "c", swap)
    grad_one, grad_two = call(
        last_kernel,
        "kernel_grads",
        [((9 * CH, CH), F32), ((9 * CH, CH), F32)],
        [],
        scal, mine, other,
    )
    return (
        output.reshape(ROWS, COLS, CH),
        input_grad.reshape(ROWS, COLS, CH),
        grad_one.reshape(3, 3, CH, CH),
        grad_two.reshape(3, 3, CH, CH),
    )


def solution(mesh):
    fine = Mesh(mesh.devices.reshape(SPLIT + (2, 2)), ZONAL + MERID)
    cells = P(MERID, ZONAL, None)
    return jax.shard_map(
        shards,
        mesh=fine,
        in_specs=(cells, P(), P(), P(), P(), P(MERID, ZONAL), P(), cells),
        out_specs=(cells, cells, P(), P()),
        check_vma=False,
    )
```

time: 1510 us -> 155 us (0.10)
  waiting for transfers between devices: 1150 us -> 7.73 us
  starting transfers between devices: 152 us -> 26 us
  local copies, waits for them, and re-layouts: 106 us -> 7.81 us
  blocking collectives: 0 us -> 78.6 us
  other arithmetic: 56.4 us -> 3.73 us
  Pallas kernels: 0 us -> 30.4 us
  matrix products: 25.3 us -> 0 us
    all_gather x4 -> x0, waiting for transfers between devices: 839 us -> none  [the longest x2 491 us: fold_backward(): lax.all_gather(fold_grad.astype(jnp.bfloat16), 'zonal', axis=0, tiled=True)]
    psum x1 -> x0, waiting for transfers between devices: 308 us -> none  [shards(): grad_one, grad_two = lax.psum((grad_one, grad_two), ('zonal', 'merid'))]
    ppermute x16 -> x10, starting transfers between devices: 152 us -> 26 us  [the longest x1 9.68 us: shards(): east = lax.ppermute(west_edge, ZONAL, backward)]
    all_to_all x0 -> x4, blocking collectives: none -> 78.6 us  [the longest x1 38.6 us: shards(): sums = lax.all_to_all(sums.reshape(n_p, rows, width), PLANE, 0, 0)]
    scatter-add x18 -> x0, local copies, waits for them, and re-layouts: 55.4 us -> none  [the longest x14 51.2 us: transpose_conv(): grad_pad.at[row_step:row_step + rows, col_step:col_step + columns]]
    pallas_call x0 -> x4, Pallas kernels: none -> 30.4 us  [call(): pl.pallas_call(body, name=name, out_shape=[jax.ShapeDtypeStruct(s, t) for...]
    dot_general x6 -> x0, matrix products: 25.3 us -> none  [the longest x2 10.3 us: kernel_grad(): lax.dot_general(patches, delta, (((0,), (0,)), ((), ())), preferred_eleme...]
    add x14 -> x0, other arithmetic: 22.4 us -> none  [the longest x10 19.7 us: transpose_conv(): grad_pad.at[row_step:row_step + rows, col_step:col_step + columns]]
  transfers between devices with their start and end apart: 21 -> 10, of which waited for: 8 -> 2; matrix products, arithmetic and copies ran while one was open for 11% -> 3% of each run, Pallas kernels for 0% -> 11%
where the time goes in v1:
time: 155 us; the launch traced here: 156 us
  blocking collectives  78.6 us (51%)
  Pallas kernels  30.4 us (20%)
  starting transfers between devices  26 us (17%)
  local copies, waits for them, and re-layouts  7.81 us (5%)
  waiting for transfers between devices  7.73 us (5%)
  other arithmetic  3.73 us (2%)
  between operations  1.61 us (1%)
    all_to_all x1, blocking collectives, shards(): sums = lax.all_to_all(sums.reshape(n_p, rows, width), PLANE, 0, 0)  38.6 us
    pallas_call x4, Pallas kernels, call(): pl.pallas_call(body, name=name, out_shape=[jax.ShapeDtypeStruct(s, t) for...  30.4 us
    all_to_all x1, blocking collectives, shards(): lax.all_to_all(jnp.broadcast_to(line[None], (n_p, rows, width)), PLANE, 0...  18.1 us
    all_to_all x1, blocking collectives, shards(): sums = lax.all_to_all(sums.reshape(n_low, part * 36, 128), 'z', 0, 0)  12.1 us
    all_to_all x1, blocking collectives, shards(): lax.all_to_all(jnp.broadcast_to(piece[None], (n_low, part * 36, 128)), 'z...  9.78 us
    ppermute x1, starting transfers between devices, shards(): east = lax.ppermute(west_edge, ZONAL, backward)  9.68 us
    ppermute x1, waiting for transfers between devices, shards(): west = lax.ppermute(east_edge, ZONAL, forward)  5.15 us
    ppermute x1, starting transfers between devices, shards(): other = lax.ppermute(mine, 'c', swap)  4.62 us
  transfers between devices with their start and end apart: 10, of which 2 were waited for; matrix products, arithmetic and copies ran while one was open for 3% of the time, Pallas kernels for 11%

profile of v1, /device:TPU:1, one launch (start us, length us, event | category | flops | bytes accessed | tf_op | source)
XLA Modules:
  0.0 156.0 jit_solution(2475719273959939297)
XLA Ops:
  0.6 0.7 convert_element_type.17
  1.3 0.8 fusion.8
  2.6 0.9 fusion.3
  3.5 0.9 fusion.4
  4.8 9.7 %collective-permute-start.25 = (bf16[32,640]{1,0:T(8,128)(2,1)S(1)}, bf16[32,640]{1,0:T(8,128)(2,1)S(1)}, u32[]{:S(2)}, u32[]{:S(2)}) collective-permute-start(bf16[32,640]{1,0:T(8,128)(2,1)S(1)} %reshape.130), channel_id=1, source_target_pairs={{4,0},{8,4},{12,8},{16,12},{20,16},{24,20},{28,24},{32,28},{36,32}... | collective-permute-start | bytes 122888 | tf_op jit(solution)/shard_map/ppermute | solution.py:335
  14.6 0.7 fusion.7
  15.3 1.0 compare_select_fusion
  16.5 5.1 %collective-permute-done.24.west_ref = bf16[32,640]{1,0:T(8,128)(2,1)S(1)} collective-permute-done((bf16[32,640]{1,0:T(8,128)(2,1)S(1)}, bf16[32,640]{1,0:T(8,128)(2,1)S(1)}, u32[]{:S(2)}, u32[]{:S(2)}) %collective-permute-start.24) | collective-permute-done | bytes 40992 | tf_op jit(solution)/shard_map/ppermute | solution.py:334
  21.9 0.8 pad_maximum_fusion.10
  22.7 4.0 %collective-permute-start.27 = (bf16[144,640]{1,0:T(8,128)(2,1)S(1)}, bf16[144,640]{1,0:T(8,128)(2,1)S(1)}, u32[]{:S(2)}, u32[]{:S(2)}) collective-permute-start(bf16[144,640]{1,0:T(8,128)(2,1)S(1)} %bitcast.37), channel_id=1, source_target_pairs={{1,0},{2,1},{3,2},{5,4},{6,5},{7,6},{9,8},{10,9},{11,10},{13,12},{... | collective-permute-start | bytes 552968 | tf_op jit(solution)/shard_map/ppermute | solution.py:346
  26.7 4.4 %collective-permute-start.26 = (bf16[144,640]{1,0:T(8,128)(2,1)}, bf16[144,640]{1,0:T(8,128)(2,1)S(1)}, u32[]{:S(2)}, u32[]{:S(2)}) collective-permute-start(bf16[144,640]{1,0:T(8,128)(2,1)} %bitcast.6), channel_id=1, source_target_pairs={{0,1},{1,2},{2,3},{4,5},{5,6},{6,7},{8,9},{9,10},{10,11},{12,13},{... | collective-permute-start | bytes 552968 | tf_op jit(solution)/shard_map/ppermute | solution.py:345
  31.1 1.2 slice.67
  33.1 0.6 pad_add_fusion.scal_ref
  33.7 1.3 conditional.2
  33.7 1.3 collective-permute-start.3
  35.1 1.5 conditional.3
  35.1 0.7 collective-permute-start.21
  35.8 0.7 collective-permute-start.20
  36.6 0.9 broadcast_in_dim.44.dep_ref
  37.5 8.8 %forward_block.1 = (bf16[1456,768]{1,0:T(8,128)(2,1)}, bf16[1456,768]{1,0:T(8,128)(2,1)}, bf16[1304,768]{1,0:T(8,128)(2,1)}, f32[1304,256]{1,0:T(8,128)}, f32[128,2304]{1,0:T(8,128)}, /*index=5*/f32[128,2304]{1,0:T(8,128)}) custom-call(s32[3]{0:T(128)} %pad_add_fusion.scal_ref, bf16[1024,256]{1,0:T(8,128)(2,1)} %bitcast.32, bf16[1024,256]{1,0:T(8,128)(2,1)} %bitcast.33, ...), custom_call_target="tpu_custom_call" | custom-call | tf_op jit(solution)/shard_map/forward_block/pallas_call | solution.py:302
  46.3 9.1 %backward_block.1 = (bf16[1304,768]{1,0:T(8,128)(2,1)}, f32[128,2304]{1,0:T(8,128)}, f32[128,2304]{1,0:T(8,128)}) custom-call(s32[3]{0:T(128)} %pad_add_fusion.scal_ref, bf16[1456,768]{1,0:T(8,128)(2,1)} %get-tuple-element.52.pd_ref, bf16[1456,768]{1,0:T(8,128)(2,1)} %get-tuple-element.53.pf_ref, f32[1304,256]{1,0:T(8,128)} %get-tuple-element.54.slope_ref, ...), custom_call_target="tpu_custom_call" | custom-call | tf_op jit(solution)/shard_map/backward_block/pallas_call | solution.py:302
  55.4 0.5 collective-permute-start.28
  56.0 2.6 %collective-permute-done.28 = f32[128,2304]{1,0:T(8,128)S(1)} collective-permute-done((f32[128,2304]{1,0:T(8,128)}, f32[128,2304]{1,0:T(8,128)S(1)}, u32[]{:S(2)}, u32[]{:S(2)}) %collective-permute-start.28) | collective-permute-done | bytes 1179680 | tf_op jit(solution)/shard_map/ppermute | solution.py:394
  58.8 38.6 %all_to_all.20 = bf16[16,8,4608]{2,1,0:T(8,128)(2,1)S(1)} all-to-all(bf16[16,8,4608]{2,1,0:T(8,128)(2,1)S(1)} %pad_maximum_fusion.8), channel_id=1, replica_groups=mesh['yl'=2,'x'=4,'z'=8,'yh'=2,'c'=2] {'yl','x','yh'}, dimensions={0} | all-to-all | bytes 2359296 | tf_op jit(solution)/shard_map/all_to_all | solution.py:407
  97.4 0.2 convert_reduce_fusion
  97.6 12.1 %all_to_all.21 = f32[8,36,128]{2,1,0:T(8,128)S(1)} all-to-all(f32[8,36,128]{2,1,0:T(8,128)S(1)} %copy.32), channel_id=1, replica_groups=mesh['yl'=2,'x'=4,'z'=8,'yh'=2,'c'=2] {'z'}, dimensions={0} | all-to-all | bytes 294912 | tf_op jit(solution)/shard_map/all_to_all | solution.py:410
  109.7 9.8 %all_to_all.22 = bf16[8,36,128]{2,1,0:T(8,128)(2,1)S(1)} all-to-all(bf16[8,36,128]{2,1,0:T(8,128)(2,1)S(1)} %broadcast_in_dim.51), channel_id=1, replica_groups=mesh['yl'=2,'x'=4,'z'=8,'yh'=2,'c'=2] {'z'}, dimensions={0} | all-to-all | bytes 147456 | tf_op jit(solution)/shard_map/all_to_all | solution.py:412
  119.6 18.1 %all_to_all.23 = bf16[16,8,4608]{2,1,0:T(8,128)(2,1)S(1)} all-to-all(bf16[16,8,4608]{2,1,0:T(8,128)(2,1)S(1)} %broadcast_in_dim.53), channel_id=1, replica_groups=mesh['yl'=2,'x'=4,'z'=8,'yh'=2,'c'=2] {'yl','x','yh'}, dimensions={0} | all-to-all | bytes 2359296 | tf_op jit(solution)/shard_map/all_to_all | solution.py:414
  137.7 4.6 %collective-permute-start.30 = (bf16[128,4608]{1,0:T(8,128)(2,1)S(1)}, bf16[128,4608]{1,0:T(8,128)(2,1)S(1)}, u32[]{:S(2)}, u32[]{:S(2)}) collective-permute-start(bf16[128,4608]{1,0:T(8,128)(2,1)S(1)} %bitcast.30), channel_id=1, source_target_pairs={{0,1},{1,0},{2,3},{3,2},{4,5},{5,4},{6,7},{7,6},{8,9},{9,8},{10,11... | collective-permute-start | bytes 3538952 | tf_op jit(solution)/shard_map/ppermute | solution.py:416
  142.4 8.2 %outputs_block.1 = (bf16[1024,256]{1,0:T(8,128)(2,1)}, bf16[1024,256]{1,0:T(8,128)(2,1)}) custom-call(s32[3]{0:T(128)} %pad_add_fusion.scal_ref, bf16[1304,768]{1,0:T(8,128)(2,1)} %get-tuple-element.51.ph_ref, bf16[1304,768]{1,0:T(8,128)(2,1)} %get-tuple-element.55.pe_ref, bf16[1456,768]{1,0:T(8,128)(2,1)} %get-tuple-element.53.pf_ref, ...), custom_call_target="tpu_custom_call" | custom-call | tf_op jit(solution)/shard_map/outputs_block/pallas_call | solution.py:302
  150.5 1.1 copy-done.1
  151.6 4.4 %kernel_grads.1 = (f32[2304,256]{1,0:T(8,128)}, f32[2304,256]{1,0:T(8,128)}) custom-call(s32[3]{0:T(128)} %pad_add_fusion.scal_ref, bf16[128,4608]{1,0:T(8,128)(2,1)} %bitcast.31, bf16[128,4608]{1,0:T(8,128)(2,1)} %copy-done.1), custom_call_target="tpu_custom_call" | custom-call | tf_op jit(solution)/shard_map/kernel_grads/pallas_call | solution.py:302
  (62 shorter events, 1.8 us)
Async XLA Ops:
  4.8 11.7 %collective-permute-start.25 = (bf16[32,640]{1,0:T(8,128)(2,1)S(1)}, bf16[32,640]{1,0:T(8,128)(2,1)S(1)}, u32[]{:S(2)}, u32[]{:S(2)}) collective-permute-start(bf16[32,640]{1,0:T(8,128)(2,1)S(1)} %reshape.130), channel_id=1, source_target_pairs={{4,0},{8,4},{12,8},{16,12},{20,16},{24,20},{28,24},{32,28},{36,32}... | collective-permute-start | bytes 122888 | tf_op jit(solution)/shard_map/ppermute | solution.py:335
  14.5 7.1 %collective-permute-start.24 = (bf16[32,640]{1,0:T(8,128)(2,1)S(1)}, bf16[32,640]{1,0:T(8,128)(2,1)S(1)}, u32[]{:S(2)}, u32[]{:S(2)}) collective-permute-start(bf16[32,640]{1,0:T(8,128)(2,1)S(1)} %reshape.129), channel_id=1, source_target_pairs={{0,4},{4,8},{8,12},{12,16},{16,20},{20,24},{24,28},{28,32},{32,36}... | collective-permute-start | bytes 122888 | tf_op jit(solution)/shard_map/ppermute | solution.py:334
  16.5 18.6 %copy-start.6 = (bf16[32,640]{1,0:T(8,128)(2,1)}, bf16[32,640]{1,0:T(8,128)(2,1)S(1)}, u32[]{:S(2)}) copy-start(bf16[32,640]{1,0:T(8,128)(2,1)S(1)} %collective-permute-done.25.east_ref) | copy-start | bytes 122884
  21.7 13.4 %copy-start.7 = (bf16[32,640]{1,0:T(8,128)(2,1)}, bf16[32,640]{1,0:T(8,128)(2,1)S(1)}, u32[]{:S(2)}) copy-start(bf16[32,640]{1,0:T(8,128)(2,1)S(1)} %collective-permute-done.24.west_ref) | copy-start | bytes 122884
  22.7 13.8 %collective-permute-start.27 = (bf16[144,640]{1,0:T(8,128)(2,1)S(1)}, bf16[144,640]{1,0:T(8,128)(2,1)S(1)}, u32[]{:S(2)}, u32[]{:S(2)}) collective-permute-start(bf16[144,640]{1,0:T(8,128)(2,1)S(1)} %bitcast.37), channel_id=1, source_target_pairs={{1,0},{2,1},{3,2},{5,4},{6,5},{7,6},{9,8},{10,9},{11,10},{13,12},{... | collective-permute-start | bytes 552968 | tf_op jit(solution)/shard_map/ppermute | solution.py:346
  26.7 9.9 %collective-permute-start.26 = (bf16[144,640]{1,0:T(8,128)(2,1)}, bf16[144,640]{1,0:T(8,128)(2,1)S(1)}, u32[]{:S(2)}, u32[]{:S(2)}) collective-permute-start(bf16[144,640]{1,0:T(8,128)(2,1)} %bitcast.6), channel_id=1, source_target_pairs={{0,1},{1,2},{2,3},{4,5},{5,6},{6,7},{8,9},{9,10},{10,11},{12,13},{... | collective-permute-start | bytes 552968 | tf_op jit(solution)/shard_map/ppermute | solution.py:345
  33.7 1.3 collective-permute-start.3
  35.1 1.4 collective-permute-start.21
  35.8 0.7 collective-permute-start.20
  36.6 1.0 copy-start.4
  36.6 0.9 copy-start.5
  46.3 9.7 %collective-permute-start.29 = (f32[128,2304]{1,0:T(8,128)}, f32[128,2304]{1,0:T(8,128)S(1)}, u32[]{:S(2)}, u32[]{:S(2)}) collective-permute-start(f32[128,2304]{1,0:T(8,128)} %get-tuple-element.61), channel_id=1, source_target_pairs={{0,1},{1,0},{2,3},{3,2},{4,5},{5,4},{6,7},{7,6},{8,9},{9,8},{10,11... | collective-permute-start | bytes 3538952 | tf_op jit(solution)/shard_map/ppermute | solution.py:386
  46.3 9.7 %copy-start.2 = (f32[128,2304]{1,0:T(8,128)S(1)}, f32[128,2304]{1,0:T(8,128)}, u32[]{:S(2)}) copy-start(f32[128,2304]{1,0:T(8,128)} %get-tuple-element.60) | copy-start | bytes 3538948
  55.4 3.2 %collective-permute-start.28 = (f32[128,2304]{1,0:T(8,128)}, f32[128,2304]{1,0:T(8,128)S(1)}, u32[]{:S(2)}, u32[]{:S(2)}) collective-permute-start(f32[128,2304]{1,0:T(8,128)} %get-tuple-element.59), channel_id=1, source_target_pairs={{0,1},{1,0},{2,3},{3,2},{4,5},{5,4},{6,7},{7,6},{8,9},{9,8},{10,11... | collective-permute-start | bytes 3538952 | tf_op jit(solution)/shard_map/ppermute | solution.py:394
  55.9 2.7 %copy-start.3 = (f32[128,2304]{1,0:T(8,128)S(1)}, f32[128,2304]{1,0:T(8,128)}, u32[]{:S(2)}) copy-start(f32[128,2304]{1,0:T(8,128)} %get-tuple-element.58) | copy-start | bytes 3538948
  137.7 12.8 %copy-start = (bf16[16,8,4608]{2,1,0:T(8,128)(2,1)}, bf16[16,8,4608]{2,1,0:T(8,128)(2,1)S(1)}, u32[]{:S(2)}) copy-start(bf16[16,8,4608]{2,1,0:T(8,128)(2,1)S(1)} %all_to_all.23) | copy-start | bytes 3538948
  137.7 12.8 %collective-permute-start.30 = (bf16[128,4608]{1,0:T(8,128)(2,1)S(1)}, bf16[128,4608]{1,0:T(8,128)(2,1)S(1)}, u32[]{:S(2)}, u32[]{:S(2)}) collective-permute-start(bf16[128,4608]{1,0:T(8,128)(2,1)S(1)} %bitcast.30), channel_id=1, source_target_pairs={{0,1},{1,0},{2,3},{3,2},{4,5},{5,4},{6,7},{7,6},{8,9},{9,8},{10,11... | collective-permute-start | bytes 3538952 | tf_op jit(solution)/shard_map/ppermute | solution.py:416
  150.5 1.1 copy-start.1

commit v2 on v1

--- a/solution.py
+++ b/solution.py
@@ -7,6 +7,7 @@
 from jax.experimental.pallas import tpu as pltpu
 from jax.sharding import Mesh
 from jax.sharding import PartitionSpec as P
+
 
 LEV = 64
 SPLIT = (2, 4, 8)
@@ -35,19 +36,20 @@
 
 def taps(lhs_ref, row, count, w_ref, picks, transposed):
     total = None
-    for a, b, index in picks:
-        lhs = lhs_ref[row + a * PITCH : row + a * PITCH + count, b * CH : (b + 1) * CH]
-        part = dot(lhs, w_ref[index], ((1,), (1 if transposed else 0,)))
+    for a, indices in picks:
+        lhs = lhs_ref[row + a * PITCH : row + a * PITCH + count, :]
+        side = jnp.concatenate([w_ref[k] for k in indices], axis=1 if transposed else 0)
+        part = dot(lhs, side, ((1,), (1 if transposed else 0,)))
         total = part if total is None else total + part
     return total
 
 
 def plain(rows_of=(0, 1, 2)):
-    return [(a, b, 3 * a + b) for a in rows_of for b in range(3)]
+    return [(a, [3 * a + b for b in range(3)]) for a in rows_of]
 
 
 def turned(rows_of=(0, 1, 2)):
-    return [(a, b, 8 - 3 * a - b) for a in rows_of for b in range(3)]
+    return [(a, [8 - 3 * a - b for b in range(3)]) for a in rows_of]
 
 
 def shifted(out_ref, src_ref, count):
@@ -84,6 +86,69 @@
             low, high = sums[: CH // 2], sums[CH // 2 :]
             keep_ref[:, at : at + CH] = jnp.where(core == 0, low, high)
             send_ref[:, at : at + CH] = jnp.where(core == 0, high, low)
+
+
+def pack_kernel(field_ref, cot_ref, dep_ref, deep_ref, top_ref, low_ref, west_ref, east_ref, edge):
+    eye = (
+        lax.broadcasted_iota(jnp.int32, (COLS, COLS), 0) == lax.broadcasted_iota(jnp.int32, (COLS, COLS), 1)
+    ).astype(F32)
+    ones = jnp.ones((COLS, 128), BF16)
+    level = (lax.broadcasted_iota(jnp.int32, (1, CH), 1) % LEV).astype(F32)
+
+    def masked(at, count):
+        deep = deep_ref[at : at + count, :].astype(F32)
+        keep = level < jnp.concatenate([deep, deep], axis=1)
+        return jnp.where(keep, cot_ref[at : at + count, :].astype(F32), 0.0)
+
+    for y in range(ROWS):
+        line = dep_ref[y : y + 1, :].astype(F32)
+        deep_ref[y * COLS : (y + 1) * COLS, :] = dot((eye * line).astype(BF16), ones).astype(BF16)
+    for out_ref, first in ((top_ref, ROWS - 2), (low_ref, 0)):
+        at = first * COLS
+        out_ref[:, 0:CH] = field_ref[at : at + 2 * COLS, :]
+        out_ref[:, CH : 2 * CH] = masked(at, 2 * COLS).astype(BF16)
+        out_ref[:, 2 * CH : LANES] = deep_ref[at : at + 2 * COLS, :]
+    for out_ref, column, skip in ((west_ref, 0, 0), (east_ref, COLS - 16, 14)):
+        for y in range(ROWS):
+            at = y * COLS + column
+            cells = slice(2 * y, 2 * y + 2)
+            edge[cells, 0:CH] = field_ref[at : at + 16, :].astype(F32)[skip : skip + 2]
+            edge[cells, CH : 2 * CH] = masked(at, 16)[skip : skip + 2]
+            edge[cells, 2 * CH : LANES] = deep_ref[at : at + 16, :].astype(F32)[skip : skip + 2]
+        out_ref[...] = edge[...].astype(BF16)
+
+
+def strip_kernel(
+    scal_ref, top_ref, low_ref, west_ref, east_ref, near_ref, far_ref, upper_ref, lower_ref, fold_ref, west, east, far,
+    extra, strip,
+):
+    west[...] = west_ref[...].astype(F32)
+    east[...] = east_ref[...].astype(F32)
+    far[...] = far_ref[...].astype(F32)
+    strip[...] = jnp.zeros(strip.shape, F32)
+    for out_ref, rows_ref, first in ((upper_ref, top_ref, ROWS - 2), (lower_ref, low_ref, 0)):
+        for k in range(2):
+            y, at = first + k, k * PITCH
+            strip[at : at + COLS, :] = rows_ref[k * COLS : (k + 1) * COLS, :].astype(F32)
+            strip[at + 64 : at + 66, :] = east[2 * y : 2 * y + 2, :]
+            strip[at + 70 : at + 72, :] = west[2 * y : 2 * y + 2, :]
+        out_ref[...] = strip[...].astype(BF16)
+    to = lax.broadcasted_iota(jnp.int32, (PITCH, 144), 0)
+    at = lax.broadcasted_iota(jnp.int32, (PITCH, 144), 1)
+    want = 63 - jnp.where(to >= 70, to - PITCH, to) + scal_ref[1]
+    want = jnp.where((to >= 66) & (to < 70), -98, want)
+    have = jnp.where(at < 128, at, jnp.where(at < 130, at - 130, jnp.where(at < 132, at - 2, -99)))
+    pick = (want == have).astype(F32).astype(BF16)
+    extra[...] = jnp.zeros(extra.shape, F32)
+    for j in range(2):
+        i = 1 - j
+        y = ROWS - 2 + i
+        extra[0:2, :] = west[2 * y : 2 * y + 2, :]
+        extra[2:4, :] = far[2 * i : 2 * i + 2, :]
+        rows = slice(i * COLS, (i + 1) * COLS)
+        cells = jnp.concatenate([top_ref[rows, :], near_ref[rows, :], extra[...].astype(BF16)], axis=0)
+        strip[j * PITCH : (j + 1) * PITCH, :] = dot(pick, cells)
+    fold_ref[...] = strip[...].astype(BF16)
 
 
 def first_kernel(
@@ -96,25 +161,7 @@
     west[...] = west_ref[...].astype(F32)
     east[...] = east_ref[...].astype(F32)
     south[...] = south_ref[...].astype(F32)
-    to = lax.broadcasted_iota(jnp.int32, (PITCH, 2 * PITCH), 0)
-    at = lax.broadcasted_iota(jnp.int32, (PITCH, 2 * PITCH), 1)
-    want = 63 - jnp.where(to >= 70, to - PITCH, to) + scal_ref[1]
-    near = at < PITCH
-    here = jnp.where(at >= 70, at - PITCH, at)
-    have = jnp.where(near, jnp.where((at >= 64) & (at < 70), -99, here), at - PITCH + 64)
-    have = jnp.where(at >= PITCH + 66, -99, have)
-    want = jnp.where((to >= 66) & (to < 70), -98, want)
-    pick = (want == have).astype(F32).astype(BF16)
-    for j in range(2):
-        i = 1 - j
-        blocks = jnp.concatenate(
-            [
-                fold_ref[i * PITCH : (i + 1) * PITCH, :],
-                fold_ref[(2 + i) * PITCH : (3 + i) * PITCH, :],
-            ],
-            axis=0,
-        )
-        north[j * PITCH : (j + 1) * PITCH, :] = north_ref[j * PITCH : (j + 1) * PITCH, :].astype(F32) + dot(pick, blocks)
+    north[...] = north_ref[...].astype(F32) + fold_ref[...].astype(F32)
 
     def fill(out_ref, lanes, own, width, head):
         if head:
@@ -195,7 +242,7 @@
         ext[HEAD + start - first : HEAD + start - first + step, :] = hidden
         slope_ref[start - first : start - first + step, :] = slope
     start = 1296
-    picks = [(a, b, jnp.where(top, 8 - 3 * a - b, 3 * a + b)) for a in range(3) for b in range(3)]
+    picks = [(a, [jnp.where(top, 8 - 3 * a - b, 3 * a + b) for b in range(3)]) for a in range(3)]
     hidden, slope = finish(taps(pf_ref, start - PITCH, 80, w_ref, picks, False), start)
     at = start - first
     beyond = lax.broadcasted_iota(jnp.int32, (8, CH), 0) >= 4
@@ -228,10 +275,10 @@
         put(taps(pd_ref, start - PITCH, step, w_ref, turned(), True), start)
     start = 1232
     sums = taps(pd_ref, start - PITCH, 144, w_ref, turned((0,)), True)
-    over = [(2, b, jnp.where(top, 6 + b, 2 - b)) for b in range(3)]
+    over = [(2, [jnp.where(top, 6 + b, 2 - b) for b in range(3)])]
     sums = sums + taps(pd_ref, start - PITCH, 144, w_ref, over, True)
     middle = taps(pd_ref, start - PITCH, 72, w_ref, turned((1,)), True)
-    beside = [(1, b, jnp.where(top, 3 + b, 5 - b)) for b in range(3)]
+    beside = [(1, [jnp.where(top, 3 + b, 5 - b) for b in range(3)])]
     upper = taps(pd_ref, 1296 - PITCH, 80, w_ref, beside, True)
     beyond = lax.broadcasted_iota(jnp.int32, (8, CH), 0) >= 4
     put(sums[:64] + middle[:64], 1232)
@@ -249,25 +296,28 @@
 
 
 def third_kernel(
-    scal_ref, ph_ref, pe_ref, pf_ref, pd_ref, dep_ref, w1_ref, w2_ref, bias_ref, out_ref, in_ref
+    scal_ref, ph_ref, pe_ref, field_ref, cot_ref, dep_ref, w1_ref, w2_ref, bias_ref, out_ref, in_ref
 ):
     top = scal_ref[0] == 1
     level = (lax.broadcasted_iota(jnp.int32, (1, CH), 1) % LEV).astype(F32)
     bias = bias_ref[...]
+
+    def wet(at):
+        deep = dep_ref[at, :].astype(F32)
+        return level < jnp.concatenate([deep, deep], axis=1)
+
     for y in range(0, 16, 4):
         p = 144 + y * PITCH
         sums = taps(ph_ref, p - 144, 4 * PITCH, w2_ref, plain(), False)
         for k in range(4):
-            at = p + k * PITCH + 8
-            cells = pf_ref[at : at + 64, CH : 2 * CH].astype(F32) + sums[k * PITCH + 8 : (k + 1) * PITCH] + bias
-            deep = dep_ref[(y + k) * 64 : (y + k + 1) * 64, :].astype(F32)
-            keep = level < jnp.concatenate([deep, deep], axis=1)
-            out_ref[(y + k) * 64 : (y + k + 1) * 64, :] = jnp.where(keep, cells, 0.0).astype(BF16)
+            at = slice((y + k) * 64, (y + k + 1) * 64)
+            cells = field_ref[at, :].astype(F32) + sums[k * PITCH + 8 : (k + 1) * PITCH] + bias
+            out_ref[at, :] = jnp.where(wet(at), cells, 0.0).astype(BF16)
 
     def put(cells, y):
-        at = 144 + y * PITCH + 8
-        total = pd_ref[at : at + 64, CH : 2 * CH].astype(F32) + cells
-        in_ref[y * 64 : (y + 1) * 64, :] = total.astype(BF16)
+        at = slice(y * 64, (y + 1) * 64)
+        total = jnp.where(wet(at), cot_ref[at, :].astype(F32), 0.0) + cells
+        in_ref[at, :] = total.astype(BF16)
 
     for y in range(0, 15, 5):
         p = 144 + y * PITCH
@@ -275,7 +325,7 @@
         for k in range(5):
             put(sums[k * PITCH + 8 : (k + 1) * PITCH], y + k)
     p = 144 + 15 * PITCH + 8
-    over = [(2, b, jnp.where(top, 6 + b, 2 - b)) for b in range(3)]
+    over = [(2, [jnp.where(top, 6 + b, 2 - b) for b in range(3)])]
     sums = taps(pe_ref, p - 144, 64, w1_ref, turned((0, 1)), True)
     put(sums + taps(pe_ref, p - 144, 64, w1_ref, over, True), 15)
 
@@ -298,19 +348,21 @@
 SM = pl.BlockSpec(memory_space=pltpu.SMEM)
 
 
-def call(body, name, outs, scratch, *args):
+def call(body, outs, scratch, *args, flops=10**7, scalars=True):
+    moved = sum(math.prod(a.shape) * a.dtype.itemsize for a in args)
+    moved += sum(math.prod(s) * jnp.dtype(t).itemsize for s, t in outs)
     return pl.pallas_call(
         body,
-        name=name,
+        cost_estimate=pl.CostEstimate(flops=flops, bytes_accessed=moved, transcendentals=0),
         out_shape=[jax.ShapeDtypeStruct(s, t) for s, t in outs],
-        in_specs=[SM] + [VM] * (len(args) - 1),
+        in_specs=([SM] if scalars else [VM]) + [VM] * (len(args) - 1),
         out_specs=[VM] * len(outs),
         scratch_shapes=scratch,
-        compiler_params=pltpu.CompilerParams(vmem_limit_bytes=60 << 20),
+        compiler_params=pltpu.CompilerParams(vmem_limit_bytes=24 << 20),
     )(*args)
 
 
-def shards(
+def block(
     field, weight_one, bias_one, weight_two, bias_two, depth_levels, fold_partner, cotangent
 ):
     n_low = lax.axis_size("z")
@@ -318,58 +370,58 @@
     n_z, n_m = n_low * n_high, 4
     merid = lax.axis_index(MERID)
     core = lax.axis_index("c")
-    deep = jnp.broadcast_to(depth_levels[:, :, None].astype(BF16), (ROWS, COLS, 128))
-
-    def packed(y, x):
-        cut_depth = depth_levels[y, x][:, :, None]
-        level = lax.broadcasted_iota(jnp.int32, (1, 1, CH), 2) % LEV
-        own = jnp.where(level < cut_depth, cotangent[y, x], jnp.zeros((), BF16))
-        return jnp.concatenate([field[y, x], own, deep[y, x]], axis=2)
-
-    whole = slice(None)
-    east_edge = packed(whole, slice(COLS - 2, COLS)).reshape(2 * ROWS, LANES)
-    west_edge = packed(whole, slice(0, 2)).reshape(2 * ROWS, LANES)
-    forward = [(i, (i + 1) % n_z) for i in range(n_z)]
-    backward = [((i + 1) % n_z, i) for i in range(n_z)]
-    west = lax.ppermute(east_edge, ZONAL, forward)
-    east = lax.ppermute(west_edge, ZONAL, backward)
-
-    def strip(y):
-        rows = slice(y, y + 2)
-        left = west[2 * y : 2 * y + 4].reshape(2, 2, LANES)
-        right = east[2 * y : 2 * y + 4].reshape(2, 2, LANES)
-        gap = jnp.zeros((2, 4, LANES), BF16)
-        return jnp.concatenate([packed(rows, whole), right, gap, left], axis=1).reshape(2 * PITCH, LANES)
-
-    upper, lower = strip(ROWS - 2), strip(0)
-    south = lax.ppermute(upper, MERID, [(i, i + 1) for i in range(n_m - 1)])
-    north = lax.ppermute(lower, MERID, [(i + 1, i) for i in range(n_m - 1)])
+    flat_field = field.reshape(ROWS * COLS, CH)
+    flat_cot = cotangent.reshape(ROWS * COLS, CH)
+    edge, rim = ((2 * ROWS, LANES), BF16), ((2 * COLS, LANES), BF16)
+    flat_deep, top_rows, low_rows, west_edge, east_edge = call(
+        pack_kernel,
+        [((ROWS * COLS, 128), BF16), rim, rim, edge, edge],
+        [pltpu.VMEM((2 * ROWS, LANES), F32)],
+        flat_field, flat_cot, depth_levels, scalars=False,
+    )
+
+    fold_partner, west_edge = lax.optimization_barrier((fold_partner, west_edge))
     shift = (fold_partner[0] + 1) % (n_z * COLS)
     quotient, rest = shift // COLS, shift % COLS
+    scal = jnp.stack([(merid == n_m - 1).astype(jnp.int32), rest.astype(jnp.int32), core.astype(jnp.int32)])
 
     def hop(rows, target):
         route = [(m * n_m + n_m - 1, (target(m) % n_z) * n_m + n_m - 1) for m in range(n_z)]
         return lax.ppermute(rows, ZONAL + MERID, route)
 
+    near = hop(top_rows, lambda m: m - 1)
+    far = hop(west_edge[2 * ROWS - 4 :], lambda m: m - 2)
+    west = lax.ppermute(east_edge, ZONAL, [(i, (i + 1) % n_z) for i in range(n_z)])
+    east = lax.ppermute(west_edge, ZONAL, [((i + 1) % n_z, i) for i in range(n_z)])
+    strip = ((2 * PITCH, LANES), BF16)
+    upper, lower, fold = call(
+        strip_kernel,
+        [strip, strip, strip],
+        [
+            pltpu.VMEM((2 * ROWS, LANES), F32),
+            pltpu.VMEM((2 * ROWS, LANES), F32),
+            pltpu.VMEM((4, LANES), F32),
+            pltpu.VMEM((16, LANES), F32),
+            pltpu.VMEM((2 * PITCH, LANES), F32),
+        ],
+        scal, top_rows, low_rows, west, east, near, far,
+    )
+    south = lax.ppermute(upper, MERID, [(i, i + 1) for i in range(n_m - 1)])
+    north = lax.ppermute(lower, MERID, [(i + 1, i) for i in range(n_m - 1)])
+
     def turn(rows, high):
-        return hop(rows, lambda m: n_z - 1 + n_low * high - m)
+        return hop(rows, lambda m: n_low * ((n_high - 1 - m // n_low + high) % n_high) + m % n_low)
 
     def slide(rows, low):
-        return jnp.concatenate([hop(rows, lambda m: m + low), hop(rows, lambda m: m + low + 1)], axis=0)
-
-    fold = lax.switch(quotient // n_low, [lambda rows, h=h: turn(rows, h) for h in range(n_high)], upper)
+        return hop(rows, lambda m: n_low * (m // n_low) + n_low - 1 + low - m % n_low)
+
+    fold = lax.switch(quotient // n_low, [lambda rows, h=h: turn(rows, h) for h in range(n_high)], fold)
     fold = lax.switch(quotient % n_low, [lambda rows, h=h: slide(rows, h) for h in range(n_low)], fold)
-
-    scal = jnp.stack([(merid == n_m - 1).astype(jnp.int32), rest.astype(jnp.int32), core.astype(jnp.int32)])
-    flat_field = field.reshape(ROWS * COLS, CH)
-    flat_cot = cotangent.reshape(ROWS * COLS, CH)
-    flat_deep = deep.reshape(ROWS * COLS, 128)
     w1 = weight_one.reshape(9, CH, CH)
     w2 = weight_two.reshape(9, CH, CH)
     half = ((CH // 2, 9 * CH), F32)
     pf, pd, ph, slope, keep_two, send_two = call(
         first_kernel,
-        "forward_block",
         [((EXT, 3 * CH), BF16), ((EXT, 3 * CH), BF16), ((MID, 3 * CH), BF16), ((MID, CH), F32), half, half],
         [
             pltpu.VMEM((EXT + 16, CH), F32),
@@ -381,23 +433,24 @@
             pltpu.VMEM((CH, INNER), BF16),
         ],
         scal, flat_field, flat_cot, flat_deep, west, east, south, north, fold, w1, bias_one.reshape(1, CH),
+        flops=3 * 10**9,
     )
     swap = [(0, 1), (1, 0)]
     came_two = lax.ppermute(send_two, "c", swap)
     pe, keep_one, send_one = call(
         second_kernel,
-        "backward_block",
         [((MID, 3 * CH), BF16), half, half],
         [pltpu.VMEM((MID + 16, CH), F32), pltpu.VMEM((CH, INNER), BF16)],
         scal, pd, pf, slope, w2,
+        flops=3 * 10**9,
     )
     came_one = lax.ppermute(send_one, "c", swap)
     output, input_grad = call(
         third_kernel,
-        "outputs_block",
         [((ROWS * COLS, CH), BF16), ((ROWS * COLS, CH), BF16)],
         [],
-        scal, ph, pe, pf, pd, flat_deep, w1, w2, bias_two.reshape(1, CH),
+        scal, ph, pe, flat_field, flat_cot, flat_deep, w1, w2, bias_two.reshape(1, CH),
+        flops=3 * 10**9,
     )
 
     n_p = lax.axis_size("yl") * lax.axis_size("x") * lax.axis_size("yh")
@@ -416,7 +469,6 @@
     other = lax.ppermute(mine, "c", swap)
     grad_one, grad_two = call(
         last_kernel,
-        "kernel_grads",
         [((9 * CH, CH), F32), ((9 * CH, CH), F32)],
         [],
         scal, mine, other,
@@ -433,7 +485,7 @@
     fine = Mesh(mesh.devices.reshape(SPLIT + (2, 2)), ZONAL + MERID)
     cells = P(MERID, ZONAL, None)
     return jax.shard_map(
-        shards,
+        block,
         mesh=fine,
         in_specs=(cells, P(), P(), P(), P(), P(MERID, ZONAL), P(), cells),
         out_specs=(cells, cells, P(), P()),

time: 155 us -> 142 us (0.916); the launches traced: 156 us -> 141 us
  Pallas kernels: 30.4 us -> 20.6 us
  blocking collectives: 78.6 us -> 71.2 us
  other arithmetic: 3.73 us -> 0.62 us
  waiting for transfers between devices: 7.73 us -> 10.6 us
    pallas_call x4 -> x6, Pallas kernels: 30.4 us -> 20.6 us  [call(): pl.pallas_call(body, cost_estimate=pl.CostEstimate(flops=flops, bytes_acc...]
    all_to_all x4, blocking collectives: 78.6 us -> 71.2 us  [the longest x1 32.1 us: block(): sums = lax.all_to_all(sums.reshape(n_p, rows, width), PLANE, 0, 0)]
    unnamed x19 -> x29, local copies, waits for them, and re-layouts: 1.11 us -> 7.46 us
    slice x13 -> x2, local copies, waits for them, and re-layouts: 5.01 us -> 1.21 us  [the longest x1 1.2 us: block(): shift = (fold_partner[0] + 1) % (n_z * COLS)]
    ppermute x7, waiting for transfers between devices: 7.72 us -> 10.6 us  [the longest x1 5.07 us: block(): lax.ppermute(east_edge, ZONAL, [(i, (i + 1) % n_z) for i in range(n_z)])]
    ppermute x3 -> x4, starting transfers between devices: 2.68 us -> 4.12 us  [hop(): return lax.ppermute(rows, ZONAL + MERID, route)]
  transfers between devices with their start and end apart: 10 -> 11, of which waited for: 2 -> 3; matrix products, arithmetic and copies ran while one was open for 3% -> 1% of each run, Pallas kernels for 11% -> 7%
where the time goes in v2:
time: 142 us; the launch traced here: 141 us
  blocking collectives  71.2 us (50%)
  starting transfers between devices  27.5 us (19%)
  Pallas kernels  20.6 us (15%)
  waiting for transfers between devices  10.6 us (7%)
  local copies, waits for them, and re-layouts  8.78 us (6%)
  between operations  1.59 us (1%)
    all_to_all x1, blocking collectives, block(): sums = lax.all_to_all(sums.reshape(n_p, rows, width), PLANE, 0, 0)  32.1 us
    pallas_call x6, Pallas kernels, call(): pl.pallas_call(body, cost_estimate=pl.CostEstimate(flops=flops, bytes_acc...  20.6 us
    all_to_all x1, blocking collectives, block(): lax.all_to_all(jnp.broadcast_to(line[None], (n_p, rows, width)), PLANE, 0...  18.4 us
    all_to_all x1, blocking collectives, block(): sums = lax.all_to_all(sums.reshape(n_low, part * 36, 128), 'z', 0, 0)  10.9 us
    all_to_all x1, blocking collectives, block(): lax.all_to_all(jnp.broadcast_to(piece[None], (n_low, part * 36, 128)), 'z...  9.78 us
    ppermute x1, starting transfers between devices, block(): lax.ppermute(west_edge, ZONAL, [((i + 1) % n_z, i) for i in range(n_z)])  9.68 us
    unnamed x29, local copies, waits for them, and re-layouts  7.46 us
    ppermute x1, starting transfers between devices, block(): south = lax.ppermute(upper, MERID, [(i, i + 1) for i in range(n_m - 1)])  6.52 us
  transfers between devices with their start and end apart: 11, of which 3 were waited for; matrix products, arithmetic and copies ran while one was open for 1% of the time, Pallas kernels for 7%

profile of v2, /device:TPU:1, one launch (start us, length us, event | category | flops | bytes accessed | tf_op | source)
XLA Modules:
  0.0 140.9 jit_solution(13676691417099552179)
XLA Ops:
  0.7 1.0 copy-done
  1.7 1.0 copy-done.2
  2.7 0.7 copy-done.4
  3.4 0.3 shard_map.111
  3.7 0.8 collective-permute-start.18
  4.5 9.7 %collective-permute-start.17 = (bf16[32,640]{1,0:T(8,128)(2,1)S(1)}, bf16[32,640]{1,0:T(8,128)(2,1)S(1)}, u32[]{:S(2)}, u32[]{:S(2)}) collective-permute-start(bf16[32,640]{1,0:T(8,128)(2,1)S(1)} %get-tuple-element.65), channel_id=1, source_target_pairs={{4,0},{8,4},{12,8},{16,12},{20,16},{24,20},{28,24},{32,28},{36,32}... | collective-permute-start | bytes 122888 | tf_op jit(solution)/shard_map/ppermute | solution.py:395
  14.2 0.6 collective-permute-start.19
  14.9 1.2 slice.6
  16.9 5.1 %collective-permute-done.16.west_ref = bf16[32,640]{1,0:T(8,128)(2,1)S(1)} collective-permute-done((bf16[32,640]{1,0:T(8,128)(2,1)S(1)}, bf16[32,640]{1,0:T(8,128)(2,1)S(1)}, u32[]{:S(2)}, u32[]{:S(2)}) %collective-permute-start.16) | collective-permute-done | bytes 40992 | tf_op jit(solution)/shard_map/ppermute | solution.py:394
  22.0 0.8 shard_map.112
  22.8 6.5 %collective-permute-start.20 = (bf16[144,640]{1,0:T(8,128)(2,1)S(1)}, bf16[144,640]{1,0:T(8,128)(2,1)S(1)}, u32[]{:S(2)}, u32[]{:S(2)}) collective-permute-start(bf16[144,640]{1,0:T(8,128)(2,1)S(1)} %get-tuple-element.68), channel_id=1, source_target_pairs={{0,1},{1,2},{2,3},{4,5},{5,6},{6,7},{8,9},{9,10},{10,11},{12,13},{... | collective-permute-start | bytes 552968 | tf_op jit(solution)/shard_map/ppermute | solution.py:409
  29.3 1.9 %collective-permute-start.21 = (bf16[144,640]{1,0:T(8,128)(2,1)S(1)}, bf16[144,640]{1,0:T(8,128)(2,1)S(1)}, u32[]{:S(2)}, u32[]{:S(2)}) collective-permute-start(bf16[144,640]{1,0:T(8,128)(2,1)S(1)} %get-tuple-element.69), channel_id=1, source_target_pairs={{1,0},{2,1},{3,2},{5,4},{6,5},{7,6},{9,8},{10,9},{11,10},{13,12},{... | collective-permute-start | bytes 552968 | tf_op jit(solution)/shard_map/ppermute | solution.py:410
  31.3 1.4 conditional.2
  31.3 1.3 collective-permute-start.4
  32.6 1.3 conditional.3
  32.6 1.3 collective-permute-start.9
  34.0 3.7 %collective-permute-done.21.north_ref = bf16[144,640]{1,0:T(8,128)(2,1)S(1)} collective-permute-done((bf16[144,640]{1,0:T(8,128)(2,1)S(1)}, bf16[144,640]{1,0:T(8,128)(2,1)S(1)}, u32[]{:S(2)}, u32[]{:S(2)}) %collective-permute-start.21) | collective-permute-done | bytes 184352 | tf_op jit(solution)/shard_map/ppermute | solution.py:410
  37.7 1.3 copy-done.5
  38.9 6.4 %shard_map.113 = (bf16[1456,768]{1,0:T(8,128)(2,1)S(1)}, bf16[1456,768]{1,0:T(8,128)(2,1)S(1)}, bf16[1304,768]{1,0:T(8,128)(2,1)S(1)}, f32[1304,256]{1,0:T(8,128...) custom-call(s32[3]{0:T(128)S(1)} %pad_add_fusion.scal_ref, bf16[1024,256]{1,0:T(8,128)(2,1)S(1)} %bitcast.27, ...), custom_call_target="tpu_custom_call" | custom-call | flops 3000000000 | bytes 13296652 | tf_op jit(solution)/shard_map/pallas_call | solution.py:354
  45.3 1.3 copy-done.10
  46.6 5.3 %shard_map.114 = (bf16[1304,768]{1,0:T(8,128)(2,1)S(1)}, f32[128,2304]{1,0:T(8,128)S(1)}, f32[128,2304]{1,0:T(8,128)S(1)}) custom-call(s32[3]{0:T(128)S(1)} %pad_add_fusion.scal_ref, bf16[1456,768]{1,0:T(8,128)(2,1)S(1)} %get-tuple-element.72.pd_ref, bf16[1456,768]{1,0:T(8,128)(2,1)S(1)} %get-tuple-element.73.pf_ref, ...), custom_call_target="tpu_custom_call" | custom-call | flops 3000000000 | bytes 11350028 | tf_op jit(solution)/shard_map/pallas_call | solution.py:354
  51.9 0.6 collective-permute-start.22
  52.6 0.5 copy-done.12
  53.2 1.8 %collective-permute-done.22 = f32[128,2304]{1,0:T(8,128)S(1)} collective-permute-done((f32[128,2304]{1,0:T(8,128)S(1)}, f32[128,2304]{1,0:T(8,128)S(1)}, u32[]{:S(2)}, u32[]{:S(2)}) %collective-permute-start.22) | collective-permute-done | bytes 1179680 | tf_op jit(solution)/shard_map/ppermute | solution.py:447
  55.2 32.1 %all_to_all.20 = bf16[16,8,4608]{2,1,0:T(8,128)(2,1)S(1)} all-to-all(bf16[16,8,4608]{2,1,0:T(8,128)(2,1)S(1)} %pad_maximum_fusion), channel_id=1, replica_groups=mesh['yl'=2,'x'=4,'z'=8,'yh'=2,'c'=2] {'yl','x','yh'}, dimensions={0} | all-to-all | bytes 2359296 | tf_op jit(solution)/shard_map/all_to_all | solution.py:460
  87.5 10.9 %all_to_all.21 = f32[8,36,128]{2,1,0:T(8,128)S(1)} all-to-all(f32[8,36,128]{2,1,0:T(8,128)S(1)} %copy.12), channel_id=1, replica_groups=mesh['yl'=2,'x'=4,'z'=8,'yh'=2,'c'=2] {'z'}, dimensions={0} | all-to-all | bytes 294912 | tf_op jit(solution)/shard_map/all_to_all | solution.py:463
  98.4 9.8 %all_to_all.22 = bf16[8,36,128]{2,1,0:T(8,128)(2,1)S(1)} all-to-all(bf16[8,36,128]{2,1,0:T(8,128)(2,1)S(1)} %broadcast_in_dim.6), channel_id=1, replica_groups=mesh['yl'=2,'x'=4,'z'=8,'yh'=2,'c'=2] {'z'}, dimensions={0} | all-to-all | bytes 147456 | tf_op jit(solution)/shard_map/all_to_all | solution.py:465
  108.3 18.4 %all_to_all.23 = bf16[16,8,4608]{2,1,0:T(8,128)(2,1)S(1)} all-to-all(bf16[16,8,4608]{2,1,0:T(8,128)(2,1)S(1)} %broadcast_in_dim.15), channel_id=1, replica_groups=mesh['yl'=2,'x'=4,'z'=8,'yh'=2,'c'=2] {'yl','x','yh'}, dimensions={0} | all-to-all | bytes 2359296 | tf_op jit(solution)/shard_map/all_to_all | solution.py:467
  126.7 4.6 %collective-permute-start.24 = (bf16[128,4608]{1,0:T(8,128)(2,1)S(1)}, bf16[128,4608]{1,0:T(8,128)(2,1)S(1)}, u32[]{:S(2)}, u32[]{:S(2)}) collective-permute-start(bf16[128,4608]{1,0:T(8,128)(2,1)S(1)} %bitcast.24), channel_id=1, source_target_pairs={{0,1},{1,0},{2,3},{3,2},{4,5},{5,4},{6,7},{7,6},{8,9},{9,8},{10,11... | collective-permute-start | bytes 3538952 | tf_op jit(solution)/shard_map/ppermute | solution.py:469
  131.4 1.6 %copy-done.13 = bf16[1304,768]{1,0:T(8,128)(2,1)S(1)} copy-done((bf16[1304,768]{1,0:T(8,128)(2,1)S(1)}, bf16[1304,768]{1,0:T(8,128)(2,1)}, u32[]{:S(2)}) %copy-start.13) | copy-done | bytes 2002968
  132.9 4.6 %shard_map.115 = (bf16[1024,256]{1,0:T(8,128)(2,1)}, bf16[1024,256]{1,0:T(8,128)(2,1)}) custom-call(s32[3]{0:T(128)S(1)} %pad_add_fusion.scal_ref, bf16[1304,768]{1,0:T(8,128)(2,1)S(1)} %copy-done.11, bf16[1304,768]{1,0:T(8,128)(2,1)S(1)} %copy-done.13, bf16[1024,256]{1,0:T(8,128)(2,1)S(1)} %bitcast.28, bf16[1024,256]{1,0:T(8,128)(2,1)S(1)} %bitcast.31, ...), custom_call_target="tpu_custom_call" | custom-call | flops 3000000000 | bytes 8725516 | tf_op jit(solution)/shard_map/pallas_call | solution.py:354
  137.6 3.3 %shard_map.116 = (f32[2304,256]{1,0:T(8,128)}, f32[2304,256]{1,0:T(8,128)}) custom-call(s32[3]{0:T(128)S(1)} %pad_add_fusion.scal_ref, bf16[128,4608]{1,0:T(8,128)(2,1)S(1)} %bitcast.25, bf16[128,4608]{1,0:T(8,128)(2,1)S(1)} %collective-permute-done.24.other_ref), custom_call_target="tpu_custom_call" | custom-call | flops 10000000 | bytes 7077900 | tf_op jit(solution)/shard_map/pallas_call | solution.py:354
  (42 shorter events, 0.9 us)
Async XLA Ops:
  0.6 37.0 %copy-start.8 = (f32[256]{0:T(256)S(1)}, f32[256]{0:T(256)}, u32[]{:S(2)}) copy-start(f32[256]{0:T(256)} %param.26) | copy-start | bytes 3076
  0.6 1.0 copy-start
  1.7 1.0 copy-start.2
  2.7 0.7 copy-start.4
  3.4 34.2 %copy-start.1 = (bf16[16,64,256]{2,1,0:T(8,128)(2,1)S(1)}, bf16[16,64,256]{2,1,0:T(8,128)(2,1)}, u32[]{:S(2)}) copy-start(bf16[16,64,256]{2,1,0:T(8,128)(2,1)} %param.24) | copy-start | bytes 1572868
  3.4 34.2 %copy-start.3 = (bf16[16,64,256]{2,1,0:T(8,128)(2,1)S(1)}, bf16[16,64,256]{2,1,0:T(8,128)(2,1)}, u32[]{:S(2)}) copy-start(bf16[16,64,256]{2,1,0:T(8,128)(2,1)} %param.31) | copy-start | bytes 1572868
  3.7 18.3 %collective-permute-start.18 = (bf16[128,640]{1,0:T(8,128)(2,1)S(1)}, bf16[128,640]{1,0:T(8,128)(2,1)S(1)}, u32[]{:S(2)}, u32[]{:S(2)}) collective-permute-start(bf16[128,640]{1,0:T(8,128)(2,1)S(1)} %get-tuple-element.66.top_ref), channel_id=1, source_target_pairs={{3,255},{7,3},{11,7},{15,11},{19,15},{23,19},{27,23},{31,27},{35,3... | collective-permute-start | bytes 491528 | tf_op jit(solution)/shard_map/ppermute | solution.py:390
  4.5 12.4 %collective-permute-start.17 = (bf16[32,640]{1,0:T(8,128)(2,1)S(1)}, bf16[32,640]{1,0:T(8,128)(2,1)S(1)}, u32[]{:S(2)}, u32[]{:S(2)}) collective-permute-start(bf16[32,640]{1,0:T(8,128)(2,1)S(1)} %get-tuple-element.65), channel_id=1, source_target_pairs={{4,0},{8,4},{12,8},{16,12},{20,16},{24,20},{28,24},{32,28},{36,32}... | collective-permute-start | bytes 122888 | tf_op jit(solution)/shard_map/ppermute | solution.py:395
  14.2 2.7 %collective-permute-start.19 = (bf16[4,640]{1,0:T(4,128)(2,1)S(1)}, bf16[4,640]{1,0:T(4,128)(2,1)S(1)}, u32[]{:S(2)}, u32[]{:S(2)}) collective-permute-start(bf16[4,640]{1,0:T(4,128)(2,1)S(1)} %slice.7), channel_id=1, source_target_pairs={{3,251},{7,255},{11,3},{15,7},{19,11},{23,15},{27,19},{31,23},{35,... | collective-permute-start | bytes 15368 | tf_op jit(solution)/shard_map/ppermute | solution.py:390
  14.8 7.1 %collective-permute-start.16 = (bf16[32,640]{1,0:T(8,128)(2,1)S(1)}, bf16[32,640]{1,0:T(8,128)(2,1)S(1)}, u32[]{:S(2)}, u32[]{:S(2)}) collective-permute-start(bf16[32,640]{1,0:T(8,128)(2,1)S(1)} %get-tuple-element.64), channel_id=1, source_target_pairs={{0,4},{4,8},{8,12},{12,16},{16,20},{20,24},{24,28},{28,32},{32,36}... | collective-permute-start | bytes 122888 | tf_op jit(solution)/shard_map/ppermute | solution.py:394
  22.8 11.2 %collective-permute-start.20 = (bf16[144,640]{1,0:T(8,128)(2,1)S(1)}, bf16[144,640]{1,0:T(8,128)(2,1)S(1)}, u32[]{:S(2)}, u32[]{:S(2)}) collective-permute-start(bf16[144,640]{1,0:T(8,128)(2,1)S(1)} %get-tuple-element.68), channel_id=1, source_target_pairs={{0,1},{1,2},{2,3},{4,5},{5,6},{6,7},{8,9},{9,10},{10,11},{12,13},{... | collective-permute-start | bytes 552968 | tf_op jit(solution)/shard_map/ppermute | solution.py:409
  29.3 8.4 %collective-permute-start.21 = (bf16[144,640]{1,0:T(8,128)(2,1)S(1)}, bf16[144,640]{1,0:T(8,128)(2,1)S(1)}, u32[]{:S(2)}, u32[]{:S(2)}) collective-permute-start(bf16[144,640]{1,0:T(8,128)(2,1)S(1)} %get-tuple-element.69), channel_id=1, source_target_pairs={{1,0},{2,1},{3,2},{5,4},{6,5},{7,6},{9,8},{10,9},{11,10},{13,12},{... | collective-permute-start | bytes 552968 | tf_op jit(solution)/shard_map/ppermute | solution.py:410
  31.3 1.3 collective-permute-start.4
  32.6 1.3 collective-permute-start.9
  37.7 1.3 copy-start.5
  38.9 7.7 %copy-start.7 = (bf16[3,3,256,256]{3,2,1,0:T(8,128)(2,1)S(1)}, bf16[3,3,256,256]{3,2,1,0:T(8,128)(2,1)}, u32[]{:S(2)}) copy-start(bf16[3,3,256,256]{3,2,1,0:T(8,128)(2,1)} %param.27) | copy-start | bytes 3538948
  45.3 1.3 copy-start.10
  46.6 5.9 %collective-permute-start.23 = (f32[128,2304]{1,0:T(8,128)S(1)}, f32[128,2304]{1,0:T(8,128)S(1)}, u32[]{:S(2)}, u32[]{:S(2)}) collective-permute-start(f32[128,2304]{1,0:T(8,128)S(1)} %get-tuple-element.81), channel_id=1, source_target_pairs={{0,1},{1,0},{2,3},{3,2},{4,5},{5,4},{6,7},{7,6},{8,9},{9,8},{10,11... | collective-permute-start | bytes 3538952 | tf_op jit(solution)/shard_map/ppermute | solution.py:439
  51.9 1.3 copy-start.12
  51.9 3.1 %collective-permute-start.22 = (f32[128,2304]{1,0:T(8,128)S(1)}, f32[128,2304]{1,0:T(8,128)S(1)}, u32[]{:S(2)}, u32[]{:S(2)}) collective-permute-start(f32[128,2304]{1,0:T(8,128)S(1)} %get-tuple-element.79), channel_id=1, source_target_pairs={{0,1},{1,0},{2,3},{3,2},{4,5},{5,4},{6,7},{7,6},{8,9},{9,8},{10,11... | collective-permute-start | bytes 3538952 | tf_op jit(solution)/shard_map/ppermute | solution.py:447
  108.2 23.2 %copy-start.11 = (bf16[1304,768]{1,0:T(8,128)(2,1)S(1)}, bf16[1304,768]{1,0:T(8,128)(2,1)}, u32[]{:S(2)}) copy-start(bf16[1304,768]{1,0:T(8,128)(2,1)} %copy-done.10) | copy-start | bytes 6008836
  108.3 23.1 %copy-start.6 = (bf16[3,3,256,256]{3,2,1,0:T(8,128)(2,1)S(1)}, bf16[3,3,256,256]{3,2,1,0:T(8,128)(2,1)}, u32[]{:S(2)}) copy-start(bf16[3,3,256,256]{3,2,1,0:T(8,128)(2,1)} %param.25) | copy-start | bytes 3538948
  108.3 23.0 %copy-start.9 = (f32[256]{0:T(256)S(1)}, f32[256]{0:T(256)}, u32[]{:S(2)}) copy-start(f32[256]{0:T(256)} %param.28) | copy-start | bytes 3076
  126.7 10.8 %collective-permute-start.24 = (bf16[128,4608]{1,0:T(8,128)(2,1)S(1)}, bf16[128,4608]{1,0:T(8,128)(2,1)S(1)}, u32[]{:S(2)}, u32[]{:S(2)}) collective-permute-start(bf16[128,4608]{1,0:T(8,128)(2,1)S(1)} %bitcast.24), channel_id=1, source_target_pairs={{0,1},{1,0},{2,3},{3,2},{4,5},{5,4},{6,7},{7,6},{8,9},{9,8},{10,11... | collective-permute-start | bytes 3538952 | tf_op jit(solution)/shard_map/ppermute | solution.py:469
  131.4 1.6 %copy-start.13 = (bf16[1304,768]{1,0:T(8,128)(2,1)S(1)}, bf16[1304,768]{1,0:T(8,128)(2,1)}, u32[]{:S(2)}) copy-start(bf16[1304,768]{1,0:T(8,128)(2,1)} %copy-done.12) | copy-start | bytes 6008836

commit v3 on v2

--- a/solution.py
+++ b/solution.py
@@ -88,7 +88,18 @@
             send_ref[:, at : at + CH] = jnp.where(core == 0, high, low)
 
 
-def pack_kernel(field_ref, cot_ref, dep_ref, deep_ref, top_ref, low_ref, west_ref, east_ref, edge):
+def pack_kernel(
+    field_far, cot_far, dep_far, deep_ref, top_ref, low_ref, west_ref, east_ref, far_ref,
+    edge, field_ref, cot_ref, dep_ref, sems,
+):
+    copies = [
+        pltpu.make_async_copy(dep_far, dep_ref, sems.at[0]),
+        pltpu.make_async_copy(field_far, field_ref, sems.at[1]),
+        pltpu.make_async_copy(cot_far, cot_ref, sems.at[2]),
+    ]
+    for copy in copies:
+        copy.start()
+    copies[0].wait()
     eye = (
         lax.broadcasted_iota(jnp.int32, (COLS, COLS), 0) == lax.broadcasted_iota(jnp.int32, (COLS, COLS), 1)
     ).astype(F32)
@@ -103,6 +114,8 @@
     for y in range(ROWS):
         line = dep_ref[y : y + 1, :].astype(F32)
         deep_ref[y * COLS : (y + 1) * COLS, :] = dot((eye * line).astype(BF16), ones).astype(BF16)
+    copies[1].wait()
+    copies[2].wait()
     for out_ref, first in ((top_ref, ROWS - 2), (low_ref, 0)):
         at = first * COLS
         out_ref[:, 0:CH] = field_ref[at : at + 2 * COLS, :]
@@ -116,6 +129,8 @@
             edge[cells, CH : 2 * CH] = masked(at, 16)[skip : skip + 2]
             edge[cells, 2 * CH : LANES] = deep_ref[at : at + 16, :].astype(F32)[skip : skip + 2]
         out_ref[...] = edge[...].astype(BF16)
+        if skip == 0:
+            far_ref[...] = edge[2 * ROWS - 4 : 2 * ROWS, :].astype(BF16)
 
 
 def strip_kernel(
@@ -140,6 +155,8 @@
     have = jnp.where(at < 128, at, jnp.where(at < 130, at - 130, jnp.where(at < 132, at - 2, -99)))
     pick = (want == have).astype(F32).astype(BF16)
     extra[...] = jnp.zeros(extra.shape, F32)
+    here = lax.broadcasted_iota(jnp.int32, (PITCH, 128), 0) == lax.broadcasted_iota(jnp.int32, (PITCH, 128), 1)
+    third = lax.broadcasted_iota(jnp.int32, (8, 128), 0) == 2
     for j in range(2):
         i = 1 - j
         y = ROWS - 2 + i
@@ -147,21 +164,33 @@
         extra[2:4, :] = far[2 * i : 2 * i + 2, :]
         rows = slice(i * COLS, (i + 1) * COLS)
         cells = jnp.concatenate([top_ref[rows, :], near_ref[rows, :], extra[...].astype(BF16)], axis=0)
-        strip[j * PITCH : (j + 1) * PITCH, :] = dot(pick, cells)
-    fold_ref[...] = strip[...].astype(BF16)
+        cells = dot(pick, cells)
+        fold_ref[j * PITCH : (j + 1) * PITCH, :] = cells[:, : 2 * CH].astype(BF16)
+        line = jnp.sum(jnp.where(here, cells[:, 2 * CH :], 0.0), axis=0, keepdims=True)
+        free = slice(j * PITCH + COLS, j * PITCH + COLS + 8)
+        tile = jnp.where(third, jnp.broadcast_to(line, (8, 128)), cells[COLS:, :128])
+        fold_ref[free, 0:128] = tile.astype(BF16)
 
 
 def first_kernel(
     scal_ref, field_ref, cot_ref, dep_ref, west_ref, east_ref, south_ref, north_ref, fold_ref,
-    w_ref, bias_ref,
-    pf_ref, pd_ref, ph_ref, slope_ref, keep_ref, send_ref,
-    ext, depth, west, east, south, north, back,
+    w_far, bias_ref,
+    pf_ref, pd_ref, ph_far, slope_ref, keep_ref, send_ref,
+    ext, depth, west, east, south, north, back, w_ref, ph_ref, sems,
 ):
+    weights = pltpu.make_async_copy(w_far, w_ref, sems.at[0])
+    weights.start()
     top = scal_ref[0] == 1
     west[...] = west_ref[...].astype(F32)
     east[...] = east_ref[...].astype(F32)
     south[...] = south_ref[...].astype(F32)
-    north[...] = north_ref[...].astype(F32) + fold_ref[...].astype(F32)
+    north[:, 0 : 2 * CH] = north_ref[:, 0 : 2 * CH].astype(F32) + fold_ref[...].astype(F32)
+    here = lax.broadcasted_iota(jnp.int32, (PITCH, 128), 0) == lax.broadcasted_iota(jnp.int32, (PITCH, 128), 1)
+    for j in range(2):
+        tile = fold_ref[j * PITCH + COLS : j * PITCH + COLS + 8, 0:128].astype(F32)
+        spread = jnp.where(here, jnp.broadcast_to(tile[2:3, :], (PITCH, 128)), 0.0).astype(BF16)
+        rows = slice(j * PITCH, (j + 1) * PITCH)
+        north[rows, 2 * CH :] = north_ref[rows, 2 * CH :].astype(F32) + dot(spread, jnp.ones((128, 128), BF16))
 
     def fill(out_ref, lanes, own, width, head):
         if head:
@@ -223,6 +252,7 @@
     shifted(pd_ref, ext, EXT)
 
     bias = bias_ref[...]
+    weights.wait()
 
     def finish(pre, p):
         count = pre.shape[0]
@@ -252,12 +282,15 @@
     slope_ref[at + 8 : at + 80, :] = slope[8:]
     ext[HEAD + MID : HEAD + MID + 8, :] = jnp.zeros((8, CH), F32)
     shifted(ph_ref, ext, MID)
+    leave = pltpu.make_async_copy(ph_ref, ph_far, sems.at[1])
+    leave.start()
     transposed_own(pd_ref, 144, back)
     weight_grad(keep_ref, send_ref, scal_ref[2], back, ph_ref, 0)
+    leave.wait()
 
 
 def second_kernel(
-    scal_ref, pd_ref, pf_ref, slope_ref, w_ref, pe_ref, keep_ref, send_ref, ext, back
+    scal_ref, pd_ref, pf_ref, slope_ref, w_ref, pe_far, keep_ref, send_ref, ext, back, pe_ref, sem
 ):
     top = scal_ref[0] == 1
     first = 72
@@ -291,8 +324,11 @@
     delta = (slope_ref[at : at + 8, :] * gap[:8]).astype(BF16).astype(F32)
     ext[HEAD + at : HEAD + at + 8, :] = jnp.where(beyond, delta, ext[HEAD + at : HEAD + at + 8, :])
     shifted(pe_ref, ext, MID)
+    leave = pltpu.make_async_copy(pe_ref, pe_far, sem)
+    leave.start()
     transposed_own(pe_ref, 72, back)
     weight_grad(keep_ref, send_ref, scal_ref[2], back, pf_ref, 72)
+    leave.wait()
 
 
 def third_kernel(
@@ -346,17 +382,19 @@
 
 VM = pl.BlockSpec(memory_space=pltpu.VMEM)
 SM = pl.BlockSpec(memory_space=pltpu.SMEM)
-
-
-def call(body, outs, scratch, *args, flops=10**7, scalars=True):
+HB = pl.BlockSpec(memory_space=pltpu.HBM)
+
+
+def call(body, outs, scratch, *args, flops=10**7, scalars=True, far_args=(), far_outs=()):
     moved = sum(math.prod(a.shape) * a.dtype.itemsize for a in args)
     moved += sum(math.prod(s) * jnp.dtype(t).itemsize for s, t in outs)
+    args = [pltpu.with_memory_space_constraint(a, pltpu.HBM) if k in far_args else a for k, a in enumerate(args)]
     return pl.pallas_call(
         body,
         cost_estimate=pl.CostEstimate(flops=flops, bytes_accessed=moved, transcendentals=0),
-        out_shape=[jax.ShapeDtypeStruct(s, t) for s, t in outs],
-        in_specs=([SM] if scalars else [VM]) + [VM] * (len(args) - 1),
-        out_specs=[VM] * len(outs),
+        out_shape=[pltpu.HBM(s, t) if k in far_outs else jax.ShapeDtypeStruct(s, t) for k, (s, t) in enumerate(outs)],
+        in_specs=[SM if scalars and k == 0 else HB if k in far_args else VM for k in range(len(args))],
+        out_specs=[HB if k in far_outs else VM for k in range(len(outs))],
         scratch_shapes=scratch,
         compiler_params=pltpu.CompilerParams(vmem_limit_bytes=24 << 20),
     )(*args)
@@ -373,11 +411,17 @@
     flat_field = field.reshape(ROWS * COLS, CH)
     flat_cot = cotangent.reshape(ROWS * COLS, CH)
     edge, rim = ((2 * ROWS, LANES), BF16), ((2 * COLS, LANES), BF16)
-    flat_deep, top_rows, low_rows, west_edge, east_edge = call(
+    flat_deep, top_rows, low_rows, west_edge, east_edge, far_edge = call(
         pack_kernel,
-        [((ROWS * COLS, 128), BF16), rim, rim, edge, edge],
-        [pltpu.VMEM((2 * ROWS, LANES), F32)],
-        flat_field, flat_cot, depth_levels, scalars=False,
+        [((ROWS * COLS, 128), BF16), rim, rim, edge, edge, ((4, LANES), BF16)],
+        [
+            pltpu.VMEM((2 * ROWS, LANES), F32),
+            pltpu.VMEM((ROWS * COLS, CH), BF16),
+            pltpu.VMEM((ROWS * COLS, CH), BF16),
+            pltpu.VMEM((ROWS, COLS), jnp.int32),
+            pltpu.SemaphoreType.DMA((3,)),
+        ],
+        flat_field, flat_cot, depth_levels, scalars=False, far_args=(0, 1, 2),
     )
 
     fold_partner, west_edge = lax.optimization_barrier((fold_partner, west_edge))
@@ -390,13 +434,13 @@
         return lax.ppermute(rows, ZONAL + MERID, route)
 
     near = hop(top_rows, lambda m: m - 1)
-    far = hop(west_edge[2 * ROWS - 4 :], lambda m: m - 2)
+    far = hop(far_edge, lambda m: m - 2)
     west = lax.ppermute(east_edge, ZONAL, [(i, (i + 1) % n_z) for i in range(n_z)])
     east = lax.ppermute(west_edge, ZONAL, [((i + 1) % n_z, i) for i in range(n_z)])
     strip = ((2 * PITCH, LANES), BF16)
     upper, lower, fold = call(
         strip_kernel,
-        [strip, strip, strip],
+        [strip, strip, ((2 * PITCH, 2 * CH), BF16)],
         [
             pltpu.VMEM((2 * ROWS, LANES), F32),
             pltpu.VMEM((2 * ROWS, LANES), F32),
@@ -406,16 +450,17 @@
         ],
         scal, top_rows, low_rows, west, east, near, far,
     )
+
+    def turn(rows, high):
+        return hop(rows, lambda m: n_low * ((n_high - 1 - m // n_low + high) % n_high) + m % n_low)
+
+    def slide(rows, low):
+        return hop(rows, lambda m: n_low * (m // n_low) + n_low - 1 + low - m % n_low)
+
+    fold = lax.switch(quotient // n_low, [lambda rows, h=h: turn(rows, h) for h in range(n_high)], fold)
+    upper, lower, fold = lax.optimization_barrier((upper, lower, fold))
     south = lax.ppermute(upper, MERID, [(i, i + 1) for i in range(n_m - 1)])
     north = lax.ppermute(lower, MERID, [(i + 1, i) for i in range(n_m - 1)])
-
-    def turn(rows, high):
-        return hop(rows, lambda m: n_low * ((n_high - 1 - m // n_low + high) % n_high) + m % n_low)
-
-    def slide(rows, low):
-        return hop(rows, lambda m: n_low * (m // n_low) + n_low - 1 + low - m % n_low)
-
-    fold = lax.switch(quotient // n_low, [lambda rows, h=h: turn(rows, h) for h in range(n_high)], fold)
     fold = lax.switch(quotient % n_low, [lambda rows, h=h: slide(rows, h) for h in range(n_low)], fold)
     w1 = weight_one.reshape(9, CH, CH)
     w2 = weight_two.reshape(9, CH, CH)
@@ -431,18 +476,26 @@
             pltpu.VMEM((2 * PITCH, LANES), F32),
             pltpu.VMEM((2 * PITCH, LANES), F32),
             pltpu.VMEM((CH, INNER), BF16),
+            pltpu.VMEM((9, CH, CH), BF16),
+            pltpu.VMEM((MID, 3 * CH), BF16),
+            pltpu.SemaphoreType.DMA((2,)),
         ],
         scal, flat_field, flat_cot, flat_deep, west, east, south, north, fold, w1, bias_one.reshape(1, CH),
-        flops=3 * 10**9,
+        flops=3 * 10**9, far_args=(9,), far_outs=(2,),
     )
     swap = [(0, 1), (1, 0)]
     came_two = lax.ppermute(send_two, "c", swap)
     pe, keep_one, send_one = call(
         second_kernel,
         [((MID, 3 * CH), BF16), half, half],
-        [pltpu.VMEM((MID + 16, CH), F32), pltpu.VMEM((CH, INNER), BF16)],
+        [
+            pltpu.VMEM((MID + 16, CH), F32),
+            pltpu.VMEM((CH, INNER), BF16),
+            pltpu.VMEM((MID, 3 * CH), BF16),
+            pltpu.SemaphoreType.DMA,
+        ],
         scal, pd, pf, slope, w2,
-        flops=3 * 10**9,
+        flops=3 * 10**9, far_outs=(0,),
     )
     came_one = lax.ppermute(send_one, "c", swap)
     output, input_grad = call(

time: 142 us -> 138 us (0.972)
  blocking collectives: 71.2 us -> 63.2 us
  waiting for transfers between devices: 10.6 us -> 18 us
  local copies, waits for them, and re-layouts: 8.78 us -> 2.92 us
  Pallas kernels: 20.6 us -> 23.5 us
    all_to_all x1, blocking collectives: 32.1 us -> 24.5 us  [block(): sums = lax.all_to_all(sums.reshape(n_p, rows, width), PLANE, 0, 0)]
    ppermute x1, waiting for transfers between devices: 3.68 us -> 10.5 us  [block(): north = lax.ppermute(lower, MERID, [(i + 1, i) for i in range(n_m - 1)])]
    unnamed x29 -> x17, local copies, waits for them, and re-layouts: 7.46 us -> 1.6 us
    pallas_call x6, Pallas kernels: 20.6 us -> 23.5 us  [call(): pl.pallas_call(body, cost_estimate=pl.CostEstimate(flops=flops, bytes_acc...]
where the time goes in v3:
time: 138 us; the launch traced here: 137 us
  blocking collectives  63.2 us (46%)
  starting transfers between devices  27.6 us (20%)
  Pallas kernels  23.5 us (17%)
  waiting for transfers between devices  18 us (13%)
  local copies, waits for them, and re-layouts  2.92 us (2%)
  between operations  1.54 us (1%)
    all_to_all x1, blocking collectives, block(): sums = lax.all_to_all(sums.reshape(n_p, rows, width), PLANE, 0, 0)  24.5 us
    pallas_call x6, Pallas kernels, call(): pl.pallas_call(body, cost_estimate=pl.CostEstimate(flops=flops, bytes_acc...  23.5 us
    all_to_all x1, blocking collectives, block(): lax.all_to_all(jnp.broadcast_to(line[None], (n_p, rows, width)), PLANE, 0...  18.1 us
    all_to_all x1, blocking collectives, block(): sums = lax.all_to_all(sums.reshape(n_low, part * 36, 128), 'z', 0, 0)  10.8 us
    ppermute x1, waiting for transfers between devices, block(): north = lax.ppermute(lower, MERID, [(i + 1, i) for i in range(n_m - 1)])  10.5 us
    all_to_all x1, blocking collectives, block(): lax.all_to_all(jnp.broadcast_to(piece[None], (n_low, part * 36, 128)), 'z...  9.78 us
    ppermute x1, starting transfers between devices, block(): lax.ppermute(west_edge, ZONAL, [((i + 1) % n_z, i) for i in range(n_z)])  9.68 us
    ppermute x1, starting transfers between devices, block(): south = lax.ppermute(upper, MERID, [(i, i + 1) for i in range(n_m - 1)])  6.5 us
  transfers between devices with their start and end apart: 11, of which 3 were waited for; matrix products, arithmetic and copies ran while one was open for 1% of the time, Pallas kernels for 7%

profile of v3, /device:TPU:1, one launch (start us, length us, event | category | flops | bytes accessed | tf_op | source)
XLA Modules:
  0.0 137.2 jit_solution(15584928232274112804)
XLA Ops:
  0.7 1.5 %shard_map.111 = (bf16[1024,128]{1,0:T(8,128)(2,1)S(1)}, bf16[128,640]{1,0:T(8,128)(2,1)S(1)}, bf16[128,640]{1,0:T(8,128)(2,1)S(1)}, bf16[32,640]{1,0:T(8,128)(2...) custom-call(bf16[1024,256]{1,0:T(8,128)(2,1)} %bitcast.26, bf16[1024,256]{1,0:T(8,128)(2,1)} %bitcast.29, ...), custom_call_target="tpu_custom_call" | custom-call | flops 10000000 | bytes 1729536 | tf_op jit(solution)/shard_map/pallas_call | solution.py:392
  2.1 0.7 collective-permute-start.18
  2.8 0.7 collective-permute-start.19
  3.5 9.7 %collective-permute-start.17 = (bf16[32,640]{1,0:T(8,128)(2,1)S(1)}, bf16[32,640]{1,0:T(8,128)(2,1)S(1)}, u32[]{:S(2)}, u32[]{:S(2)}) collective-permute-start(bf16[32,640]{1,0:T(8,128)(2,1)S(1)} %get-tuple-element.69), channel_id=1, source_target_pairs={{4,0},{8,4},{12,8},{16,12},{20,16},{24,20},{28,24},{32,28},{36,32}... | collective-permute-start | bytes 122888 | tf_op jit(solution)/shard_map/ppermute | solution.py:439
  13.2 1.2 slice.3
  15.1 5.1 %collective-permute-done.16.west_ref = bf16[32,640]{1,0:T(8,128)(2,1)S(1)} collective-permute-done((bf16[32,640]{1,0:T(8,128)(2,1)S(1)}, bf16[32,640]{1,0:T(8,128)(2,1)S(1)}, u32[]{:S(2)}, u32[]{:S(2)}) %collective-permute-start.16) | collective-permute-done | bytes 40992 | tf_op jit(solution)/shard_map/ppermute | solution.py:438
  20.2 0.8 shard_map.112
  21.0 1.3 conditional.2
  21.1 1.3 collective-permute-start.4
  22.4 6.5 %collective-permute-start.20 = (bf16[144,640]{1,0:T(8,128)(2,1)S(1)}, bf16[144,640]{1,0:T(8,128)(2,1)S(1)}, u32[]{:S(2)}, u32[]{:S(2)}) collective-permute-start(bf16[144,640]{1,0:T(8,128)(2,1)S(1)} %get-tuple-element.76), channel_id=1, source_target_pairs={{0,1},{1,2},{2,3},{4,5},{5,6},{6,7},{8,9},{9,10},{10,11},{12,13},{... | collective-permute-start | bytes 552968 | tf_op jit(solution)/shard_map/ppermute | solution.py:462
  28.9 1.9 %collective-permute-start.21 = (bf16[144,640]{1,0:T(8,128)(2,1)S(1)}, bf16[144,640]{1,0:T(8,128)(2,1)S(1)}, u32[]{:S(2)}, u32[]{:S(2)}) collective-permute-start(bf16[144,640]{1,0:T(8,128)(2,1)S(1)} %get-tuple-element.77), channel_id=1, source_target_pairs={{1,0},{2,1},{3,2},{5,4},{6,5},{7,6},{9,8},{10,9},{11,10},{13,12},{... | collective-permute-start | bytes 552968 | tf_op jit(solution)/shard_map/ppermute | solution.py:463
  30.8 1.3 conditional.3
  30.9 1.3 collective-permute-start.9
  32.2 10.5 %collective-permute-done.21.north_ref = bf16[144,640]{1,0:T(8,128)(2,1)S(1)} collective-permute-done((bf16[144,640]{1,0:T(8,128)(2,1)S(1)}, bf16[144,640]{1,0:T(8,128)(2,1)S(1)}, u32[]{:S(2)}, u32[]{:S(2)}) %collective-permute-start.21) | collective-permute-done | bytes 184352 | tf_op jit(solution)/shard_map/ppermute | solution.py:463
  42.7 8.0 %shard_map.113 = (bf16[1456,768]{1,0:T(8,128)(2,1)S(1)}, bf16[1456,768]{1,0:T(8,128)(2,1)S(1)}, bf16[1304,768]{1,0:T(8,128)(2,1)}, f32[1304,256]{1,0:T(8,128)S(1...) custom-call(s32[3]{0:T(128)S(1)} %pad_add_fusion.scal_ref, bf16[1024,256]{1,0:T(8,128)(2,1)S(1)} %bitcast.27, ...), custom_call_target="tpu_custom_call" | custom-call | flops 3000000000 | bytes 13259788 | tf_op jit(solution)/shard_map/pallas_call | solution.py:392
  50.8 0.3 collective-permute-start.23
  51.0 5.2 %shard_map.114 = (bf16[1304,768]{1,0:T(8,128)(2,1)}, f32[128,2304]{1,0:T(8,128)S(1)}, f32[128,2304]{1,0:T(8,128)S(1)}) custom-call(s32[3]{0:T(128)S(1)} %pad_add_fusion.scal_ref, bf16[1456,768]{1,0:T(8,128)(2,1)S(1)} %get-tuple-element.80.pd_ref, bf16[1456,768]{1,0:T(8,128)(2,1)S(1)} %get-tuple-element.81.pf_ref, ...), custom_call_target="tpu_custom_call" | custom-call | flops 3000000000 | bytes 11350028 | tf_op jit(solution)/shard_map/pallas_call | solution.py:392
  56.3 0.6 collective-permute-start.22
  56.8 0.1 fusion.1
  57.0 2.4 %collective-permute-done.22 = f32[128,2304]{1,0:T(8,128)S(1)} collective-permute-done((f32[128,2304]{1,0:T(8,128)S(1)}, f32[128,2304]{1,0:T(8,128)S(1)}, u32[]{:S(2)}, u32[]{:S(2)}) %collective-permute-start.22) | collective-permute-done | bytes 1179680 | tf_op jit(solution)/shard_map/ppermute | solution.py:500
  59.3 0.1 fusion
  59.4 0.1 pad_maximum_fusion
  59.5 24.5 %all_to_all.20 = bf16[16,8,4608]{2,1,0:T(8,128)(2,1)S(1)} all-to-all(bf16[16,8,4608]{2,1,0:T(8,128)(2,1)S(1)} %pad_maximum_fusion), channel_id=1, replica_groups=mesh['yl'=2,'x'=4,'z'=8,'yh'=2,'c'=2] {'yl','x','yh'}, dimensions={0} | all-to-all | bytes 2359296 | tf_op jit(solution)/shard_map/all_to_all | solution.py:513
  84.0 0.2 convert_reduce_fusion
  84.2 10.8 %all_to_all.21 = f32[8,36,128]{2,1,0:T(8,128)S(1)} all-to-all(f32[8,36,128]{2,1,0:T(8,128)S(1)} %copy.12), channel_id=1, replica_groups=mesh['yl'=2,'x'=4,'z'=8,'yh'=2,'c'=2] {'z'}, dimensions={0} | all-to-all | bytes 294912 | tf_op jit(solution)/shard_map/all_to_all | solution.py:516
  95.1 9.8 %all_to_all.22 = bf16[8,36,128]{2,1,0:T(8,128)(2,1)S(1)} all-to-all(bf16[8,36,128]{2,1,0:T(8,128)(2,1)S(1)} %broadcast_in_dim.6), channel_id=1, replica_groups=mesh['yl'=2,'x'=4,'z'=8,'yh'=2,'c'=2] {'z'}, dimensions={0} | all-to-all | bytes 147456 | tf_op jit(solution)/shard_map/all_to_all | solution.py:518
  104.9 0.1 broadcast_in_dim.15
  105.0 18.1 %all_to_all.23 = bf16[16,8,4608]{2,1,0:T(8,128)(2,1)S(1)} all-to-all(bf16[16,8,4608]{2,1,0:T(8,128)(2,1)S(1)} %broadcast_in_dim.15), channel_id=1, replica_groups=mesh['yl'=2,'x'=4,'z'=8,'yh'=2,'c'=2] {'yl','x','yh'}, dimensions={0} | all-to-all | bytes 2359296 | tf_op jit(solution)/shard_map/all_to_all | solution.py:520
  123.1 4.6 %collective-permute-start.24 = (bf16[128,4608]{1,0:T(8,128)(2,1)S(1)}, bf16[128,4608]{1,0:T(8,128)(2,1)S(1)}, u32[]{:S(2)}, u32[]{:S(2)}) collective-permute-start(bf16[128,4608]{1,0:T(8,128)(2,1)S(1)} %bitcast.24), channel_id=1, source_target_pairs={{0,1},{1,0},{2,3},{3,2},{4,5},{5,4},{6,7},{7,6},{8,9},{9,8},{10,11... | collective-permute-start | bytes 3538952 | tf_op jit(solution)/shard_map/ppermute | solution.py:522
  127.7 1.6 %copy-done.7 = bf16[1304,768]{1,0:T(8,128)(2,1)S(1)} copy-done((bf16[1304,768]{1,0:T(8,128)(2,1)S(1)}, bf16[1304,768]{1,0:T(8,128)(2,1)}, u32[]{:S(2)}) %copy-start.7) | copy-done | bytes 2002968
  129.2 4.6 %shard_map.115 = (bf16[1024,256]{1,0:T(8,128)(2,1)}, bf16[1024,256]{1,0:T(8,128)(2,1)}) custom-call(s32[3]{0:T(128)S(1)} %pad_add_fusion.scal_ref, bf16[1304,768]{1,0:T(8,128)(2,1)S(1)} %copy-done.6, bf16[1304,768]{1,0:T(8,128)(2,1)S(1)} %copy-done.7, bf16[1024,256]{1,0:T(8,128)(2,1)S(1)} %bitcast.28, bf16[1024,256]{1,0:T(8,128)(2,1)S(1)} %bitcast.31, ...), custom_call_target="tpu_custom_call" | custom-call | flops 3000000000 | bytes 8725516 | tf_op jit(solution)/shard_map/pallas_call | solution.py:392
  133.9 3.3 %shard_map.116 = (f32[2304,256]{1,0:T(8,128)}, f32[2304,256]{1,0:T(8,128)}) custom-call(s32[3]{0:T(128)S(1)} %pad_add_fusion.scal_ref, bf16[128,4608]{1,0:T(8,128)(2,1)S(1)} %bitcast.25, bf16[128,4608]{1,0:T(8,128)(2,1)S(1)} %collective-permute-done.24.other_ref), custom_call_target="tpu_custom_call" | custom-call | flops 10000000 | bytes 7077900 | tf_op jit(solution)/shard_map/pallas_call | solution.py:392
  (29 shorter events, 0.2 us)
Async XLA Ops:
  0.6 42.1 %copy-start.1 = (bf16[16,64,256]{2,1,0:T(8,128)(2,1)S(1)}, bf16[16,64,256]{2,1,0:T(8,128)(2,1)}, u32[]{:S(2)}) copy-start(bf16[16,64,256]{2,1,0:T(8,128)(2,1)} %param.31) | copy-start | bytes 1572868
  0.6 42.1 %copy-start = (bf16[16,64,256]{2,1,0:T(8,128)(2,1)S(1)}, bf16[16,64,256]{2,1,0:T(8,128)(2,1)}, u32[]{:S(2)}) copy-start(bf16[16,64,256]{2,1,0:T(8,128)(2,1)} %param.24) | copy-start | bytes 1572868
  0.7 42.0 %copy-start.4 = (f32[256]{0:T(256)S(1)}, f32[256]{0:T(256)}, u32[]{:S(2)}) copy-start(f32[256]{0:T(256)} %param.26) | copy-start | bytes 3076
  2.1 18.1 %collective-permute-start.18 = (bf16[128,640]{1,0:T(8,128)(2,1)S(1)}, bf16[128,640]{1,0:T(8,128)(2,1)S(1)}, u32[]{:S(2)}, u32[]{:S(2)}) collective-permute-start(bf16[128,640]{1,0:T(8,128)(2,1)S(1)} %get-tuple-element.70.top_ref), channel_id=1, source_target_pairs={{3,255},{7,3},{11,7},{15,11},{19,15},{23,19},{27,23},{31,27},{35,3... | collective-permute-start | bytes 491528 | tf_op jit(solution)/shard_map/ppermute | solution.py:434
  2.8 12.3 %collective-permute-start.19 = (bf16[4,640]{1,0:T(4,128)(2,1)S(1)}, bf16[4,640]{1,0:T(4,128)(2,1)S(1)}, u32[]{:S(2)}, u32[]{:S(2)}) collective-permute-start(bf16[4,640]{1,0:T(4,128)(2,1)S(1)} %get-tuple-element.72), channel_id=1, source_target_pairs={{3,251},{7,255},{11,3},{15,7},{19,11},{23,15},{27,19},{31,23},{35,... | collective-permute-start | bytes 15368 | tf_op jit(solution)/shard_map/ppermute | solution.py:434
  3.5 11.7 %collective-permute-start.17 = (bf16[32,640]{1,0:T(8,128)(2,1)S(1)}, bf16[32,640]{1,0:T(8,128)(2,1)S(1)}, u32[]{:S(2)}, u32[]{:S(2)}) collective-permute-start(bf16[32,640]{1,0:T(8,128)(2,1)S(1)} %get-tuple-element.69), channel_id=1, source_target_pairs={{4,0},{8,4},{12,8},{16,12},{20,16},{24,20},{28,24},{32,28},{36,32}... | collective-permute-start | bytes 122888 | tf_op jit(solution)/shard_map/ppermute | solution.py:439
  13.1 7.1 %collective-permute-start.16 = (bf16[32,640]{1,0:T(8,128)(2,1)S(1)}, bf16[32,640]{1,0:T(8,128)(2,1)S(1)}, u32[]{:S(2)}, u32[]{:S(2)}) collective-permute-start(bf16[32,640]{1,0:T(8,128)(2,1)S(1)} %get-tuple-element.68), channel_id=1, source_target_pairs={{0,4},{4,8},{8,12},{12,16},{16,20},{20,24},{24,28},{28,32},{32,36}... | collective-permute-start | bytes 122888 | tf_op jit(solution)/shard_map/ppermute | solution.py:438
  21.1 1.3 collective-permute-start.4
  22.4 9.8 %collective-permute-start.20 = (bf16[144,640]{1,0:T(8,128)(2,1)S(1)}, bf16[144,640]{1,0:T(8,128)(2,1)S(1)}, u32[]{:S(2)}, u32[]{:S(2)}) collective-permute-start(bf16[144,640]{1,0:T(8,128)(2,1)S(1)} %get-tuple-element.76), channel_id=1, source_target_pairs={{0,1},{1,2},{2,3},{4,5},{5,6},{6,7},{8,9},{9,10},{10,11},{12,13},{... | collective-permute-start | bytes 552968 | tf_op jit(solution)/shard_map/ppermute | solution.py:462
  28.9 13.8 %collective-permute-start.21 = (bf16[144,640]{1,0:T(8,128)(2,1)S(1)}, bf16[144,640]{1,0:T(8,128)(2,1)S(1)}, u32[]{:S(2)}, u32[]{:S(2)}) collective-permute-start(bf16[144,640]{1,0:T(8,128)(2,1)S(1)} %get-tuple-element.77), channel_id=1, source_target_pairs={{1,0},{2,1},{3,2},{5,4},{6,5},{7,6},{9,8},{10,9},{11,10},{13,12},{... | collective-permute-start | bytes 552968 | tf_op jit(solution)/shard_map/ppermute | solution.py:463
  30.9 1.3 collective-permute-start.9
  42.7 8.3 %copy-start.3 = (bf16[3,3,256,256]{3,2,1,0:T(8,128)(2,1)S(1)}, bf16[3,3,256,256]{3,2,1,0:T(8,128)(2,1)}, u32[]{:S(2)}) copy-start(bf16[3,3,256,256]{3,2,1,0:T(8,128)(2,1)} %param.27) | copy-start | bytes 3538948
  50.8 6.1 %collective-permute-start.23 = (f32[128,2304]{1,0:T(8,128)S(1)}, f32[128,2304]{1,0:T(8,128)S(1)}, u32[]{:S(2)}, u32[]{:S(2)}) collective-permute-start(f32[128,2304]{1,0:T(8,128)S(1)} %get-tuple-element.89), channel_id=1, source_target_pairs={{0,1},{1,0},{2,3},{3,2},{4,5},{5,4},{6,7},{7,6},{8,9},{9,8},{10,11... | collective-permute-start | bytes 3538952 | tf_op jit(solution)/shard_map/ppermute | solution.py:487
  56.3 3.0 %collective-permute-start.22 = (f32[128,2304]{1,0:T(8,128)S(1)}, f32[128,2304]{1,0:T(8,128)S(1)}, u32[]{:S(2)}, u32[]{:S(2)}) collective-permute-start(f32[128,2304]{1,0:T(8,128)S(1)} %get-tuple-element.87), channel_id=1, source_target_pairs={{0,1},{1,0},{2,3},{3,2},{4,5},{5,4},{6,7},{7,6},{8,9},{9,8},{10,11... | collective-permute-start | bytes 3538952 | tf_op jit(solution)/shard_map/ppermute | solution.py:500
  104.8 22.8 %copy-start.6 = (bf16[1304,768]{1,0:T(8,128)(2,1)S(1)}, bf16[1304,768]{1,0:T(8,128)(2,1)}, u32[]{:S(2)}) copy-start(bf16[1304,768]{1,0:T(8,128)(2,1)} %get-tuple-element.79.ph_ref) | copy-start | bytes 6008836
  104.9 22.7 %copy-start.2 = (bf16[3,3,256,256]{3,2,1,0:T(8,128)(2,1)S(1)}, bf16[3,3,256,256]{3,2,1,0:T(8,128)(2,1)}, u32[]{:S(2)}) copy-start(bf16[3,3,256,256]{3,2,1,0:T(8,128)(2,1)} %param.25) | copy-start | bytes 3538948
  105.0 22.7 %copy-start.5 = (f32[256]{0:T(256)S(1)}, f32[256]{0:T(256)}, u32[]{:S(2)}) copy-start(f32[256]{0:T(256)} %param.28) | copy-start | bytes 3076
  123.1 10.8 %collective-permute-start.24 = (bf16[128,4608]{1,0:T(8,128)(2,1)S(1)}, bf16[128,4608]{1,0:T(8,128)(2,1)S(1)}, u32[]{:S(2)}, u32[]{:S(2)}) collective-permute-start(bf16[128,4608]{1,0:T(8,128)(2,1)S(1)} %bitcast.24), channel_id=1, source_target_pairs={{0,1},{1,0},{2,3},{3,2},{4,5},{5,4},{6,7},{7,6},{8,9},{9,8},{10,11... | collective-permute-start | bytes 3538952 | tf_op jit(solution)/shard_map/ppermute | solution.py:522
  127.7 1.6 %copy-start.7 = (bf16[1304,768]{1,0:T(8,128)(2,1)S(1)}, bf16[1304,768]{1,0:T(8,128)(2,1)}, u32[]{:S(2)}) copy-start(bf16[1304,768]{1,0:T(8,128)(2,1)} %get-tuple-element.83.pe_ref) | copy-start | bytes 6008836

commit v4 on v3

--- a/solution.py
+++ b/solution.py
@@ -89,7 +89,7 @@
 
 
 def pack_kernel(
-    field_far, cot_far, dep_far, deep_ref, top_ref, low_ref, west_ref, east_ref, far_ref,
+    field_far, cot_far, dep_far, deep_ref, top_ref, low_ref, west_ref, east_ref,
     edge, field_ref, cot_ref, dep_ref, sems,
 ):
     copies = [
@@ -128,18 +128,22 @@
             edge[cells, 0:CH] = field_ref[at : at + 16, :].astype(F32)[skip : skip + 2]
             edge[cells, CH : 2 * CH] = masked(at, 16)[skip : skip + 2]
             edge[cells, 2 * CH : LANES] = deep_ref[at : at + 16, :].astype(F32)[skip : skip + 2]
-        out_ref[...] = edge[...].astype(BF16)
-        if skip == 0:
-            far_ref[...] = edge[2 * ROWS - 4 : 2 * ROWS, :].astype(BF16)
+        if skip:
+            edge[2 * ROWS : 2 * ROWS + 8, :] = jnp.zeros((8, LANES), F32)
+            for k in range(2):
+                at = (ROWS - 2 + k) * COLS + column
+                cells = slice(2 * ROWS + k, 2 * ROWS + k + 1)
+                edge[cells, 0:CH] = field_ref[at : at + 16, :].astype(F32)[skip - 1 : skip]
+                edge[cells, CH : 2 * CH] = masked(at, 16)[skip - 1 : skip]
+                edge[cells, 2 * CH : LANES] = deep_ref[at : at + 16, :].astype(F32)[skip - 1 : skip]
+        out_ref[...] = edge[0 : out_ref.shape[0], :].astype(BF16)
 
 
 def strip_kernel(
-    scal_ref, top_ref, low_ref, west_ref, east_ref, near_ref, far_ref, upper_ref, lower_ref, fold_ref, west, east, far,
-    extra, strip,
+    scal_ref, top_ref, low_ref, west_ref, east_ref, near_ref, upper_ref, lower_ref, fold_ref, west, east, extra, strip,
 ):
     west[...] = west_ref[...].astype(F32)
     east[...] = east_ref[...].astype(F32)
-    far[...] = far_ref[...].astype(F32)
     strip[...] = jnp.zeros(strip.shape, F32)
     for out_ref, rows_ref, first in ((upper_ref, top_ref, ROWS - 2), (lower_ref, low_ref, 0)):
         for k in range(2):
@@ -152,7 +156,7 @@
     at = lax.broadcasted_iota(jnp.int32, (PITCH, 144), 1)
     want = 63 - jnp.where(to >= 70, to - PITCH, to) + scal_ref[1]
     want = jnp.where((to >= 66) & (to < 70), -98, want)
-    have = jnp.where(at < 128, at, jnp.where(at < 130, at - 130, jnp.where(at < 132, at - 2, -99)))
+    have = jnp.where(at < 128, at, jnp.where(at < 130, at - 130, jnp.where(at == 130, -3, -99)))
     pick = (want == have).astype(F32).astype(BF16)
     extra[...] = jnp.zeros(extra.shape, F32)
     here = lax.broadcasted_iota(jnp.int32, (PITCH, 128), 0) == lax.broadcasted_iota(jnp.int32, (PITCH, 128), 1)
@@ -161,7 +165,7 @@
         i = 1 - j
         y = ROWS - 2 + i
         extra[0:2, :] = west[2 * y : 2 * y + 2, :]
-        extra[2:4, :] = far[2 * i : 2 * i + 2, :]
+        extra[2:3, :] = west[2 * ROWS + i : 2 * ROWS + i + 1, :]
         rows = slice(i * COLS, (i + 1) * COLS)
         cells = jnp.concatenate([top_ref[rows, :], near_ref[rows, :], extra[...].astype(BF16)], axis=0)
         cells = dot(pick, cells)
@@ -181,7 +185,7 @@
     weights = pltpu.make_async_copy(w_far, w_ref, sems.at[0])
     weights.start()
     top = scal_ref[0] == 1
-    west[...] = west_ref[...].astype(F32)
+    west[...] = west_ref[0 : 2 * ROWS, :].astype(F32)
     east[...] = east_ref[...].astype(F32)
     south[...] = south_ref[...].astype(F32)
     north[:, 0 : 2 * CH] = north_ref[:, 0 : 2 * CH].astype(F32) + fold_ref[...].astype(F32)
@@ -366,6 +370,24 @@
     put(sums + taps(pe_ref, p - 144, 64, w1_ref, over, True), 15)
 
 
+def join_kernel(keep_one, came_one, keep_two, came_two, out_ref):
+    width = 9 * CH
+    for at in range(0, CH // 2, 16):
+        rows = slice(at, at + 16)
+        out_ref[rows, 0:width] = (keep_one[rows, :] + came_one[rows, :]).astype(BF16)
+        out_ref[rows, width:] = (keep_two[rows, :] + came_two[rows, :]).astype(BF16)
+
+
+def total_kernel(parts_ref, out_ref):
+    count, _, width = parts_ref.shape
+    step = 512
+    for at in range(0, width, step):
+        total = parts_ref[0, :, at : at + step].astype(F32)
+        for k in range(1, count):
+            total = total + parts_ref[k, :, at : at + step].astype(F32)
+        out_ref[:, at : at + step] = total
+
+
 def last_kernel(scal_ref, mine_ref, other_ref, one_ref, two_ref):
     first = scal_ref[2] == 0
     down = lax.broadcasted_iota(jnp.int32, (CH, CH), 0)
@@ -411,11 +433,11 @@
     flat_field = field.reshape(ROWS * COLS, CH)
     flat_cot = cotangent.reshape(ROWS * COLS, CH)
     edge, rim = ((2 * ROWS, LANES), BF16), ((2 * COLS, LANES), BF16)
-    flat_deep, top_rows, low_rows, west_edge, east_edge, far_edge = call(
+    flat_deep, top_rows, low_rows, west_edge, east_edge = call(
         pack_kernel,
-        [((ROWS * COLS, 128), BF16), rim, rim, edge, edge, ((4, LANES), BF16)],
+        [((ROWS * COLS, 128), BF16), rim, rim, edge, ((2 * ROWS + 8, LANES), BF16)],
         [
-            pltpu.VMEM((2 * ROWS, LANES), F32),
+            pltpu.VMEM((2 * ROWS + 8, LANES), F32),
             pltpu.VMEM((ROWS * COLS, CH), BF16),
             pltpu.VMEM((ROWS * COLS, CH), BF16),
             pltpu.VMEM((ROWS, COLS), jnp.int32),
@@ -425,8 +447,8 @@
     )
 
     fold_partner, west_edge = lax.optimization_barrier((fold_partner, west_edge))
-    shift = (fold_partner[0] + 1) % (n_z * COLS)
-    quotient, rest = shift // COLS, shift % COLS
+    shift = fold_partner[0] + 2
+    quotient, rest = shift // COLS % n_z, shift % COLS - 1
     scal = jnp.stack([(merid == n_m - 1).astype(jnp.int32), rest.astype(jnp.int32), core.astype(jnp.int32)])
 
     def hop(rows, target):
@@ -434,7 +456,6 @@
         return lax.ppermute(rows, ZONAL + MERID, route)
 
     near = hop(top_rows, lambda m: m - 1)
-    far = hop(far_edge, lambda m: m - 2)
     west = lax.ppermute(east_edge, ZONAL, [(i, (i + 1) % n_z) for i in range(n_z)])
     east = lax.ppermute(west_edge, ZONAL, [((i + 1) % n_z, i) for i in range(n_z)])
     strip = ((2 * PITCH, LANES), BF16)
@@ -442,13 +463,12 @@
         strip_kernel,
         [strip, strip, ((2 * PITCH, 2 * CH), BF16)],
         [
+            pltpu.VMEM((2 * ROWS + 8, LANES), F32),
             pltpu.VMEM((2 * ROWS, LANES), F32),
-            pltpu.VMEM((2 * ROWS, LANES), F32),
-            pltpu.VMEM((4, LANES), F32),
             pltpu.VMEM((16, LANES), F32),
             pltpu.VMEM((2 * PITCH, LANES), F32),
         ],
-        scal, top_rows, low_rows, west, east, near, far,
+        scal, top_rows, low_rows, west, east, near,
     )
 
     def turn(rows, high):
@@ -509,9 +529,9 @@
     n_p = lax.axis_size("yl") * lax.axis_size("x") * lax.axis_size("yh")
     rows = CH // 2 // n_p
     width = 18 * CH
-    sums = jnp.concatenate([keep_one + came_one, keep_two + came_two], axis=1).astype(BF16)
+    (sums,) = call(join_kernel, [((CH // 2, width), BF16)], [], keep_one, came_one, keep_two, came_two, scalars=False)
     sums = lax.all_to_all(sums.reshape(n_p, rows, width), PLANE, 0, 0)
-    sums = jnp.sum(sums.astype(F32), axis=0)
+    (sums,) = call(total_kernel, [((rows, width), F32)], [], sums, scalars=False)
     part = rows // n_low
     sums = lax.all_to_all(sums.reshape(n_low, part * 36, 128), "z", 0, 0)
     piece = jnp.sum(sums, axis=0).astype(BF16)

time: 138 us -> 135 us (0.978)
  waiting for transfers between devices: 18 us -> 15.8 us
    ppermute x1, waiting for transfers between devices: 10.5 us -> 8.08 us  [block(): north = lax.ppermute(lower, MERID, [(i + 1, i) for i in range(n_m - 1)])]
    ppermute x4 -> x3, starting transfers between devices: 3.97 us -> 3.31 us  [hop(): return lax.ppermute(rows, ZONAL + MERID, route)]
    pallas_call x6 -> x8, Pallas kernels: 23.5 us -> 23.9 us  [call(): pl.pallas_call(body, cost_estimate=pl.CostEstimate(flops=flops, bytes_acc...]
  transfers between devices with their start and end apart: 11 -> 10, of which waited for: 3 -> 3; matrix products, arithmetic and copies ran while one was open for 1% -> 1% of each run, Pallas kernels for 7% -> 7%
where the time goes in v4:
time: 135 us; the launch traced here: 134 us
  blocking collectives  63.2 us (47%)
  starting transfers between devices  26.9 us (20%)
  Pallas kernels  23.9 us (18%)
  waiting for transfers between devices  15.8 us (12%)
  local copies, waits for them, and re-layouts  2.92 us (2%)
  between operations  1.52 us (1%)
    all_to_all x1, blocking collectives, block(): sums = lax.all_to_all(sums.reshape(n_p, rows, width), PLANE, 0, 0)  24.5 us
    pallas_call x8, Pallas kernels, call(): pl.pallas_call(body, cost_estimate=pl.CostEstimate(flops=flops, bytes_acc...  23.9 us
    all_to_all x1, blocking collectives, block(): lax.all_to_all(jnp.broadcast_to(line[None], (n_p, rows, width)), PLANE, 0...  18.1 us
    all_to_all x1, blocking collectives, block(): sums = lax.all_to_all(sums.reshape(n_low, part * 36, 128), 'z', 0, 0)  10.8 us
    all_to_all x1, blocking collectives, block(): lax.all_to_all(jnp.broadcast_to(piece[None], (n_low, part * 36, 128)), 'z...  9.78 us
    ppermute x1, starting transfers between devices, block(): lax.ppermute(west_edge, ZONAL, [((i + 1) % n_z, i) for i in range(n_z)])  9.68 us
    ppermute x1, waiting for transfers between devices, block(): north = lax.ppermute(lower, MERID, [(i + 1, i) for i in range(n_m - 1)])  8.08 us
    ppermute x1, starting transfers between devices, block(): south = lax.ppermute(upper, MERID, [(i, i + 1) for i in range(n_m - 1)])  6.51 us
  transfers between devices with their start and end apart: 10, of which 3 were waited for; matrix products, arithmetic and copies ran while one was open for 1% of the time, Pallas kernels for 7%

profile of v4, /device:TPU:1, one launch (start us, length us, event | category | flops | bytes accessed | tf_op | source)
XLA Modules:
  0.0 134.3 jit_solution(1572011508493170722)
XLA Ops:
  0.7 1.5 %shard_map.111 = (bf16[1024,128]{1,0:T(8,128)(2,1)S(1)}, bf16[128,640]{1,0:T(8,128)(2,1)S(1)}, bf16[128,640]{1,0:T(8,128)(2,1)S(1)}, bf16[32,640]{1,0:T(8,128)(2,1)S(1)}, bf16[40,640]{1,0:T(8,128)(2,1)S(1)}) custom-call(bf16[1024,256]{1,0:T(8,128)(2,1)} %bitcast.25, bf16[1024,256]{1,0:T(8,128)(2,1)} %bitcast.28, s32[16,64]{1,0:T(8,128)} %dep_far.1), custom_call_target="tpu_custom_call" | custom-call | flops 10000000 | bytes 1734656 | tf_op jit(solution)/shard_map/pallas_call | solution.py:414
  2.1 0.7 collective-permute-start.18
  2.8 9.7 %collective-permute-start.17 = (bf16[32,640]{1,0:T(8,128)(2,1)S(1)}, bf16[32,640]{1,0:T(8,128)(2,1)S(1)}, u32[]{:S(2)}, u32[]{:S(2)}) collective-permute-start(bf16[32,640]{1,0:T(8,128)(2,1)S(1)} %get-tuple-element.68), channel_id=1, source_target_pairs={{4,0},{8,4},{12,8},{16,12},{20,16},{24,20},{28,24},{32,28},{36,32}... | collective-permute-start | bytes 122888 | tf_op jit(solution)/shard_map/ppermute | solution.py:460
  12.5 1.2 slice.3
  14.4 0.1 pad_add_fusion.scal_ref
  14.5 5.2 %collective-permute-done.16.west_ref = bf16[40,640]{1,0:T(8,128)(2,1)S(1)} collective-permute-done((bf16[40,640]{1,0:T(8,128)(2,1)S(1)}, bf16[40,640]{1,0:T(8,128)(2,1)S(1)}, u32[]{:S(2)}, u32[]{:S(2)}) %collective-permute-start.16) | collective-permute-done | bytes 51232 | tf_op jit(solution)/shard_map/ppermute | solution.py:459
  19.7 0.8 shard_map.112
  20.5 1.3 %conditional.2 = (bf16[144,512]{1,0:T(8,128)(2,1)}) conditional(s32[]{:T(128)} %clamp.6, bf16[144,512]{1,0:T(8,128)(2,1)S(1)} %get-tuple-element.73, bf16[144,512]{1,0:T(8,128)(2,1)S(1)} %get-tuple-element.73, bf16[144,512]{1,0:T(8,128)(2,1)S(1)} %get-tuple-element.73, ...), branch_computations={%region_0.1_spmd, %region_1.2_spmd, %region_2.3_spmd, %region_3.4_... | conditional | bytes 589872 | solution.py:480
  20.5 1.3 collective-permute-start.4
  21.8 6.5 %collective-permute-start.19 = (bf16[144,640]{1,0:T(8,128)(2,1)S(1)}, bf16[144,640]{1,0:T(8,128)(2,1)S(1)}, u32[]{:S(2)}, u32[]{:S(2)}) collective-permute-start(bf16[144,640]{1,0:T(8,128)(2,1)S(1)} %get-tuple-element.74), channel_id=1, source_target_pairs={{0,1},{1,2},{2,3},{4,5},{5,6},{6,7},{8,9},{9,10},{10,11},{12,13},{... | collective-permute-start | bytes 552968 | tf_op jit(solution)/shard_map/ppermute | solution.py:482
  28.3 1.9 %collective-permute-start.20 = (bf16[144,640]{1,0:T(8,128)(2,1)S(1)}, bf16[144,640]{1,0:T(8,128)(2,1)S(1)}, u32[]{:S(2)}, u32[]{:S(2)}) collective-permute-start(bf16[144,640]{1,0:T(8,128)(2,1)S(1)} %get-tuple-element.75), channel_id=1, source_target_pairs={{1,0},{2,1},{3,2},{5,4},{6,5},{7,6},{9,8},{10,9},{11,10},{13,12},{... | collective-permute-start | bytes 552968 | tf_op jit(solution)/shard_map/ppermute | solution.py:483
  30.3 1.3 %conditional.3 = (bf16[144,512]{1,0:T(8,128)(2,1)}) conditional(s32[]{:T(128)} %clamp.7, bf16[144,512]{1,0:T(8,128)(2,1)} %get-tuple-element.90, bf16[144,512]{1,0:T(8,128)(2,1)} %get-tuple-element.90, bf16[144,512]{1,0:T(8,128)(2,1)} %get-tuple-element.90, bf16[144,512]{1,0:T(8,128)(2,1)} %get-tuple-element.90, ...), branch_computations={%region_8.9_spmd, %region_9.10_spmd, %region_10.11_spmd, %region_1... | conditional | bytes 589872 | solution.py:484
  30.3 1.3 collective-permute-start.9
  31.6 8.1 %collective-permute-done.20.north_ref = bf16[144,640]{1,0:T(8,128)(2,1)S(1)} collective-permute-done((bf16[144,640]{1,0:T(8,128)(2,1)S(1)}, bf16[144,640]{1,0:T(8,128)(2,1)S(1)}, u32[]{:S(2)}, u32[]{:S(2)}) %collective-permute-start.20) | collective-permute-done | bytes 184352 | tf_op jit(solution)/shard_map/ppermute | solution.py:483
  39.7 0.0 copy-start.3
  39.7 8.0 %shard_map.113 = (bf16[1456,768]{1,0:T(8,128)(2,1)S(1)}, bf16[1456,768]{1,0:T(8,128)(2,1)S(1)}, bf16[1304,768]{1,0:T(8,128)(2,1)}, f32[1304,256]{1,0:T(8,128)S(1...) custom-call(s32[3]{0:T(128)S(1)} %pad_add_fusion.scal_ref, bf16[1024,256]{1,0:T(8,128)(2,1)S(1)} %bitcast.26, ...), custom_call_target="tpu_custom_call" | custom-call | flops 3000000000 | bytes 13270028 | tf_op jit(solution)/shard_map/pallas_call | solution.py:414
  47.8 0.3 collective-permute-start.22
  48.1 5.2 %shard_map.114 = (bf16[1304,768]{1,0:T(8,128)(2,1)}, f32[128,2304]{1,0:T(8,128)S(1)}, f32[128,2304]{1,0:T(8,128)S(1)}) custom-call(s32[3]{0:T(128)S(1)} %pad_add_fusion.scal_ref, bf16[1456,768]{1,0:T(8,128)(2,1)S(1)} %get-tuple-element.78.pd_ref, bf16[1456,768]{1,0:T(8,128)(2,1)S(1)} %get-tuple-element.79.pf_ref, ...), custom_call_target="tpu_custom_call" | custom-call | flops 3000000000 | bytes 11350028 | tf_op jit(solution)/shard_map/pallas_call | solution.py:414
  53.3 0.6 collective-permute-start.21
  53.9 2.5 %collective-permute-done.21.came_one = f32[128,2304]{1,0:T(8,128)S(1)} collective-permute-done((f32[128,2304]{1,0:T(8,128)S(1)}, f32[128,2304]{1,0:T(8,128)S(1)}, u32[]{:S(2)}, u32[]{:S(2)}) %collective-permute-start.21) | collective-permute-done | bytes 1179680 | tf_op jit(solution)/shard_map/ppermute | solution.py:520
  56.3 0.3 shard_map.116
  56.6 24.5 %all_to_all.20.parts_ref = bf16[16,8,4608]{2,1,0:T(8,128)(2,1)S(1)} all-to-all(bf16[16,8,4608]{2,1,0:T(8,128)(2,1)S(1)} %bitcast.23), channel_id=1, replica_groups=mesh['yl'=2,'x'=4,'z'=8,'yh'=2,'c'=2] {'yl','x','yh'}, dimensions={0} | all-to-all | bytes 2359296 | tf_op jit(solution)/shard_map/all_to_all | solution.py:533
  81.2 0.2 shard_map.117
  81.4 10.8 %all_to_all.21 = f32[8,36,128]{2,1,0:T(8,128)S(1)} all-to-all(f32[8,36,128]{2,1,0:T(8,128)S(1)} %copy.13), channel_id=1, replica_groups=mesh['yl'=2,'x'=4,'z'=8,'yh'=2,'c'=2] {'z'}, dimensions={0} | all-to-all | bytes 294912 | tf_op jit(solution)/shard_map/all_to_all | solution.py:536
  92.2 9.8 %all_to_all.22 = bf16[8,36,128]{2,1,0:T(8,128)(2,1)S(1)} all-to-all(bf16[8,36,128]{2,1,0:T(8,128)(2,1)S(1)} %broadcast_in_dim.6), channel_id=1, replica_groups=mesh['yl'=2,'x'=4,'z'=8,'yh'=2,'c'=2] {'z'}, dimensions={0} | all-to-all | bytes 147456 | tf_op jit(solution)/shard_map/all_to_all | solution.py:538
  102.0 0.1 broadcast_in_dim.15
  102.1 0.0 copy-start.2
  102.1 18.1 %all_to_all.23 = bf16[16,8,4608]{2,1,0:T(8,128)(2,1)S(1)} all-to-all(bf16[16,8,4608]{2,1,0:T(8,128)(2,1)S(1)} %broadcast_in_dim.15), channel_id=1, replica_groups=mesh['yl'=2,'x'=4,'z'=8,'yh'=2,'c'=2] {'yl','x','yh'}, dimensions={0} | all-to-all | bytes 2359296 | tf_op jit(solution)/shard_map/all_to_all | solution.py:540
  120.2 4.6 %collective-permute-start.23 = (bf16[128,4608]{1,0:T(8,128)(2,1)S(1)}, bf16[128,4608]{1,0:T(8,128)(2,1)S(1)}, u32[]{:S(2)}, u32[]{:S(2)}) collective-permute-start(bf16[128,4608]{1,0:T(8,128)(2,1)S(1)} %bitcast.21), channel_id=1, source_target_pairs={{0,1},{1,0},{2,3},{3,2},{4,5},{5,4},{6,7},{7,6},{8,9},{9,8},{10,11... | collective-permute-start | bytes 3538952 | tf_op jit(solution)/shard_map/ppermute | solution.py:542
  124.8 1.6 %copy-done.7 = bf16[1304,768]{1,0:T(8,128)(2,1)S(1)} copy-done((bf16[1304,768]{1,0:T(8,128)(2,1)S(1)}, bf16[1304,768]{1,0:T(8,128)(2,1)}, u32[]{:S(2)}) %copy-start.7) | copy-done | bytes 2002968
  126.4 4.6 %shard_map.115 = (bf16[1024,256]{1,0:T(8,128)(2,1)}, bf16[1024,256]{1,0:T(8,128)(2,1)}) custom-call(s32[3]{0:T(128)S(1)} %pad_add_fusion.scal_ref, bf16[1304,768]{1,0:T(8,128)(2,1)S(1)} %copy-done.6, bf16[1304,768]{1,0:T(8,128)(2,1)S(1)} %copy-done.7, bf16[1024,256]{1,0:T(8,128)(2,1)S(1)} %bitcast.27, bf16[1024,256]{1,0:T(8,128)(2,1)S(1)} %bitcast.30, ...), custom_call_target="tpu_custom_call" | custom-call | flops 3000000000 | bytes 8725516 | tf_op jit(solution)/shard_map/pallas_call | solution.py:414
  131.0 3.3 %shard_map.118 = (f32[2304,256]{1,0:T(8,128)}, f32[2304,256]{1,0:T(8,128)}) custom-call(s32[3]{0:T(128)S(1)} %pad_add_fusion.scal_ref, bf16[128,4608]{1,0:T(8,128)(2,1)S(1)} %bitcast.22, bf16[128,4608]{1,0:T(8,128)(2,1)S(1)} %collective-permute-done.23.other_ref), custom_call_target="tpu_custom_call" | custom-call | flops 10000000 | bytes 7077900 | tf_op jit(solution)/shard_map/pallas_call | solution.py:414
  (25 shorter events, 0.1 us)
Async XLA Ops:
  0.6 39.1 %copy-start.1 = (bf16[16,64,256]{2,1,0:T(8,128)(2,1)S(1)}, bf16[16,64,256]{2,1,0:T(8,128)(2,1)}, u32[]{:S(2)}) copy-start(bf16[16,64,256]{2,1,0:T(8,128)(2,1)} %param.31) | copy-start | bytes 1572868
  0.6 39.1 %copy-start = (bf16[16,64,256]{2,1,0:T(8,128)(2,1)S(1)}, bf16[16,64,256]{2,1,0:T(8,128)(2,1)}, u32[]{:S(2)}) copy-start(bf16[16,64,256]{2,1,0:T(8,128)(2,1)} %param.24) | copy-start | bytes 1572868
  0.7 39.1 %copy-start.4 = (f32[256]{0:T(256)S(1)}, f32[256]{0:T(256)}, u32[]{:S(2)}) copy-start(f32[256]{0:T(256)} %param.26) | copy-start | bytes 3076
  2.1 17.5 %collective-permute-start.18 = (bf16[128,640]{1,0:T(8,128)(2,1)S(1)}, bf16[128,640]{1,0:T(8,128)(2,1)S(1)}, u32[]{:S(2)}, u32[]{:S(2)}) collective-permute-start(bf16[128,640]{1,0:T(8,128)(2,1)S(1)} %get-tuple-element.69.top_ref), channel_id=1, source_target_pairs={{3,255},{7,3},{11,7},{15,11},{19,15},{23,19},{27,23},{31,27},{35,3... | collective-permute-start | bytes 491528 | tf_op jit(solution)/shard_map/ppermute | solution.py:456
  2.8 11.6 %collective-permute-start.17 = (bf16[32,640]{1,0:T(8,128)(2,1)S(1)}, bf16[32,640]{1,0:T(8,128)(2,1)S(1)}, u32[]{:S(2)}, u32[]{:S(2)}) collective-permute-start(bf16[32,640]{1,0:T(8,128)(2,1)S(1)} %get-tuple-element.68), channel_id=1, source_target_pairs={{4,0},{8,4},{12,8},{16,12},{20,16},{24,20},{28,24},{32,28},{36,32}... | collective-permute-start | bytes 122888 | tf_op jit(solution)/shard_map/ppermute | solution.py:460
  12.5 7.2 %collective-permute-start.16 = (bf16[40,640]{1,0:T(8,128)(2,1)S(1)}, bf16[40,640]{1,0:T(8,128)(2,1)S(1)}, u32[]{:S(2)}, u32[]{:S(2)}) collective-permute-start(bf16[40,640]{1,0:T(8,128)(2,1)S(1)} %get-tuple-element.67), channel_id=1, source_target_pairs={{0,4},{4,8},{8,12},{12,16},{16,20},{20,24},{24,28},{28,32},{32,36}... | collective-permute-start | bytes 153608 | tf_op jit(solution)/shard_map/ppermute | solution.py:459
  20.5 1.3 collective-permute-start.4
  21.8 9.8 %collective-permute-start.19 = (bf16[144,640]{1,0:T(8,128)(2,1)S(1)}, bf16[144,640]{1,0:T(8,128)(2,1)S(1)}, u32[]{:S(2)}, u32[]{:S(2)}) collective-permute-start(bf16[144,640]{1,0:T(8,128)(2,1)S(1)} %get-tuple-element.74), channel_id=1, source_target_pairs={{0,1},{1,2},{2,3},{4,5},{5,6},{6,7},{8,9},{9,10},{10,11},{12,13},{... | collective-permute-start | bytes 552968 | tf_op jit(solution)/shard_map/ppermute | solution.py:482
  28.3 11.4 %collective-permute-start.20 = (bf16[144,640]{1,0:T(8,128)(2,1)S(1)}, bf16[144,640]{1,0:T(8,128)(2,1)S(1)}, u32[]{:S(2)}, u32[]{:S(2)}) collective-permute-start(bf16[144,640]{1,0:T(8,128)(2,1)S(1)} %get-tuple-element.75), channel_id=1, source_target_pairs={{1,0},{2,1},{3,2},{5,4},{6,5},{7,6},{9,8},{10,9},{11,10},{13,12},{... | collective-permute-start | bytes 552968 | tf_op jit(solution)/shard_map/ppermute | solution.py:483
  30.3 1.3 collective-permute-start.9
  39.7 8.3 %copy-start.3 = (bf16[3,3,256,256]{3,2,1,0:T(8,128)(2,1)S(1)}, bf16[3,3,256,256]{3,2,1,0:T(8,128)(2,1)}, u32[]{:S(2)}) copy-start(bf16[3,3,256,256]{3,2,1,0:T(8,128)(2,1)} %param.27) | copy-start | bytes 3538948
  47.8 6.1 %collective-permute-start.22 = (f32[128,2304]{1,0:T(8,128)S(1)}, f32[128,2304]{1,0:T(8,128)S(1)}, u32[]{:S(2)}, u32[]{:S(2)}) collective-permute-start(f32[128,2304]{1,0:T(8,128)S(1)} %get-tuple-element.87), channel_id=1, source_target_pairs={{0,1},{1,0},{2,3},{3,2},{4,5},{5,4},{6,7},{7,6},{8,9},{9,8},{10,11... | collective-permute-start | bytes 3538952 | tf_op jit(solution)/shard_map/ppermute | solution.py:507
  53.3 3.0 %collective-permute-start.21 = (f32[128,2304]{1,0:T(8,128)S(1)}, f32[128,2304]{1,0:T(8,128)S(1)}, u32[]{:S(2)}, u32[]{:S(2)}) collective-permute-start(f32[128,2304]{1,0:T(8,128)S(1)} %get-tuple-element.85), channel_id=1, source_target_pairs={{0,1},{1,0},{2,3},{3,2},{4,5},{5,4},{6,7},{7,6},{8,9},{9,8},{10,11... | collective-permute-start | bytes 3538952 | tf_op jit(solution)/shard_map/ppermute | solution.py:520
  102.0 22.8 %copy-start.6 = (bf16[1304,768]{1,0:T(8,128)(2,1)S(1)}, bf16[1304,768]{1,0:T(8,128)(2,1)}, u32[]{:S(2)}) copy-start(bf16[1304,768]{1,0:T(8,128)(2,1)} %get-tuple-element.77.ph_ref) | copy-start | bytes 6008836
  102.1 22.7 %copy-start.2 = (bf16[3,3,256,256]{3,2,1,0:T(8,128)(2,1)S(1)}, bf16[3,3,256,256]{3,2,1,0:T(8,128)(2,1)}, u32[]{:S(2)}) copy-start(bf16[3,3,256,256]{3,2,1,0:T(8,128)(2,1)} %param.25) | copy-start | bytes 3538948
  102.1 22.7 %copy-start.5 = (f32[256]{0:T(256)S(1)}, f32[256]{0:T(256)}, u32[]{:S(2)}) copy-start(f32[256]{0:T(256)} %param.28) | copy-start | bytes 3076
  120.2 10.8 %collective-permute-start.23 = (bf16[128,4608]{1,0:T(8,128)(2,1)S(1)}, bf16[128,4608]{1,0:T(8,128)(2,1)S(1)}, u32[]{:S(2)}, u32[]{:S(2)}) collective-permute-start(bf16[128,4608]{1,0:T(8,128)(2,1)S(1)} %bitcast.21), channel_id=1, source_target_pairs={{0,1},{1,0},{2,3},{3,2},{4,5},{5,4},{6,7},{7,6},{8,9},{9,8},{10,11... | collective-permute-start | bytes 3538952 | tf_op jit(solution)/shard_map/ppermute | solution.py:542
  124.8 1.6 %copy-start.7 = (bf16[1304,768]{1,0:T(8,128)(2,1)S(1)}, bf16[1304,768]{1,0:T(8,128)(2,1)}, u32[]{:S(2)}) copy-start(bf16[1304,768]{1,0:T(8,128)(2,1)} %get-tuple-element.81.pe_ref) | copy-start | bytes 6008836

commit v5 on v4

--- a/solution.py
+++ b/solution.py
@@ -140,18 +140,21 @@
 
 
 def strip_kernel(
-    scal_ref, top_ref, low_ref, west_ref, east_ref, near_ref, upper_ref, lower_ref, fold_ref, west, east, extra, strip,
+    scal_ref, top_ref, low_ref, west_ref, east_ref, near_ref, inner_ref, outer_ref, fold_ref, west, east, extra,
+    upper, lower,
 ):
     west[...] = west_ref[...].astype(F32)
     east[...] = east_ref[...].astype(F32)
-    strip[...] = jnp.zeros(strip.shape, F32)
-    for out_ref, rows_ref, first in ((upper_ref, top_ref, ROWS - 2), (lower_ref, low_ref, 0)):
+    for strip, rows_ref, first in ((upper, top_ref, ROWS - 2), (lower, low_ref, 0)):
+        strip[...] = jnp.zeros(strip.shape, F32)
         for k in range(2):
             y, at = first + k, k * PITCH
             strip[at : at + COLS, :] = rows_ref[k * COLS : (k + 1) * COLS, :].astype(F32)
             strip[at + 64 : at + 66, :] = east[2 * y : 2 * y + 2, :]
             strip[at + 70 : at + 72, :] = west[2 * y : 2 * y + 2, :]
-        out_ref[...] = strip[...].astype(BF16)
+    first = scal_ref[2] == 0
+    inner_ref[...] = jnp.where(first, upper[...], lower[...]).astype(BF16)
+    outer_ref[...] = jnp.where(first, lower[...], upper[...]).astype(BF16)
     to = lax.broadcasted_iota(jnp.int32, (PITCH, 144), 0)
     at = lax.broadcasted_iota(jnp.int32, (PITCH, 144), 1)
     want = 63 - jnp.where(to >= 70, to - PITCH, to) + scal_ref[1]
@@ -177,7 +180,7 @@
 
 
 def first_kernel(
-    scal_ref, field_ref, cot_ref, dep_ref, west_ref, east_ref, south_ref, north_ref, fold_ref,
+    scal_ref, field_ref, cot_ref, dep_ref, west_ref, east_ref, inner_ref, outer_ref, fold_ref,
     w_far, bias_ref,
     pf_ref, pd_ref, ph_far, slope_ref, keep_ref, send_ref,
     ext, depth, west, east, south, north, back, w_ref, ph_ref, sems,
@@ -187,14 +190,17 @@
     top = scal_ref[0] == 1
     west[...] = west_ref[0 : 2 * ROWS, :].astype(F32)
     east[...] = east_ref[...].astype(F32)
-    south[...] = south_ref[...].astype(F32)
-    north[:, 0 : 2 * CH] = north_ref[:, 0 : 2 * CH].astype(F32) + fold_ref[...].astype(F32)
+    core_first = scal_ref[2] == 0
+    inner, outer = inner_ref[...].astype(F32), outer_ref[...].astype(F32)
+    south[...] = jnp.where(core_first, outer, inner)
+    north[...] = jnp.where(core_first, inner, outer)
+    north[:, 0 : 2 * CH] = north[:, 0 : 2 * CH] + fold_ref[...].astype(F32)
     here = lax.broadcasted_iota(jnp.int32, (PITCH, 128), 0) == lax.broadcasted_iota(jnp.int32, (PITCH, 128), 1)
     for j in range(2):
         tile = fold_ref[j * PITCH + COLS : j * PITCH + COLS + 8, 0:128].astype(F32)
         spread = jnp.where(here, jnp.broadcast_to(tile[2:3, :], (PITCH, 128)), 0.0).astype(BF16)
         rows = slice(j * PITCH, (j + 1) * PITCH)
-        north[rows, 2 * CH :] = north_ref[rows, 2 * CH :].astype(F32) + dot(spread, jnp.ones((128, 128), BF16))
+        north[rows, 2 * CH :] = north[rows, 2 * CH :] + dot(spread, jnp.ones((128, 128), BF16))
 
     def fill(out_ref, lanes, own, width, head):
         if head:
@@ -428,6 +434,7 @@
     n_low = lax.axis_size("z")
     n_high = lax.axis_size("yl") * lax.axis_size("x")
     n_z, n_m = n_low * n_high, 4
+    swap = [(0, 1), (1, 0)]
     merid = lax.axis_index(MERID)
     core = lax.axis_index("c")
     flat_field = field.reshape(ROWS * COLS, CH)
@@ -459,7 +466,7 @@
     west = lax.ppermute(east_edge, ZONAL, [(i, (i + 1) % n_z) for i in range(n_z)])
     east = lax.ppermute(west_edge, ZONAL, [((i + 1) % n_z, i) for i in range(n_z)])
     strip = ((2 * PITCH, LANES), BF16)
-    upper, lower, fold = call(
+    inner, outer, fold = call(
         strip_kernel,
         [strip, strip, ((2 * PITCH, 2 * CH), BF16)],
         [
@@ -467,6 +474,7 @@
             pltpu.VMEM((2 * ROWS, LANES), F32),
             pltpu.VMEM((16, LANES), F32),
             pltpu.VMEM((2 * PITCH, LANES), F32),
+            pltpu.VMEM((2 * PITCH, LANES), F32),
         ],
         scal, top_rows, low_rows, west, east, near,
     )
@@ -478,9 +486,9 @@
         return hop(rows, lambda m: n_low * (m // n_low) + n_low - 1 + low - m % n_low)
 
     fold = lax.switch(quotient // n_low, [lambda rows, h=h: turn(rows, h) for h in range(n_high)], fold)
-    upper, lower, fold = lax.optimization_barrier((upper, lower, fold))
-    south = lax.ppermute(upper, MERID, [(i, i + 1) for i in range(n_m - 1)])
-    north = lax.ppermute(lower, MERID, [(i + 1, i) for i in range(n_m - 1)])
+    inner, outer, fold = lax.optimization_barrier((inner, outer, fold))
+    inner = lax.ppermute(inner, "c", swap)
+    outer = lax.ppermute(outer, MERID, [(1, 2), (2, 1)])
     fold = lax.switch(quotient % n_low, [lambda rows, h=h: slide(rows, h) for h in range(n_low)], fold)
     w1 = weight_one.reshape(9, CH, CH)
     w2 = weight_two.reshape(9, CH, CH)
@@ -500,10 +508,9 @@
             pltpu.VMEM((MID, 3 * CH), BF16),
             pltpu.SemaphoreType.DMA((2,)),
         ],
-        scal, flat_field, flat_cot, flat_deep, west, east, south, north, fold, w1, bias_one.reshape(1, CH),
+        scal, flat_field, flat_cot, flat_deep, west, east, inner, outer, fold, w1, bias_one.reshape(1, CH),
         flops=3 * 10**9, far_args=(9,), far_outs=(2,),
     )
-    swap = [(0, 1), (1, 0)]
     came_two = lax.ppermute(send_two, "c", swap)
     pe, keep_one, send_one = call(
         second_kernel,

time: 135 us -> 131 us (0.970)
  waiting for transfers between devices: 15.8 us -> 9.54 us
  starting transfers between devices: 26.9 us -> 31.2 us
  blocking collectives: 63.2 us -> 61.4 us
    ppermute x2, waiting for transfers between devices: 8.08 us -> 1.85 us  [the longest x1 1.84 us: block(): outer = lax.ppermute(outer, MERID, [(1, 2), (2, 1)])]
    ppermute x2, starting transfers between devices: 8.43 us -> 12.8 us  [the longest x1 10.7 us: block(): outer = lax.ppermute(outer, MERID, [(1, 2), (2, 1)])]
    all_to_all x1, blocking collectives: 24.5 us -> 22.8 us  [block(): sums = lax.all_to_all(sums.reshape(n_p, rows, width), PLANE, 0, 0)]
  transfers between devices with their start and end apart: 10 -> 10, of which waited for: 3 -> 3; matrix products, arithmetic and copies ran while one was open for 1% -> 1% of each run, Pallas kernels for 7% -> 8%
where the time goes in v5:
time: 131 us
  blocking collectives  61.4 us (47%)
  starting transfers between devices  31.2 us (24%)
  Pallas kernels  24 us (18%)
  waiting for transfers between devices  9.54 us (7%)
  local copies, waits for them, and re-layouts  2.92 us (2%)
  between operations  1.51 us (1%)
    pallas_call x8, Pallas kernels, call(): pl.pallas_call(body, cost_estimate=pl.CostEstimate(flops=flops, bytes_acc...  24 us
    all_to_all x1, blocking collectives, block(): sums = lax.all_to_all(sums.reshape(n_p, rows, width), PLANE, 0, 0)  22.8 us
    all_to_all x1, blocking collectives, block(): lax.all_to_all(jnp.broadcast_to(line[None], (n_p, rows, width)), PLANE, 0...  18.1 us
    all_to_all x1, blocking collectives, block(): sums = lax.all_to_all(sums.reshape(n_low, part * 36, 128), 'z', 0, 0)  10.8 us
    ppermute x1, starting transfers between devices, block(): outer = lax.ppermute(outer, MERID, [(1, 2), (2, 1)])  10.7 us
    all_to_all x1, blocking collectives, block(): lax.all_to_all(jnp.broadcast_to(piece[None], (n_low, part * 36, 128)), 'z...  9.78 us
    ppermute x1, starting transfers between devices, block(): lax.ppermute(west_edge, ZONAL, [((i + 1) % n_z, i) for i in range(n_z)])  9.68 us
    ppermute x1, waiting for transfers between devices, block(): lax.ppermute(east_edge, ZONAL, [(i, (i + 1) % n_z) for i in range(n_z)])  5.21 us
  transfers between devices with their start and end apart: 10, of which 3 were waited for; matrix products, arithmetic and copies ran while one was open for 1% of the time, Pallas kernels for 8%

profile of v5, /device:TPU:1, one launch (start us, length us, event | category | flops | bytes accessed | tf_op | source)
XLA Modules:
  0.0 130.7 jit_solution(14513977935460866943)
XLA Ops:
  0.7 1.5 %shard_map.111 = (bf16[1024,128]{1,0:T(8,128)(2,1)S(1)}, bf16[128,640]{1,0:T(8,128)(2,1)S(1)}, bf16[128,640]{1,0:T(8,128)(2,1)S(1)}, bf16[32,640]{1,0:T(8,128)(2,1)S(1)}, bf16[40,640]{1,0:T(8,128)(2,1)S(1)}) custom-call(bf16[1024,256]{1,0:T(8,128)(2,1)} %bitcast.25, bf16[1024,256]{1,0:T(8,128)(2,1)} %bitcast.28, s32[16,64]{1,0:T(8,128)} %dep_far.1), custom_call_target="tpu_custom_call" | custom-call | flops 10000000 | bytes 1734656 | tf_op jit(solution)/shard_map/pallas_call | solution.py:420
  2.1 0.7 collective-permute-start.18
  2.8 9.7 %collective-permute-start.17 = (bf16[32,640]{1,0:T(8,128)(2,1)S(1)}, bf16[32,640]{1,0:T(8,128)(2,1)S(1)}, u32[]{:S(2)}, u32[]{:S(2)}) collective-permute-start(bf16[32,640]{1,0:T(8,128)(2,1)S(1)} %get-tuple-element.68), channel_id=1, source_target_pairs={{4,0},{8,4},{12,8},{16,12},{20,16},{24,20},{28,24},{32,28},{36,32}... | collective-permute-start | bytes 122888 | tf_op jit(solution)/shard_map/ppermute | solution.py:467
  12.5 1.2 slice.3
  14.4 0.1 pad_add_fusion.scal_ref
  14.5 5.2 %collective-permute-done.16.west_ref = bf16[40,640]{1,0:T(8,128)(2,1)S(1)} collective-permute-done((bf16[40,640]{1,0:T(8,128)(2,1)S(1)}, bf16[40,640]{1,0:T(8,128)(2,1)S(1)}, u32[]{:S(2)}, u32[]{:S(2)}) %collective-permute-start.16) | collective-permute-done | bytes 51232 | tf_op jit(solution)/shard_map/ppermute | solution.py:466
  19.7 0.9 shard_map.112
  20.6 1.3 %conditional.2 = (bf16[144,512]{1,0:T(8,128)(2,1)}) conditional(s32[]{:T(128)} %clamp.6, bf16[144,512]{1,0:T(8,128)(2,1)S(1)} %get-tuple-element.73, bf16[144,512]{1,0:T(8,128)(2,1)S(1)} %get-tuple-element.73, bf16[144,512]{1,0:T(8,128)(2,1)S(1)} %get-tuple-element.73, ...), branch_computations={%region_0.1_spmd, %region_1.2_spmd, %region_2.3_spmd, %region_3.4_... | conditional | bytes 589872 | solution.py:488
  20.6 1.3 %collective-permute-start.4 = (bf16[144,512]{1,0:T(8,128)(2,1)S(1)}, bf16[144,512]{1,0:T(8,128)(2,1)}, u32[]{:S(2)}, u32[]{:S(2)}) collective-permute-start(bf16[144,512]{1,0:T(8,128)(2,1)S(1)} %param.4), channel_id=1, source_target_pairs={{3,99},{7,103},{11,107},{15,111},{19,115},{23,119},{27,123},{31,12... | collective-permute-start | bytes 442376 | tf_op jit(solution)/shard_map/cond/branch_4_fun/ppermute | solution.py:463
  21.9 2.1 %collective-permute-start.19 = (bf16[144,640]{1,0:T(8,128)(2,1)S(1)}, bf16[144,640]{1,0:T(8,128)(2,1)S(1)}, u32[]{:S(2)}, u32[]{:S(2)}) collective-permute-start(bf16[144,640]{1,0:T(8,128)(2,1)S(1)} %get-tuple-element.74), channel_id=1, source_target_pairs={{0,1},{1,0},{2,3},{3,2},{4,5},{5,4},{6,7},{7,6},{8,9},{9,8},{10,11... | collective-permute-start | bytes 552968 | tf_op jit(solution)/shard_map/ppermute | solution.py:490
  24.0 10.7 %collective-permute-start.20 = (bf16[144,640]{1,0:T(8,128)(2,1)S(1)}, bf16[144,640]{1,0:T(8,128)(2,1)S(1)}, u32[]{:S(2)}, u32[]{:S(2)}) collective-permute-start(bf16[144,640]{1,0:T(8,128)(2,1)S(1)} %get-tuple-element.75), channel_id=1, source_target_pairs={{1,2},{2,1},{5,6},{6,5},{9,10},{10,9},{13,14},{14,13},{17,18},{18,... | collective-permute-start | bytes 552968 | tf_op jit(solution)/shard_map/ppermute | solution.py:491
  34.7 1.3 %conditional.3 = (bf16[144,512]{1,0:T(8,128)(2,1)}) conditional(s32[]{:T(128)} %clamp.7, bf16[144,512]{1,0:T(8,128)(2,1)} %get-tuple-element.90, bf16[144,512]{1,0:T(8,128)(2,1)} %get-tuple-element.90, bf16[144,512]{1,0:T(8,128)(2,1)} %get-tuple-element.90, bf16[144,512]{1,0:T(8,128)(2,1)} %get-tuple-element.90, ...), branch_computations={%region_8.9_spmd, %region_9.10_spmd, %region_10.11_spmd, %region_1... | conditional | bytes 589872 | solution.py:492
  34.7 1.3 %collective-permute-start.9 = (bf16[144,512]{1,0:T(8,128)(2,1)}, bf16[144,512]{1,0:T(8,128)(2,1)}, u32[]{:S(2)}, u32[]{:S(2)}) collective-permute-start(bf16[144,512]{1,0:T(8,128)(2,1)} %param.9), channel_id=1, source_target_pairs={{3,35},{7,31},{11,27},{15,23},{19,19},{23,15},{27,11},{31,7},{35,6... | collective-permute-start | bytes 442376 | tf_op jit(solution)/shard_map/cond/branch_1_fun/ppermute | solution.py:463
  36.1 1.8 %collective-permute-done.20.outer_ref = bf16[144,640]{1,0:T(8,128)(2,1)S(1)} collective-permute-done((bf16[144,640]{1,0:T(8,128)(2,1)S(1)}, bf16[144,640]{1,0:T(8,128)(2,1)S(1)}, u32[]{:S(2)}, u32[]{:S(2)}) %collective-permute-start.20) | collective-permute-done | bytes 184352 | tf_op jit(solution)/shard_map/ppermute | solution.py:491
  37.9 8.0 %shard_map.113 = (bf16[1456,768]{1,0:T(8,128)(2,1)S(1)}, bf16[1456,768]{1,0:T(8,128)(2,1)S(1)}, bf16[1304,768]{1,0:T(8,128)(2,1)}, f32[1304,256]{1,0:T(8,128)S(1...) custom-call(s32[3]{0:T(128)S(1)} %pad_add_fusion.scal_ref, bf16[1024,256]{1,0:T(8,128)(2,1)S(1)} %bitcast.26, ...), custom_call_target="tpu_custom_call" | custom-call | flops 3000000000 | bytes 13270028 | tf_op jit(solution)/shard_map/pallas_call | solution.py:420
  46.0 0.3 collective-permute-start.22
  46.3 5.2 %shard_map.114 = (bf16[1304,768]{1,0:T(8,128)(2,1)}, f32[128,2304]{1,0:T(8,128)S(1)}, f32[128,2304]{1,0:T(8,128)S(1)}) custom-call(s32[3]{0:T(128)S(1)} %pad_add_fusion.scal_ref, bf16[1456,768]{1,0:T(8,128)(2,1)S(1)} %get-tuple-element.78.pd_ref, bf16[1456,768]{1,0:T(8,128)(2,1)S(1)} %get-tuple-element.79.pf_ref, ...), custom_call_target="tpu_custom_call" | custom-call | flops 3000000000 | bytes 11350028 | tf_op jit(solution)/shard_map/pallas_call | solution.py:420
  51.5 0.6 collective-permute-start.21
  52.0 2.5 %collective-permute-done.21.came_one = f32[128,2304]{1,0:T(8,128)S(1)} collective-permute-done((f32[128,2304]{1,0:T(8,128)S(1)}, f32[128,2304]{1,0:T(8,128)S(1)}, u32[]{:S(2)}, u32[]{:S(2)}) %collective-permute-start.21) | collective-permute-done | bytes 1179680 | tf_op jit(solution)/shard_map/ppermute | solution.py:527
  54.5 0.3 shard_map.116
  54.8 22.8 %all_to_all.20.parts_ref = bf16[16,8,4608]{2,1,0:T(8,128)(2,1)S(1)} all-to-all(bf16[16,8,4608]{2,1,0:T(8,128)(2,1)S(1)} %bitcast.23), channel_id=1, replica_groups=mesh['yl'=2,'x'=4,'z'=8,'yh'=2,'c'=2] {'yl','x','yh'}, dimensions={0} | all-to-all | bytes 2359296 | tf_op jit(solution)/shard_map/all_to_all | solution.py:540
  77.6 0.2 shard_map.117
  77.8 10.8 %all_to_all.21 = f32[8,36,128]{2,1,0:T(8,128)S(1)} all-to-all(f32[8,36,128]{2,1,0:T(8,128)S(1)} %copy.13), channel_id=1, replica_groups=mesh['yl'=2,'x'=4,'z'=8,'yh'=2,'c'=2] {'z'}, dimensions={0} | all-to-all | bytes 294912 | tf_op jit(solution)/shard_map/all_to_all | solution.py:543
  88.6 9.8 %all_to_all.22 = bf16[8,36,128]{2,1,0:T(8,128)(2,1)S(1)} all-to-all(bf16[8,36,128]{2,1,0:T(8,128)(2,1)S(1)} %broadcast_in_dim.6), channel_id=1, replica_groups=mesh['yl'=2,'x'=4,'z'=8,'yh'=2,'c'=2] {'z'}, dimensions={0} | all-to-all | bytes 147456 | tf_op jit(solution)/shard_map/all_to_all | solution.py:545
  98.4 0.0 copy-start.6
  98.4 0.1 broadcast_in_dim.15
  98.5 0.0 copy-start.2
  98.5 18.1 %all_to_all.23 = bf16[16,8,4608]{2,1,0:T(8,128)(2,1)S(1)} all-to-all(bf16[16,8,4608]{2,1,0:T(8,128)(2,1)S(1)} %broadcast_in_dim.15), channel_id=1, replica_groups=mesh['yl'=2,'x'=4,'z'=8,'yh'=2,'c'=2] {'yl','x','yh'}, dimensions={0} | all-to-all | bytes 2359296 | tf_op jit(solution)/shard_map/all_to_all | solution.py:547
  116.6 4.6 %collective-permute-start.23 = (bf16[128,4608]{1,0:T(8,128)(2,1)S(1)}, bf16[128,4608]{1,0:T(8,128)(2,1)S(1)}, u32[]{:S(2)}, u32[]{:S(2)}) collective-permute-start(bf16[128,4608]{1,0:T(8,128)(2,1)S(1)} %bitcast.21), channel_id=1, source_target_pairs={{0,1},{1,0},{2,3},{3,2},{4,5},{5,4},{6,7},{7,6},{8,9},{9,8},{10,11... | collective-permute-start | bytes 3538952 | tf_op jit(solution)/shard_map/ppermute | solution.py:549
  121.3 1.6 %copy-done.7 = bf16[1304,768]{1,0:T(8,128)(2,1)S(1)} copy-done((bf16[1304,768]{1,0:T(8,128)(2,1)S(1)}, bf16[1304,768]{1,0:T(8,128)(2,1)}, u32[]{:S(2)}) %copy-start.7) | copy-done | bytes 2002968
  122.8 4.6 %shard_map.115 = (bf16[1024,256]{1,0:T(8,128)(2,1)}, bf16[1024,256]{1,0:T(8,128)(2,1)}) custom-call(s32[3]{0:T(128)S(1)} %pad_add_fusion.scal_ref, bf16[1304,768]{1,0:T(8,128)(2,1)S(1)} %copy-done.6, bf16[1304,768]{1,0:T(8,128)(2,1)S(1)} %copy-done.7, bf16[1024,256]{1,0:T(8,128)(2,1)S(1)} %bitcast.27, bf16[1024,256]{1,0:T(8,128)(2,1)S(1)} %bitcast.30, ...), custom_call_target="tpu_custom_call" | custom-call | flops 3000000000 | bytes 8725516 | tf_op jit(solution)/shard_map/pallas_call | solution.py:420
  127.4 3.3 %shard_map.118 = (f32[2304,256]{1,0:T(8,128)}, f32[2304,256]{1,0:T(8,128)}) custom-call(s32[3]{0:T(128)S(1)} %pad_add_fusion.scal_ref, bf16[128,4608]{1,0:T(8,128)(2,1)S(1)} %bitcast.22, bf16[128,4608]{1,0:T(8,128)(2,1)S(1)} %collective-permute-done.23.other_ref), custom_call_target="tpu_custom_call" | custom-call | flops 10000000 | bytes 7077900 | tf_op jit(solution)/shard_map/pallas_call | solution.py:420
  (25 shorter events, 0.1 us)
Async XLA Ops:
  0.6 37.3 %copy-start.1 = (bf16[16,64,256]{2,1,0:T(8,128)(2,1)S(1)}, bf16[16,64,256]{2,1,0:T(8,128)(2,1)}, u32[]{:S(2)}) copy-start(bf16[16,64,256]{2,1,0:T(8,128)(2,1)} %param.31) | copy-start | bytes 1572868
  0.6 37.3 %copy-start = (bf16[16,64,256]{2,1,0:T(8,128)(2,1)S(1)}, bf16[16,64,256]{2,1,0:T(8,128)(2,1)}, u32[]{:S(2)}) copy-start(bf16[16,64,256]{2,1,0:T(8,128)(2,1)} %param.24) | copy-start | bytes 1572868
  0.7 37.3 %copy-start.4 = (f32[256]{0:T(256)S(1)}, f32[256]{0:T(256)}, u32[]{:S(2)}) copy-start(f32[256]{0:T(256)} %param.26) | copy-start | bytes 3076
  2.1 17.5 %collective-permute-start.18 = (bf16[128,640]{1,0:T(8,128)(2,1)S(1)}, bf16[128,640]{1,0:T(8,128)(2,1)S(1)}, u32[]{:S(2)}, u32[]{:S(2)}) collective-permute-start(bf16[128,640]{1,0:T(8,128)(2,1)S(1)} %get-tuple-element.69.top_ref), channel_id=1, source_target_pairs={{3,255},{7,3},{11,7},{15,11},{19,15},{23,19},{27,23},{31,27},{35,3... | collective-permute-start | bytes 491528 | tf_op jit(solution)/shard_map/ppermute | solution.py:463
  2.8 11.6 %collective-permute-start.17 = (bf16[32,640]{1,0:T(8,128)(2,1)S(1)}, bf16[32,640]{1,0:T(8,128)(2,1)S(1)}, u32[]{:S(2)}, u32[]{:S(2)}) collective-permute-start(bf16[32,640]{1,0:T(8,128)(2,1)S(1)} %get-tuple-element.68), channel_id=1, source_target_pairs={{4,0},{8,4},{12,8},{16,12},{20,16},{24,20},{28,24},{32,28},{36,32}... | collective-permute-start | bytes 122888 | tf_op jit(solution)/shard_map/ppermute | solution.py:467
  12.5 7.2 %collective-permute-start.16 = (bf16[40,640]{1,0:T(8,128)(2,1)S(1)}, bf16[40,640]{1,0:T(8,128)(2,1)S(1)}, u32[]{:S(2)}, u32[]{:S(2)}) collective-permute-start(bf16[40,640]{1,0:T(8,128)(2,1)S(1)} %get-tuple-element.67), channel_id=1, source_target_pairs={{0,4},{4,8},{8,12},{12,16},{16,20},{20,24},{24,28},{28,32},{32,36}... | collective-permute-start | bytes 153608 | tf_op jit(solution)/shard_map/ppermute | solution.py:466
  20.6 1.3 %collective-permute-start.4 = (bf16[144,512]{1,0:T(8,128)(2,1)S(1)}, bf16[144,512]{1,0:T(8,128)(2,1)}, u32[]{:S(2)}, u32[]{:S(2)}) collective-permute-start(bf16[144,512]{1,0:T(8,128)(2,1)S(1)} %param.4), channel_id=1, source_target_pairs={{3,99},{7,103},{11,107},{15,111},{19,115},{23,119},{27,123},{31,12... | collective-permute-start | bytes 442376 | tf_op jit(solution)/shard_map/cond/branch_4_fun/ppermute | solution.py:463
  21.9 14.1 %collective-permute-start.19 = (bf16[144,640]{1,0:T(8,128)(2,1)S(1)}, bf16[144,640]{1,0:T(8,128)(2,1)S(1)}, u32[]{:S(2)}, u32[]{:S(2)}) collective-permute-start(bf16[144,640]{1,0:T(8,128)(2,1)S(1)} %get-tuple-element.74), channel_id=1, source_target_pairs={{0,1},{1,0},{2,3},{3,2},{4,5},{5,4},{6,7},{7,6},{8,9},{9,8},{10,11... | collective-permute-start | bytes 552968 | tf_op jit(solution)/shard_map/ppermute | solution.py:490
  24.0 13.9 %collective-permute-start.20 = (bf16[144,640]{1,0:T(8,128)(2,1)S(1)}, bf16[144,640]{1,0:T(8,128)(2,1)S(1)}, u32[]{:S(2)}, u32[]{:S(2)}) collective-permute-start(bf16[144,640]{1,0:T(8,128)(2,1)S(1)} %get-tuple-element.75), channel_id=1, source_target_pairs={{1,2},{2,1},{5,6},{6,5},{9,10},{10,9},{13,14},{14,13},{17,18},{18,... | collective-permute-start | bytes 552968 | tf_op jit(solution)/shard_map/ppermute | solution.py:491
  34.7 1.3 %collective-permute-start.9 = (bf16[144,512]{1,0:T(8,128)(2,1)}, bf16[144,512]{1,0:T(8,128)(2,1)}, u32[]{:S(2)}, u32[]{:S(2)}) collective-permute-start(bf16[144,512]{1,0:T(8,128)(2,1)} %param.9), channel_id=1, source_target_pairs={{3,35},{7,31},{11,27},{15,23},{19,19},{23,15},{27,11},{31,7},{35,6... | collective-permute-start | bytes 442376 | tf_op jit(solution)/shard_map/cond/branch_1_fun/ppermute | solution.py:463
  37.9 8.3 %copy-start.3 = (bf16[3,3,256,256]{3,2,1,0:T(8,128)(2,1)S(1)}, bf16[3,3,256,256]{3,2,1,0:T(8,128)(2,1)}, u32[]{:S(2)}) copy-start(bf16[3,3,256,256]{3,2,1,0:T(8,128)(2,1)} %param.27) | copy-start | bytes 3538948
  46.0 6.1 %collective-permute-start.22 = (f32[128,2304]{1,0:T(8,128)S(1)}, f32[128,2304]{1,0:T(8,128)S(1)}, u32[]{:S(2)}, u32[]{:S(2)}) collective-permute-start(f32[128,2304]{1,0:T(8,128)S(1)} %get-tuple-element.87), channel_id=1, source_target_pairs={{0,1},{1,0},{2,3},{3,2},{4,5},{5,4},{6,7},{7,6},{8,9},{9,8},{10,11... | collective-permute-start | bytes 3538952 | tf_op jit(solution)/shard_map/ppermute | solution.py:514
  51.5 3.0 %collective-permute-start.21 = (f32[128,2304]{1,0:T(8,128)S(1)}, f32[128,2304]{1,0:T(8,128)S(1)}, u32[]{:S(2)}, u32[]{:S(2)}) collective-permute-start(f32[128,2304]{1,0:T(8,128)S(1)} %get-tuple-element.85), channel_id=1, source_target_pairs={{0,1},{1,0},{2,3},{3,2},{4,5},{5,4},{6,7},{7,6},{8,9},{9,8},{10,11... | collective-permute-start | bytes 3538952 | tf_op jit(solution)/shard_map/ppermute | solution.py:527
  98.4 22.8 %copy-start.6 = (bf16[1304,768]{1,0:T(8,128)(2,1)S(1)}, bf16[1304,768]{1,0:T(8,128)(2,1)}, u32[]{:S(2)}) copy-start(bf16[1304,768]{1,0:T(8,128)(2,1)} %get-tuple-element.77.ph_ref) | copy-start | bytes 6008836
  98.5 22.7 %copy-start.2 = (bf16[3,3,256,256]{3,2,1,0:T(8,128)(2,1)S(1)}, bf16[3,3,256,256]{3,2,1,0:T(8,128)(2,1)}, u32[]{:S(2)}) copy-start(bf16[3,3,256,256]{3,2,1,0:T(8,128)(2,1)} %param.25) | copy-start | bytes 3538948
  98.5 22.7 %copy-start.5 = (f32[256]{0:T(256)S(1)}, f32[256]{0:T(256)}, u32[]{:S(2)}) copy-start(f32[256]{0:T(256)} %param.28) | copy-start | bytes 3076
  116.6 10.8 %collective-permute-start.23 = (bf16[128,4608]{1,0:T(8,128)(2,1)S(1)}, bf16[128,4608]{1,0:T(8,128)(2,1)S(1)}, u32[]{:S(2)}, u32[]{:S(2)}) collective-permute-start(bf16[128,4608]{1,0:T(8,128)(2,1)S(1)} %bitcast.21), channel_id=1, source_target_pairs={{0,1},{1,0},{2,3},{3,2},{4,5},{5,4},{6,7},{7,6},{8,9},{9,8},{10,11... | collective-permute-start | bytes 3538952 | tf_op jit(solution)/shard_map/ppermute | solution.py:549
  121.2 1.6 %copy-start.7 = (bf16[1304,768]{1,0:T(8,128)(2,1)S(1)}, bf16[1304,768]{1,0:T(8,128)(2,1)}, u32[]{:S(2)}) copy-start(bf16[1304,768]{1,0:T(8,128)(2,1)} %get-tuple-element.81.pe_ref) | copy-start | bytes 6008836

commit v6 on v5

--- a/solution.py
+++ b/solution.py
@@ -394,18 +394,36 @@
         out_ref[:, at : at + step] = total
 
 
-def last_kernel(scal_ref, mine_ref, other_ref, one_ref, two_ref):
+def last_kernel(scal_ref, mine_ref, other_ref, one_far, two_far, turned_ref, sems):
     first = scal_ref[2] == 0
     down = lax.broadcasted_iota(jnp.int32, (CH, CH), 0)
     across = lax.broadcasted_iota(jnp.int32, (CH, CH), 1)
     eye = jnp.where(down == across, SCALE, 0.0).astype(BF16)
+    copies = []
     for k in range(18):
         mine = mine_ref[:, k * CH : (k + 1) * CH]
         other = other_ref[:, k * CH : (k + 1) * CH]
         low, high = jnp.where(first, mine, other), jnp.where(first, other, mine)
         kernel = dot(eye, jnp.concatenate([low, high], axis=0), ((1,), (1,)))
-        out_ref, at = (one_ref, k) if k < 9 else (two_ref, k - 9)
-        out_ref[at * CH : (at + 1) * CH, :] = kernel
+        turned_ref[k * CH : (k + 1) * CH, :] = kernel
+        out_ref, at = (one_far, k) if k < 9 else (two_far, k - 9)
+        copies.append(
+            pltpu.make_async_copy(
+                turned_ref.at[k * CH : (k + 1) * CH, :], out_ref.at[at * CH : (at + 1) * CH, :], sems.at[k]
+            )
+        )
+        copies[k].start()
+    for copy in copies:
+        copy.wait()
+
+
+def piece_kernel(parts_ref, out_ref):
+    total = parts_ref[0]
+    for k in range(1, parts_ref.shape[0]):
+        total = total + parts_ref[k]
+    total = total.astype(BF16)
+    for k in range(out_ref.shape[0]):
+        out_ref[k] = total
 
 
 VM = pl.BlockSpec(memory_space=pltpu.VMEM)
@@ -541,8 +559,8 @@
     (sums,) = call(total_kernel, [((rows, width), F32)], [], sums, scalars=False)
     part = rows // n_low
     sums = lax.all_to_all(sums.reshape(n_low, part * 36, 128), "z", 0, 0)
-    piece = jnp.sum(sums, axis=0).astype(BF16)
-    line = lax.all_to_all(jnp.broadcast_to(piece[None], (n_low, part * 36, 128)), "z", 0, 0)
+    (piece,) = call(piece_kernel, [((n_low, part * 36, 128), BF16)], [], sums, scalars=False)
+    line = lax.all_to_all(piece, "z", 0, 0)
     line = line.reshape(rows, width)
     mine = lax.all_to_all(jnp.broadcast_to(line[None], (n_p, rows, width)), PLANE, 0, 0)
     mine = mine.reshape(CH // 2, width)
@@ -550,8 +568,8 @@
     grad_one, grad_two = call(
         last_kernel,
         [((9 * CH, CH), F32), ((9 * CH, CH), F32)],
-        [],
-        scal, mine, other,
+        [pltpu.VMEM((18 * CH, CH), F32), pltpu.SemaphoreType.DMA((18,))],
+        scal, mine, other, far_outs=(0, 1),
     )
     return (
         output.reshape(ROWS, COLS, CH),

time: 131 us -> 130 us (level)
  local copies, waits for them, and re-layouts: 2.92 us -> 1.36 us
    unnamed x17, local copies, waits for them, and re-layouts: 1.6 us -> 0.05 us
    pallas_call x8 -> x9, Pallas kernels: 24 us -> 23.8 us  [call(): pl.pallas_call(body, cost_estimate=pl.CostEstimate(flops=flops, bytes_acc...]
where the time goes in v6:
time: 130 us; the launch traced here: 129 us
  blocking collectives  61.5 us (47%)
  starting transfers between devices  31.2 us (24%)
  Pallas kernels  23.8 us (18%)
  waiting for transfers between devices  9.53 us (7%)
  between operations  1.66 us (1%)
  local copies, waits for them, and re-layouts  1.36 us (1%)
    pallas_call x9, Pallas kernels, call(): pl.pallas_call(body, cost_estimate=pl.CostEstimate(flops=flops, bytes_acc...  23.8 us
    all_to_all x1, blocking collectives, block(): sums = lax.all_to_all(sums.reshape(n_p, rows, width), PLANE, 0, 0)  22.8 us
    all_to_all x1, blocking collectives, block(): lax.all_to_all(jnp.broadcast_to(line[None], (n_p, rows, width)), PLANE, 0...  18.1 us
    all_to_all x1, blocking collectives, block(): sums = lax.all_to_all(sums.reshape(n_low, part * 36, 128), 'z', 0, 0)  10.9 us
    ppermute x1, starting transfers between devices, block(): outer = lax.ppermute(outer, MERID, [(1, 2), (2, 1)])  10.6 us
    all_to_all x1, blocking collectives, block(): line = lax.all_to_all(piece, 'z', 0, 0)  9.78 us
    ppermute x1, starting transfers between devices, block(): lax.ppermute(west_edge, ZONAL, [((i + 1) % n_z, i) for i in range(n_z)])  9.68 us
    ppermute x1, waiting for transfers between devices, block(): lax.ppermute(east_edge, ZONAL, [(i, (i + 1) % n_z) for i in range(n_z)])  5.21 us
  transfers between devices with their start and end apart: 10, of which 3 were waited for; matrix products, arithmetic and copies ran while one was open for 1% of the time, Pallas kernels for 8%

profile of v6, /device:TPU:1, one launch (start us, length us, event | category | flops | bytes accessed | tf_op | source)
XLA Modules:
  0.0 129.3 jit_solution(9244904995522875461)
XLA Ops:
  0.7 1.5 %shard_map.111 = (bf16[1024,128]{1,0:T(8,128)(2,1)S(1)}, bf16[128,640]{1,0:T(8,128)(2,1)S(1)}, bf16[128,640]{1,0:T(8,128)(2,1)S(1)}, bf16[32,640]{1,0:T(8,128)(2,1)S(1)}, bf16[40,640]{1,0:T(8,128)(2,1)S(1)}) custom-call(bf16[1024,256]{1,0:T(8,128)(2,1)} %bitcast.25, bf16[1024,256]{1,0:T(8,128)(2,1)} %bitcast.28, s32[16,64]{1,0:T(8,128)} %dep_far.1), custom_call_target="tpu_custom_call" | custom-call | flops 10000000 | bytes 1734656 | tf_op jit(solution)/shard_map/pallas_call | solution.py:438
  2.1 0.7 collective-permute-start.18
  2.8 9.7 %collective-permute-start.17 = (bf16[32,640]{1,0:T(8,128)(2,1)S(1)}, bf16[32,640]{1,0:T(8,128)(2,1)S(1)}, u32[]{:S(2)}, u32[]{:S(2)}) collective-permute-start(bf16[32,640]{1,0:T(8,128)(2,1)S(1)} %get-tuple-element.68), channel_id=1, source_target_pairs={{4,0},{8,4},{12,8},{16,12},{20,16},{24,20},{28,24},{32,28},{36,32}... | collective-permute-start | bytes 122888 | tf_op jit(solution)/shard_map/ppermute | solution.py:485
  12.5 1.2 slice.3
  14.4 0.1 pad_add_fusion.scal_ref
  14.5 5.2 %collective-permute-done.16.west_ref = bf16[40,640]{1,0:T(8,128)(2,1)S(1)} collective-permute-done((bf16[40,640]{1,0:T(8,128)(2,1)S(1)}, bf16[40,640]{1,0:T(8,128)(2,1)S(1)}, u32[]{:S(2)}, u32[]{:S(2)}) %collective-permute-start.16) | collective-permute-done | bytes 51232 | tf_op jit(solution)/shard_map/ppermute | solution.py:484
  19.7 0.9 shard_map.112
  20.6 1.3 %conditional.2 = (bf16[144,512]{1,0:T(8,128)(2,1)}) conditional(s32[]{:T(128)} %clamp.6, bf16[144,512]{1,0:T(8,128)(2,1)S(1)} %get-tuple-element.73, bf16[144,512]{1,0:T(8,128)(2,1)S(1)} %get-tuple-element.73, bf16[144,512]{1,0:T(8,128)(2,1)S(1)} %get-tuple-element.73, ...), branch_computations={%region_0.1_spmd, %region_1.2_spmd, %region_2.3_spmd, %region_3.4_... | conditional | bytes 589872 | solution.py:506
  20.6 1.3 %collective-permute-start.4 = (bf16[144,512]{1,0:T(8,128)(2,1)S(1)}, bf16[144,512]{1,0:T(8,128)(2,1)}, u32[]{:S(2)}, u32[]{:S(2)}) collective-permute-start(bf16[144,512]{1,0:T(8,128)(2,1)S(1)} %param.4), channel_id=1, source_target_pairs={{3,99},{7,103},{11,107},{15,111},{19,115},{23,119},{27,123},{31,12... | collective-permute-start | bytes 442376 | tf_op jit(solution)/shard_map/cond/branch_4_fun/ppermute | solution.py:481
  21.9 2.1 %collective-permute-start.19 = (bf16[144,640]{1,0:T(8,128)(2,1)S(1)}, bf16[144,640]{1,0:T(8,128)(2,1)S(1)}, u32[]{:S(2)}, u32[]{:S(2)}) collective-permute-start(bf16[144,640]{1,0:T(8,128)(2,1)S(1)} %get-tuple-element.74), channel_id=1, source_target_pairs={{0,1},{1,0},{2,3},{3,2},{4,5},{5,4},{6,7},{7,6},{8,9},{9,8},{10,11... | collective-permute-start | bytes 552968 | tf_op jit(solution)/shard_map/ppermute | solution.py:508
  24.0 10.6 %collective-permute-start.20 = (bf16[144,640]{1,0:T(8,128)(2,1)S(1)}, bf16[144,640]{1,0:T(8,128)(2,1)S(1)}, u32[]{:S(2)}, u32[]{:S(2)}) collective-permute-start(bf16[144,640]{1,0:T(8,128)(2,1)S(1)} %get-tuple-element.75), channel_id=1, source_target_pairs={{1,2},{2,1},{5,6},{6,5},{9,10},{10,9},{13,14},{14,13},{17,18},{18,... | collective-permute-start | bytes 552968 | tf_op jit(solution)/shard_map/ppermute | solution.py:509
  34.7 1.4 %conditional.3 = (bf16[144,512]{1,0:T(8,128)(2,1)}) conditional(s32[]{:T(128)} %clamp.7, bf16[144,512]{1,0:T(8,128)(2,1)} %get-tuple-element.90, bf16[144,512]{1,0:T(8,128)(2,1)} %get-tuple-element.90, bf16[144,512]{1,0:T(8,128)(2,1)} %get-tuple-element.90, bf16[144,512]{1,0:T(8,128)(2,1)} %get-tuple-element.90, ...), branch_computations={%region_8.9_spmd, %region_9.10_spmd, %region_10.11_spmd, %region_1... | conditional | bytes 589872 | solution.py:510
  34.7 1.3 %collective-permute-start.9 = (bf16[144,512]{1,0:T(8,128)(2,1)}, bf16[144,512]{1,0:T(8,128)(2,1)}, u32[]{:S(2)}, u32[]{:S(2)}) collective-permute-start(bf16[144,512]{1,0:T(8,128)(2,1)} %param.9), channel_id=1, source_target_pairs={{3,35},{7,31},{11,27},{15,23},{19,19},{23,15},{27,11},{31,7},{35,6... | collective-permute-start | bytes 442376 | tf_op jit(solution)/shard_map/cond/branch_1_fun/ppermute | solution.py:481
  36.1 1.8 %collective-permute-done.20.outer_ref = bf16[144,640]{1,0:T(8,128)(2,1)S(1)} collective-permute-done((bf16[144,640]{1,0:T(8,128)(2,1)S(1)}, bf16[144,640]{1,0:T(8,128)(2,1)S(1)}, u32[]{:S(2)}, u32[]{:S(2)}) %collective-permute-start.20) | collective-permute-done | bytes 184352 | tf_op jit(solution)/shard_map/ppermute | solution.py:509
  37.9 8.0 %shard_map.113 = (bf16[1456,768]{1,0:T(8,128)(2,1)S(1)}, bf16[1456,768]{1,0:T(8,128)(2,1)S(1)}, bf16[1304,768]{1,0:T(8,128)(2,1)}, f32[1304,256]{1,0:T(8,128)S(1...) custom-call(s32[3]{0:T(128)S(1)} %pad_add_fusion.scal_ref, bf16[1024,256]{1,0:T(8,128)(2,1)S(1)} %bitcast.26, ...), custom_call_target="tpu_custom_call" | custom-call | flops 3000000000 | bytes 13270028 | tf_op jit(solution)/shard_map/pallas_call | solution.py:438
  46.0 0.3 collective-permute-start.22
  46.3 5.2 %shard_map.114 = (bf16[1304,768]{1,0:T(8,128)(2,1)}, f32[128,2304]{1,0:T(8,128)S(1)}, f32[128,2304]{1,0:T(8,128)S(1)}) custom-call(s32[3]{0:T(128)S(1)} %pad_add_fusion.scal_ref, bf16[1456,768]{1,0:T(8,128)(2,1)S(1)} %get-tuple-element.78.pd_ref, bf16[1456,768]{1,0:T(8,128)(2,1)S(1)} %get-tuple-element.79.pf_ref, ...), custom_call_target="tpu_custom_call" | custom-call | flops 3000000000 | bytes 11350028 | tf_op jit(solution)/shard_map/pallas_call | solution.py:438
  51.5 0.6 collective-permute-start.21
  52.1 2.5 %collective-permute-done.21.came_one = f32[128,2304]{1,0:T(8,128)S(1)} collective-permute-done((f32[128,2304]{1,0:T(8,128)S(1)}, f32[128,2304]{1,0:T(8,128)S(1)}, u32[]{:S(2)}, u32[]{:S(2)}) %collective-permute-start.21) | collective-permute-done | bytes 1179680 | tf_op jit(solution)/shard_map/ppermute | solution.py:545
  54.5 0.3 shard_map.116
  54.9 22.8 %all_to_all.20.parts_ref = bf16[16,8,4608]{2,1,0:T(8,128)(2,1)S(1)} all-to-all(bf16[16,8,4608]{2,1,0:T(8,128)(2,1)S(1)} %bitcast.23), channel_id=1, replica_groups=mesh['yl'=2,'x'=4,'z'=8,'yh'=2,'c'=2] {'yl','x','yh'}, dimensions={0} | all-to-all | bytes 2359296 | tf_op jit(solution)/shard_map/all_to_all | solution.py:558
  77.6 0.2 shard_map.117
  77.8 10.9 %all_to_all.21.parts_ref = f32[8,36,128]{2,1,0:T(8,128)S(1)} all-to-all(f32[8,36,128]{2,1,0:T(8,128)S(1)} %copy.12), channel_id=1, replica_groups=mesh['yl'=2,'x'=4,'z'=8,'yh'=2,'c'=2] {'z'}, dimensions={0} | all-to-all | bytes 294912 | tf_op jit(solution)/shard_map/all_to_all | solution.py:561
  88.8 9.8 %all_to_all.22 = bf16[8,36,128]{2,1,0:T(8,128)(2,1)S(1)} all-to-all(bf16[8,36,128]{2,1,0:T(8,128)(2,1)S(1)} %shard_map.118), channel_id=1, replica_groups=mesh['yl'=2,'x'=4,'z'=8,'yh'=2,'c'=2] {'z'}, dimensions={0} | all-to-all | bytes 147456 | tf_op jit(solution)/shard_map/all_to_all | solution.py:563
  98.6 0.0 copy-start.6
  98.6 0.1 broadcast_in_dim.8
  98.7 0.0 copy-start.2
  98.7 0.0 copy-start.5
  98.7 18.1 %all_to_all.23 = bf16[16,8,4608]{2,1,0:T(8,128)(2,1)S(1)} all-to-all(bf16[16,8,4608]{2,1,0:T(8,128)(2,1)S(1)} %broadcast_in_dim.8), channel_id=1, replica_groups=mesh['yl'=2,'x'=4,'z'=8,'yh'=2,'c'=2] {'yl','x','yh'}, dimensions={0} | all-to-all | bytes 2359296 | tf_op jit(solution)/shard_map/all_to_all | solution.py:565
  116.8 4.6 %collective-permute-start.23 = (bf16[128,4608]{1,0:T(8,128)(2,1)S(1)}, bf16[128,4608]{1,0:T(8,128)(2,1)S(1)}, u32[]{:S(2)}, u32[]{:S(2)}) collective-permute-start(bf16[128,4608]{1,0:T(8,128)(2,1)S(1)} %bitcast.21), channel_id=1, source_target_pairs={{0,1},{1,0},{2,3},{3,2},{4,5},{5,4},{6,7},{7,6},{8,9},{9,8},{10,11... | collective-permute-start | bytes 3538952 | tf_op jit(solution)/shard_map/ppermute | solution.py:567
  121.4 4.6 %shard_map.115 = (bf16[1024,256]{1,0:T(8,128)(2,1)}, bf16[1024,256]{1,0:T(8,128)(2,1)}) custom-call(s32[3]{0:T(128)S(1)} %pad_add_fusion.scal_ref, bf16[1304,768]{1,0:T(8,128)(2,1)S(1)} %copy-done.6, bf16[1304,768]{1,0:T(8,128)(2,1)S(1)} %copy-done.7, bf16[1024,256]{1,0:T(8,128)(2,1)S(1)} %bitcast.27, bf16[1024,256]{1,0:T(8,128)(2,1)S(1)} %bitcast.30, ...), custom_call_target="tpu_custom_call" | custom-call | flops 3000000000 | bytes 8725516 | tf_op jit(solution)/shard_map/pallas_call | solution.py:438
  126.0 3.1 %shard_map.119 = (f32[2304,256]{1,0:T(8,128)}, f32[2304,256]{1,0:T(8,128)}) custom-call(s32[3]{0:T(128)S(1)} %pad_add_fusion.scal_ref, bf16[128,4608]{1,0:T(8,128)(2,1)S(1)} %bitcast.22, bf16[128,4608]{1,0:T(8,128)(2,1)S(1)} %collective-permute-done.23.other_ref), custom_call_target="tpu_custom_call" | custom-call | flops 10000000 | bytes 7077900 | tf_op jit(solution)/shard_map/pallas_call | solution.py:438
  (24 shorter events, 0.1 us)
Async XLA Ops:
  0.6 37.3 %copy-start.1 = (bf16[16,64,256]{2,1,0:T(8,128)(2,1)S(1)}, bf16[16,64,256]{2,1,0:T(8,128)(2,1)}, u32[]{:S(2)}) copy-start(bf16[16,64,256]{2,1,0:T(8,128)(2,1)} %param.31) | copy-start | bytes 1572868
  0.6 37.3 %copy-start = (bf16[16,64,256]{2,1,0:T(8,128)(2,1)S(1)}, bf16[16,64,256]{2,1,0:T(8,128)(2,1)}, u32[]{:S(2)}) copy-start(bf16[16,64,256]{2,1,0:T(8,128)(2,1)} %param.24) | copy-start | bytes 1572868
  0.7 37.3 %copy-start.4 = (f32[256]{0:T(256)S(1)}, f32[256]{0:T(256)}, u32[]{:S(2)}) copy-start(f32[256]{0:T(256)} %param.26) | copy-start | bytes 3076
  2.1 17.5 %collective-permute-start.18 = (bf16[128,640]{1,0:T(8,128)(2,1)S(1)}, bf16[128,640]{1,0:T(8,128)(2,1)S(1)}, u32[]{:S(2)}, u32[]{:S(2)}) collective-permute-start(bf16[128,640]{1,0:T(8,128)(2,1)S(1)} %get-tuple-element.69.top_ref), channel_id=1, source_target_pairs={{3,255},{7,3},{11,7},{15,11},{19,15},{23,19},{27,23},{31,27},{35,3... | collective-permute-start | bytes 491528 | tf_op jit(solution)/shard_map/ppermute | solution.py:481
  2.8 11.6 %collective-permute-start.17 = (bf16[32,640]{1,0:T(8,128)(2,1)S(1)}, bf16[32,640]{1,0:T(8,128)(2,1)S(1)}, u32[]{:S(2)}, u32[]{:S(2)}) collective-permute-start(bf16[32,640]{1,0:T(8,128)(2,1)S(1)} %get-tuple-element.68), channel_id=1, source_target_pairs={{4,0},{8,4},{12,8},{16,12},{20,16},{24,20},{28,24},{32,28},{36,32}... | collective-permute-start | bytes 122888 | tf_op jit(solution)/shard_map/ppermute | solution.py:485
  12.5 7.2 %collective-permute-start.16 = (bf16[40,640]{1,0:T(8,128)(2,1)S(1)}, bf16[40,640]{1,0:T(8,128)(2,1)S(1)}, u32[]{:S(2)}, u32[]{:S(2)}) collective-permute-start(bf16[40,640]{1,0:T(8,128)(2,1)S(1)} %get-tuple-element.67), channel_id=1, source_target_pairs={{0,4},{4,8},{8,12},{12,16},{16,20},{20,24},{24,28},{28,32},{32,36}... | collective-permute-start | bytes 153608 | tf_op jit(solution)/shard_map/ppermute | solution.py:484
  20.6 1.3 %collective-permute-start.4 = (bf16[144,512]{1,0:T(8,128)(2,1)S(1)}, bf16[144,512]{1,0:T(8,128)(2,1)}, u32[]{:S(2)}, u32[]{:S(2)}) collective-permute-start(bf16[144,512]{1,0:T(8,128)(2,1)S(1)} %param.4), channel_id=1, source_target_pairs={{3,99},{7,103},{11,107},{15,111},{19,115},{23,119},{27,123},{31,12... | collective-permute-start | bytes 442376 | tf_op jit(solution)/shard_map/cond/branch_4_fun/ppermute | solution.py:481
  21.9 14.1 %collective-permute-start.19 = (bf16[144,640]{1,0:T(8,128)(2,1)S(1)}, bf16[144,640]{1,0:T(8,128)(2,1)S(1)}, u32[]{:S(2)}, u32[]{:S(2)}) collective-permute-start(bf16[144,640]{1,0:T(8,128)(2,1)S(1)} %get-tuple-element.74), channel_id=1, source_target_pairs={{0,1},{1,0},{2,3},{3,2},{4,5},{5,4},{6,7},{7,6},{8,9},{9,8},{10,11... | collective-permute-start | bytes 552968 | tf_op jit(solution)/shard_map/ppermute | solution.py:508
  24.0 13.9 %collective-permute-start.20 = (bf16[144,640]{1,0:T(8,128)(2,1)S(1)}, bf16[144,640]{1,0:T(8,128)(2,1)S(1)}, u32[]{:S(2)}, u32[]{:S(2)}) collective-permute-start(bf16[144,640]{1,0:T(8,128)(2,1)S(1)} %get-tuple-element.75), channel_id=1, source_target_pairs={{1,2},{2,1},{5,6},{6,5},{9,10},{10,9},{13,14},{14,13},{17,18},{18,... | collective-permute-start | bytes 552968 | tf_op jit(solution)/shard_map/ppermute | solution.py:509
  34.7 1.3 %collective-permute-start.9 = (bf16[144,512]{1,0:T(8,128)(2,1)}, bf16[144,512]{1,0:T(8,128)(2,1)}, u32[]{:S(2)}, u32[]{:S(2)}) collective-permute-start(bf16[144,512]{1,0:T(8,128)(2,1)} %param.9), channel_id=1, source_target_pairs={{3,35},{7,31},{11,27},{15,23},{19,19},{23,15},{27,11},{31,7},{35,6... | collective-permute-start | bytes 442376 | tf_op jit(solution)/shard_map/cond/branch_1_fun/ppermute | solution.py:481
  37.9 8.3 %copy-start.3 = (bf16[3,3,256,256]{3,2,1,0:T(8,128)(2,1)S(1)}, bf16[3,3,256,256]{3,2,1,0:T(8,128)(2,1)}, u32[]{:S(2)}) copy-start(bf16[3,3,256,256]{3,2,1,0:T(8,128)(2,1)} %param.27) | copy-start | bytes 3538948
  46.0 6.1 %collective-permute-start.22 = (f32[128,2304]{1,0:T(8,128)S(1)}, f32[128,2304]{1,0:T(8,128)S(1)}, u32[]{:S(2)}, u32[]{:S(2)}) collective-permute-start(f32[128,2304]{1,0:T(8,128)S(1)} %get-tuple-element.87), channel_id=1, source_target_pairs={{0,1},{1,0},{2,3},{3,2},{4,5},{5,4},{6,7},{7,6},{8,9},{9,8},{10,11... | collective-permute-start | bytes 3538952 | tf_op jit(solution)/shard_map/ppermute | solution.py:532
  51.5 3.1 %collective-permute-start.21 = (f32[128,2304]{1,0:T(8,128)S(1)}, f32[128,2304]{1,0:T(8,128)S(1)}, u32[]{:S(2)}, u32[]{:S(2)}) collective-permute-start(f32[128,2304]{1,0:T(8,128)S(1)} %get-tuple-element.85), channel_id=1, source_target_pairs={{0,1},{1,0},{2,3},{3,2},{4,5},{5,4},{6,7},{7,6},{8,9},{9,8},{10,11... | collective-permute-start | bytes 3538952 | tf_op jit(solution)/shard_map/ppermute | solution.py:545
  77.6 43.7 %copy-start.7 = (bf16[1304,768]{1,0:T(8,128)(2,1)S(1)}, bf16[1304,768]{1,0:T(8,128)(2,1)}, u32[]{:S(2)}) copy-start(bf16[1304,768]{1,0:T(8,128)(2,1)} %get-tuple-element.81.pe_ref) | copy-start | bytes 6008836
  98.6 22.8 %copy-start.6 = (bf16[1304,768]{1,0:T(8,128)(2,1)S(1)}, bf16[1304,768]{1,0:T(8,128)(2,1)}, u32[]{:S(2)}) copy-start(bf16[1304,768]{1,0:T(8,128)(2,1)} %get-tuple-element.77.ph_ref) | copy-start | bytes 6008836
  98.7 22.7 %copy-start.2 = (bf16[3,3,256,256]{3,2,1,0:T(8,128)(2,1)S(1)}, bf16[3,3,256,256]{3,2,1,0:T(8,128)(2,1)}, u32[]{:S(2)}) copy-start(bf16[3,3,256,256]{3,2,1,0:T(8,128)(2,1)} %param.25) | copy-start | bytes 3538948
  98.7 22.7 %copy-start.5 = (f32[256]{0:T(256)S(1)}, f32[256]{0:T(256)}, u32[]{:S(2)}) copy-start(f32[256]{0:T(256)} %param.28) | copy-start | bytes 3076
  116.8 9.2 %collective-permute-start.23 = (bf16[128,4608]{1,0:T(8,128)(2,1)S(1)}, bf16[128,4608]{1,0:T(8,128)(2,1)S(1)}, u32[]{:S(2)}, u32[]{:S(2)}) collective-permute-start(bf16[128,4608]{1,0:T(8,128)(2,1)S(1)} %bitcast.21), channel_id=1, source_target_pairs={{0,1},{1,0},{2,3},{3,2},{4,5},{5,4},{6,7},{7,6},{8,9},{9,8},{10,11... | collective-permute-start | bytes 3538952 | tf_op jit(solution)/shard_map/ppermute | solution.py:567
